TPU v7x, 32 devices: a whole 2x2x4 slice. The times are simulated.
32 devices in a mesh: grid: 8 (over y, x, core), ao: 4 (over z).
Axes of the slice: x: 2, y: 2, z: 4, core: 2. Of those that a mesh axis runs over, the one named last changes fastest.
Arguments:
- trial: bfloat16 [12288, 16, 2, 128], P('ao'), may hold values from -0.15625 to 0.15625
- occupied: bfloat16 [12288, 2, 128], P('ao'), may hold values from -0.15625 to 0.15625
- colloc: bfloat16 [32, 128, 1536], P('grid'), may hold values from -3 to 3
- blocks: int32 [32, 12], P('grid'), may hold values from 0 to 95, as said below
- coords: float32 [32, 3, 128], P('grid'), may hold values from 0 to 4
- weights: float32 [32, 128], P('grid'), may hold values from 0.02 to 0.2
Outputs:
- exchange: float32 [16, 12288, 2, 128], P('ao', 'grid')
Inputs may be any that keep to these rules, and one draw needn't show every extreme that they name: The 12 blocks of a batch are distinct and lie among 24 cyclically consecutive shell blocks.
All inputs are finite; a program needn't handle non-finite values.
Results may differ from a plain program's by a relative error of at most 0.0053.
Values may be sent and summed in bfloat16 or wider, within the bound.
No kernel may reach another device: no remote copies, remote signals or barrier semaphores. Data moves between devices by JAX's collectives and lax.ppermute only.
A program may use at most 192 MiB of HBM per device.

v0:
```python
import functools
import math

import jax
import jax.numpy as jnp
from jax import lax
from jax.experimental import pallas as pl
from jax.experimental.pallas import tpu as pltpu
from jax.sharding import PartitionSpec as P

F32 = jnp.float32
BF16 = jnp.bfloat16
MIB = 1024 * 1024


def params(*arrays):
    total = sum(math.prod(shape) * size for shape, size in arrays)
    return pltpu.CompilerParams(vmem_limit_bytes=min(60 * MIB, total + 6 * MIB))


SMEM = pl.BlockSpec(memory_space=pltpu.SMEM)
VMEM = pl.BlockSpec(memory_space=pltpu.VMEM)
ANY = pl.BlockSpec(memory_space=pl.ANY)
HBM = pl.BlockSpec(memory_space=pltpu.HBM)


def kernel_matrix(points, quad):
    differ = points[..., :, None, :] - points[..., :, :, None]
    square = jnp.sum(differ * differ, axis=-3)
    return quad[..., :, None] * quad[..., None, :] / jnp.sqrt(square + 0.25)


def selectors(blk):
    ao = lax.broadcasted_iota(jnp.int32, (blk, 2 * blk), 0)
    col = lax.broadcasted_iota(jnp.int32, (blk, 2 * blk), 1)
    return [(col == 2 * ao + c).astype(F32).astype(BF16) for c in range(2)]


def pack_kernel(where, trial, *refs):
    outs, (rows, sem) = refs[:-2], refs[-2:]
    nb, blk, width = outs[0].shape
    nocc = width // 2
    copies = []
    for i in range(len(outs)):
        for j in range(nb):
            at = (where[0] + j) * blk
            copies.append(
                pltpu.make_async_copy(trial.at[pl.ds(at, blk), where[1 + i]], rows.at[i, j], sem.at[i, j])
            )
    for c in copies:
        c.start()
    pick = jnp.concatenate(selectors(blk), axis=0)
    for i, out in enumerate(outs):
        for j in range(0, nb, 2):
            ahead = range(j, min(j + 2, nb))
            for k in ahead:
                copies[i * nb + k].wait()
            both = jnp.concatenate([rows[i, k].reshape(2 * blk, nocc) for k in ahead], axis=1)
            split = jnp.dot(pick, both, preferred_element_type=F32).astype(BF16)
            for k in ahead:
                for c in range(2):
                    piece = split[c * blk : (c + 1) * blk, (k - j) * nocc : (k - j + 1) * nocc]
                    out[k, :, c * nocc : (c + 1) * nocc] = piece


def pack(trial, where, planes, nb, blk):
    nocc = trial.shape[3]
    return pl.pallas_call(
        pack_kernel,
        out_shape=(jax.ShapeDtypeStruct((nb, blk, 2 * nocc), BF16),) * planes,
        in_specs=[SMEM, HBM],
        out_specs=(VMEM,) * planes,
        scratch_shapes=[pltpu.VMEM((planes, nb, blk, 2, nocc), BF16), pltpu.SemaphoreType.DMA((planes, nb))],
        compiler_params=params(((planes, nb, blk, 4 * nocc), 2), ((planes, nb, blk, 2 * nocc), 2)),
        name="pack",
    )(where, trial)


def occupied_kernel(ids, meta, occupied, values, keep, send, table):
    batches, sig = ids.shape
    blk, nocc = occupied.shape[0] // (table.shape[0] - 1), occupied.shape[2]
    nlocal = table.shape[0] - 1
    pick = selectors(blk)
    for j in range(nlocal):
        both = occupied[j * blk : (j + 1) * blk].reshape(2 * blk, nocc)
        for c in range(2):
            split = jnp.dot(pick[c], both, preferred_element_type=F32)
            table[j, :, c * nocc : (c + 1) * nocc] = split.astype(BF16)
    table[nlocal] = jnp.zeros(table.shape[1:], BF16)

    def block(b, s):
        local = ids[b, s] - meta[0]
        return table[jnp.where((local >= 0) & (local < nlocal), local, nlocal)]

    for b in range(batches):
        total = jnp.zeros(keep.shape[1:], F32)
        for s in range(0, sig, 2):
            two = jnp.concatenate([block(b, s), block(b, s + 1)], axis=0)
            total += jnp.dot(values[b, :, s * blk : (s + 2) * blk], two, preferred_element_type=F32)
        keep[b] = total
        send[b] = total.astype(BF16)


def occupied_part(occupied, colloc, blocks, meta, blk):
    batches, npts, _ = colloc.shape
    nocc = occupied.shape[2]
    shape = (batches, npts, 2 * nocc)
    return pl.pallas_call(
        occupied_kernel,
        out_shape=(jax.ShapeDtypeStruct(shape, F32), jax.ShapeDtypeStruct(shape, BF16)),
        in_specs=[SMEM, SMEM, VMEM, VMEM],
        out_specs=(VMEM, VMEM),
        scratch_shapes=[pltpu.VMEM((occupied.shape[0] // blk + 1, blk, 2 * nocc), BF16)],
        compiler_params=params((colloc.shape, 2), (occupied.shape, 4), (shape, 12), (shape, 12)),
        name="occupied",
    )(blocks, meta, occupied, colloc)


def potential_kernel(sizes, ids, meta, *refs):
    tmasks, xmasks, omasks, fmasks, nlocal, rank, first = sizes
    panels, refs = refs[: len(tmasks)], refs[len(tmasks) :]
    values, refs = refs[: len(xmasks)], refs[len(xmasks) :]
    occ, refs = refs[: len(omasks)], refs[len(omasks) :]
    kern, refs = refs[0], refs[1:]
    out, table, x, left, m, tsems, xsems = refs
    nb, blk, width = panels[0].shape
    count, npts = x.shape[1], x.shape[2]
    sig = ids.shape[2]
    copies = []
    for i, (over, side) in enumerate(tmasks):
        at = (meta[3] ^ over) * nlocal + (meta[4] ^ side) * nb
        copies.append(pltpu.make_async_copy(panels[i], table.at[pl.ds(at, nb)], tsems.at[i]))
    loads = []
    todo = []
    at = 0
    for i, piece in enumerate(values):
        loads.append(pltpu.make_async_copy(piece, x.at[pl.ds(at, piece.shape[0])], xsems.at[i]))
        for j, mask in enumerate(xmasks[i]):
            todo += [(i, at + j, mask, b) for b in range(count)]
        at += piece.shape[0]
    for c in copies + loads:
        c.start()
    where = {mask: (i, j) for i, masks in enumerate(omasks) for j, mask in enumerate(masks)}
    dims = (((1,), (1,)), ((), ()))

    def turn_of(mask, b):
        piece, row = where[mask]
        og = occ[piece][row, b]
        half = width // 2
        return jnp.concatenate([og, jnp.concatenate([-og[:, half:], og[:, :half]], axis=1)], axis=0)

    for c in copies:
        c.wait()
    seen = -1
    for i, (piece, row, mask, b) in enumerate(todo):
        if piece != seen:
            loads[piece].wait()
            seen = piece
        f = fmasks.index(mask)
        dens = jnp.zeros((npts, width), F32)
        for s in range(0, sig, 2):
            two = [table[ids[f, first + b, s + t]] for t in range(2)]
            dens += jnp.dot(
                x[row, b, :, s * blk : (s + 2) * blk], jnp.concatenate(two, axis=0), preferred_element_type=F32
            )
        left[i] = dens.astype(BF16)
    for i, (_, _, mask, b) in enumerate(todo):
        rho = lax.dot_general(left[i], turn_of(mask, first + b), dims, preferred_element_type=F32)
        weight = kern[fmasks.index(mask), first + b]
        m[i] = (rho * jnp.concatenate([weight, weight], axis=1)).astype(BF16)
    for i, (_, _, mask, b) in enumerate(todo):
        e = jnp.dot(m[i], turn_of(mask, first + b), preferred_element_type=F32)
        out[meta[5] ^ (mask // rank), b] = e.astype(BF16)


def potential(panels, values, occ, kern, ids, fmasks, meta, nlocal, rank, chunk):
    tmasks = tuple(m for _, m in panels)
    xmasks = tuple(tuple(m) for _, m in values)
    omasks = tuple(tuple(m) for _, m in occ)
    count, npts, span = values[0][0].shape[1:]
    nb, blk, width = panels[0][0].shape
    nsrc = sum(len(m) for m in xmasks)
    sizes = (tmasks, xmasks, omasks, tuple(fmasks), nlocal, rank, chunk * count)
    table = (len(panels) * nb, blk, width)
    x = (nsrc, count, npts, span)
    left = (nsrc * count, npts, width)
    m = (nsrc * count, npts, 2 * npts)
    return pl.pallas_call(
        functools.partial(potential_kernel, sizes),
        out_shape=jax.ShapeDtypeStruct((nsrc, count, npts, width), BF16),
        in_specs=[SMEM, SMEM] + [VMEM] * len(panels) + [ANY] * len(values) + [VMEM] * (len(occ) + 1),
        out_specs=VMEM,
        scratch_shapes=[
            pltpu.VMEM(table, BF16),
            pltpu.VMEM(x, BF16),
            pltpu.VMEM(left, BF16),
            pltpu.VMEM(m, BF16),
            pltpu.SemaphoreType.DMA((len(panels),)),
            pltpu.SemaphoreType.DMA((len(values),)),
        ],
        compiler_params=params((table, 4), (x, 2), (left, 8), (m, 2), (kern.shape, 4)),
        name="potential",
    )(ids, meta, *[a for a, _ in panels], *[a for a, _ in values], *[a for a, _ in occ], kern)


def list_kernel(sizes, ids, meta, facts, place):
    entries, nchunk, rank, nown = sizes
    sig = ids.shape[2]
    nlist = nchunk * rank
    sizes = []
    for t in range(nlist):
        n = jnp.int32(0)
        for f, b, mask, chunk, _, _ in entries:
            if chunk * rank + mask % rank == t:
                for s in range(sig):
                    own = ids[f, b, s] - meta[2]
                    n = n + ((own >= 0) & (own < nown)).astype(jnp.int32)
        sizes.append(n)
    n = jnp.int32(0)
    for t in range(nlist):
        facts[5, t] = n
        place[t] = n
        end = n + sizes[t]
        for k in range(3):
            for f, one in enumerate((0, 0, 0, -1, 0)):
                facts[f, end + k] = jnp.int32(one)
        n = lax.div(end + 3, 4) * 4
    facts[5, nlist] = n
    for f, b, mask, chunk, row, inner in entries:
        for s in range(sig):
            own = ids[f, b, s] - meta[2]

            @pl.when((own >= 0) & (own < nown))
            def _(mask=mask, t=chunk * rank + mask % rank, row=row, inner=inner, s=s, own=own):
                to = place[t]
                place[t] = to + 1
                what = (own, meta[5] ^ (mask // rank), jnp.int32(inner), jnp.int32(row), jnp.int32(s))
                for f, one in enumerate(what):
                    facts[f, to] = one


def entries_of(xmasks, fmasks, nchunk, count):
    out = []
    at = 0
    groups = len(xmasks) // nchunk
    for i, masks in enumerate(xmasks):
        chunk = i // groups
        for j, mask in enumerate(masks):
            out += [(fmasks.index(mask), chunk * count + b, mask, chunk, at + j, b) for b in range(count)]
        at += len(masks)
    return tuple(out)


def pair_list(xmasks, ids, fmasks, meta, rank, nown, nchunk, count, group):
    nsrc, _, sig = ids.shape
    most = -(-(nchunk * (nsrc * count * sig + 3 * rank) + 4) // group) * group
    sizes = (entries_of(xmasks, fmasks, nchunk, count), nchunk, rank, nown)
    return pl.pallas_call(
        functools.partial(list_kernel, sizes),
        out_shape=jax.ShapeDtypeStruct((8, most), jnp.int32),
        in_specs=[SMEM, SMEM],
        out_specs=SMEM,
        scratch_shapes=[pltpu.SMEM((nchunk * rank,), jnp.int32)],
        compiler_params=params(),
        name="pairs",
    )(ids, meta)


def gather_kernel(group, nlist, facts, *refs):
    values, (columns, x, rows, xsems, osems) = refs[:-5], refs[-5:]
    blk = rows.shape[1]
    copies = []
    at = 0
    for i, piece in enumerate(values):
        copies.append(pltpu.make_async_copy(piece, x.at[pl.ds(at, piece.shape[0])], xsems.at[i]))
        at += piece.shape[0]
    for c in copies:
        c.start()
    for c in copies:
        c.wait()
    n = facts[5, nlist]

    def one(i, carry):
        for t in range(4):
            row = facts[3, 4 * i + t]
            start = pl.multiple_of(facts[4, 4 * i + t] * blk, blk)
            column = x[jnp.maximum(row, 0), facts[2, 4 * i + t], :, pl.ds(start, blk)]
            rows[4 * i + t] = jnp.where(row >= 0, column, jnp.zeros_like(column)).T
        return carry

    lax.fori_loop(0, lax.div(n, 4), one, 0)
    outs = [
        pltpu.make_async_copy(rows.at[pl.ds(i * group, group)], columns.at[pl.ds(i * group, group)], osems.at[i])
        for i in range(columns.shape[0] // group)
    ]
    for act in ("start", "wait"):
        for i, c in enumerate(outs):

            @pl.when(i * group < n)
            def _(c=c, act=act):
                getattr(c, act)()


def gather(values, facts, blk, group, nlist):
    flat = [a for pieces in values for a, _ in pieces]
    count, npts, span = flat[0].shape[1:]
    most = facts.shape[1]
    return pl.pallas_call(
        functools.partial(gather_kernel, group, nlist),
        out_shape=jax.ShapeDtypeStruct((most, blk, npts), BF16),
        in_specs=[SMEM] + [ANY] * len(flat),
        out_specs=ANY,
        scratch_shapes=[
            pltpu.VMEM((sum(a.shape[0] for a in flat), count, npts, span), BF16),
            pltpu.VMEM((most, blk, npts), BF16),
            pltpu.SemaphoreType.DMA((len(flat),)),
            pltpu.SemaphoreType.DMA((most // group,)),
        ],
        compiler_params=params(((most, blk, npts), 2), ((sum(a.shape[0] for a in flat), count, npts, span), 2)),
        name="gather",
    )(facts, *flat)


def project_kernel(sizes, facts, meta, columns, *refs):
    nchunk, emasks, rank, group, nown, again = sizes
    ne = len(emasks)
    potentials, refs = refs[:ne], refs[ne + again :]
    out, x, staged, total, xsems, osems = refs
    blk = x.shape[1]
    offsets = sorted({mask // rank for _, masks in emasks for mask in masks})
    n = facts[5, nchunk * rank]
    xcopies = [
        pltpu.make_async_copy(columns.at[pl.ds(i * group, group)], x.at[pl.ds(i * group, group)], xsems.at[i])
        for i in range(columns.shape[0] // group)
    ]
    for i, c in enumerate(xcopies):

        @pl.when(i * group < n)
        def _(c=c):
            c.start()

    total[...] = jnp.zeros_like(total)
    for i, c in enumerate(xcopies):

        @pl.when(i * group < n)
        def _(c=c):
            c.wait()

    for t in range(nchunk * rank):
        mine = [
            (i, j, offsets.index(mask // rank))
            for i, (chunk, masks) in enumerate(emasks)
            for j, mask in enumerate(masks)
            if chunk * rank + mask % rank == t
        ]

        def one(p, carry, mine=mine):
            for at in range(4):
                own, source, b = [facts[f, 4 * p + at] for f in range(3)]
                for i, j, k in mine:
                    total[k, own] += jnp.dot(x[4 * p + at], potentials[i][j, source, b], preferred_element_type=F32)
            return carry

        lax.fori_loop(lax.div(facts[5, t], 4), lax.div(facts[5, t + 1], 4), one, 0)
    nocc = out.shape[2]
    copies = [
        pltpu.make_async_copy(staged.at[k], out.at[meta[5] ^ off], osems.at[k]) for k, off in enumerate(offsets)
    ]
    for k in range(len(offsets)):
        for o in range(nown):
            for c in range(2):
                staged[k, pl.ds(o * 2 * blk + c, blk, stride=2), :] = total[k, o, :, c * nocc : (c + 1) * nocc]
        copies[k].start()
    for c in copies:
        c.wait()


def project(potentials, facts, columns, meta, before, rank, nown, group):
    emasks = tuple((chunk, tuple(m)) for chunk, _, m in potentials)
    nchunk = 1 + max(chunk for chunk, _, _ in potentials)
    nv, _, _, width = potentials[0][1].shape[1:]
    blk = columns.shape[1]
    ne = len(potentials)
    again = before is not None
    nk = len({mask // rank for _, masks in emasks for mask in masks})
    args = [facts, meta, columns, *[a for _, a, _ in potentials]] + ([before] if again else [])
    staged = (nk, nown * blk * 2, width // 2)
    total = (nk, nown, blk, width)
    arrays = [(a.shape, 2) for _, a, _ in potentials]
    return pl.pallas_call(
        functools.partial(project_kernel, (nchunk, emasks, rank, group, nown, int(again))),
        out_shape=jax.ShapeDtypeStruct((nv, nown * blk * 2, width // 2), F32),
        in_specs=[SMEM] * 2 + [ANY] + [VMEM] * ne + [ANY] * int(again),
        out_specs=ANY,
        input_output_aliases={3 + ne: 0} if again else {},
        scratch_shapes=[
            pltpu.VMEM(columns.shape, BF16),
            pltpu.VMEM(staged, F32),
            pltpu.VMEM(total, F32),
            pltpu.SemaphoreType.DMA((columns.shape[0] // group,)),
            pltpu.SemaphoreType.DMA((nk,)),
        ],
        compiler_params=params((columns.shape, 2), (staged, 4), (total, 4), *arrays),
        name="project",
    )(*args)


def swap(array, axis, bit):
    size = lax.axis_size(axis)
    return lax.ppermute(array, axis, [(i, i ^ bit) for i in range(size)])


def across(part, bits):
    pieces = [(part, [0])]
    for bit in bits:
        for a, masks in pieces[:]:
            pieces.append((swap(a, "grid", bit), [m ^ bit for m in masks]))
    return pieces


def within(pieces, bits):
    for bit in bits:
        pieces = pieces + [(swap(a, "grid", bit), [m ^ bit for m in masks]) for a, masks in pieces]
    return pieces


def on_device(trial, occupied, colloc, blocks, coords, weights):
    n_ao, n_grid = lax.axis_size("ao"), lax.axis_size("grid")
    batches, npts, span = colloc.shape
    sig = blocks.shape[1]
    blk = span // sig
    nvec, nocc = trial.shape[1], trial.shape[3]
    nv = nvec // n_ao
    rank = n_grid // nv
    nlocal = trial.shape[0] // blk
    nown = nlocal * n_ao // n_grid
    parts = min(rank, nlocal & -nlocal)
    nb = nlocal // parts
    count = batches // 2
    ao, grid = lax.axis_index("ao"), lax.axis_index("grid")
    vector, side = grid // rank, grid % parts
    meta = jnp.stack([ao * nlocal, ao * 0, grid * nown, ao, side, vector]).astype(jnp.int32)
    high_bits = [rank << b for b in range(nv.bit_length() - 1)]
    low_bits = [1 << b for b in range(rank.bit_length() - 1)]
    part_bits = [1 << b for b in range(parts.bit_length() - 1)]

    panels = []
    far_first = list(reversed(range(n_ao)))
    for planes in (far_first[:1], far_first[1:]):
        where = jnp.stack([side * nb] + [(ao ^ over) * nv + vector for over in planes]).astype(jnp.int32)
        rows = pack(trial, where, len(planes), nb, blk)
        if not panels:
            rows, coords, weights = lax.optimization_barrier((rows, coords, weights))
        for over, one in zip(planes, rows, strict=True):
            panels.append((swap(one, "ao", over) if over else one, (over, 0)))

    near = []
    for chunk in range(2):
        part = colloc[None, chunk * count : (chunk + 1) * count]
        near.append(across(part, high_bits[::-1] if chunk else high_bits))
    far = [within(pieces, low_bits) for pieces in near]

    held, send = occupied_part(occupied, colloc, blocks, meta, blk)
    for s in range(n_ao.bit_length() - 1):
        got = swap(send, "ao", 1 << s)
        held = held + got.astype(F32)
        send = held.astype(BF16)
        whole = send[None]
    occ = across(whole, high_bits)

    numbers = jnp.pad(blocks.astype(F32), ((0, 0), (0, npts - sig)))
    extra = jnp.concatenate([numbers[:, None], coords, weights[:, None]], axis=1)
    extra = within(across(extra[None], high_bits), low_bits)
    fmasks = [m for _, masks in extra for m in masks]
    extra = jnp.concatenate([a for a, _ in extra], axis=0)
    ids = extra[:, :, 0, :sig].astype(jnp.int32)
    exact = extra[:nv, :, 1:]
    kern = kernel_matrix(exact[:, :, :3], exact[:, :, 3])
    group = 4 * sig
    xmasks = [m for pieces in far for _, m in pieces]
    facts = pair_list(xmasks, ids, fmasks, meta, rank, nown, 2, count, group)

    for bit in part_bits:
        panels = panels + [(swap(a, "grid", bit), (over, m ^ bit)) for a, (over, m) in panels]
    columns = gather(far, facts, blk, group, 2 * rank)
    early, late = [], []
    for chunk in range(2):
        e = potential(panels, near[chunk], occ, kern, ids, fmasks, meta, nlocal, rank, chunk)
        pieces = across(e[None], high_bits[::-1] if chunk else high_bits)
        early += [(chunk, a, m) for a, m in within(pieces[:-1], low_bits)]
        late += [(chunk, a, m) for a, m in within(pieces[-1:], low_bits)]
    total = project(early, facts, columns, meta, None, rank, nown, group)
    total = project(late, facts, columns, meta, total, rank, nown, group)
    return total.reshape(nv, nown * blk, 2, nocc)


def solution(mesh):
    in_specs = (
        P("ao", None, None, None),
        P("ao", None, None),
        P("grid", None, None),
        P("grid", None),
        P("grid", None, None),
        P("grid", None),
    )
    out_specs = P("ao", "grid", None, None)

    return jax.shard_map(on_device, mesh=mesh, in_specs=in_specs, out_specs=out_specs, check_vma=False)
```

profile of v0, /device:TPU:0, one launch (start us, length us, event | category | flops | bytes accessed | tf_op | source)
XLA Modules:
  0.0 234.0 jit_solution(5398842173091742814)
XLA Ops:
  6.0 3.1 %collective-permute-start.28 = (bf16[4,128,256]{2,1,0:T(8,128)(2,1)S(1)}, bf16[4,128,256]{2,1,0:T(8,128)(2,1)S(1)}, u32[]{:S(2)}, u32[]{:S(2)}) collective-permute-start(bf16[4,128,256]{2,1,0:T(8,128)(2,1)S(1)} %get-tuple-element.20), channel_id=1, source_target_pairs={{0,1},{1,0},{2,3},{3,2},{4,5},{5,4},{6,7},{7,6},{8,9},{9,8},{10,11... | collective-permute-start | bytes 786440 | tf_op jit(solution)/shard_map/ppermute | solution.py:410
  9.1 6.3 %collective-permute-done.28 = bf16[4,128,256]{2,1,0:T(8,128)(2,1)S(1)} collective-permute-done((bf16[4,128,256]{2,1,0:T(8,128)(2,1)S(1)}, bf16[4,128,256]{2,1,0:T(8,128)(2,1)S(1)}, u32[]{:S(2)}, u32[]{:S(2)}) %collective-permute-start.28) | collective-permute-done | bytes 262176 | tf_op jit(solution)/shard_map/ppermute | solution.py:410
  22.1 8.1 %collective-permute-done.29 = bf16[4,128,256]{2,1,0:T(8,128)(2,1)} collective-permute-done((bf16[4,128,256]{2,1,0:T(8,128)(2,1)S(1)}, bf16[4,128,256]{2,1,0:T(8,128)(2,1)}, u32[]{:S(2)}, u32[]{:S(2)}) %collective-permute-start.29) | collective-permute-done | bytes 262176 | tf_op jit(solution)/shard_map/ppermute | solution.py:410
  34.6 8.2 %copy-done.1 = bf16[3072,16,2,128]{3,2,1,0:T(2,128)(2,1)S(1)} copy-done((bf16[3072,16,2,128]{3,2,1,0:T(2,128)(2,1)S(1)}, bf16[3072,16,2,128]{3,2,1,0:T(2,128)(2,1)}, u32[]{:S(2)}) %copy-start.1) | copy-done | bytes 25165848
  42.7 3.6 %pack.2 = bf16[12,128,256]{2,1,0:T(8,128)(2,1)} custom-call(s32[2]{0:T(128)S(1)} %pad_add_fusion.where, bf16[3072,16,2,128]{3,2,1,0:T(2,128)(2,1)S(1)} %copy-done.1), custom_call_target="tpu_custom_call" | custom-call | tf_op jit(solution)/shard_map/pack/pallas_call | solution.py:68
  46.9 3.1 %collective-permute-done = f32[1,4,5,128]{3,1,0,2:T(4,128)S(1)} collective-permute-done((f32[1,4,5,128]{3,1,0,2:T(4,128)S(1)}, f32[1,4,5,128]{3,1,0,2:T(4,128)S(1)}, u32[]{:S(2)}, u32[]{:S(2)}) %collective-permute-start) | collective-permute-done | bytes 10272 | tf_op jit(solution)/shard_map/ppermute | solution.py:410
  50.6 3.1 %collective-permute-done.1 = f32[1,4,5,128]{3,1,0,2:T(4,128)S(1)} collective-permute-done((f32[1,4,5,128]{3,1,0,2:T(4,128)S(1)}, f32[1,4,5,128]{3,1,0,2:T(4,128)S(1)}, u32[]{:S(2)}, u32[]{:S(2)}) %collective-permute-start.1) | collective-permute-done | bytes 10272 | tf_op jit(solution)/shard_map/ppermute | solution.py:410
  55.4 3.1 %collective-permute-done.2 = f32[1,4,5,128]{3,1,0,2:T(4,128)S(1)} collective-permute-done((f32[1,4,5,128]{3,1,0,2:T(4,128)S(1)}, f32[1,4,5,128]{3,1,0,2:T(4,128)S(1)}, u32[]{:S(2)}, u32[]{:S(2)}) %collective-permute-start.2) | collective-permute-done | bytes 10272 | tf_op jit(solution)/shard_map/ppermute | solution.py:410
  64.2 3.4 %collective-permute-start.21 = (bf16[12,128,256]{2,1,0:T(8,128)(2,1)}, bf16[12,128,256]{2,1,0:T(8,128)(2,1)}, u32[]{:S(2)}, u32[]{:S(2)}) collective-permute-start(bf16[12,128,256]{2,1,0:T(8,128)(2,1)} %pack.2), channel_id=1, source_target_pairs={{0,3},{1,2},{2,1},{3,0},{4,7},{5,6},{6,5},{7,4},{8,11},{9,10},{10,... | collective-permute-start | bytes 2359304 | tf_op jit(solution)/shard_map/ppermute | solution.py:410
  67.7 8.2 %copy-done.2 = bf16[3072,16,2,128]{3,2,1,0:T(2,128)(2,1)S(1)} copy-done((bf16[3072,16,2,128]{3,2,1,0:T(2,128)(2,1)S(1)}, bf16[3072,16,2,128]{3,2,1,0:T(2,128)(2,1)}, u32[]{:S(2)}) %copy-start.2) | copy-done | bytes 25165848
  75.9 6.9 %pack.3 = (bf16[12,128,256]{2,1,0:T(8,128)(2,1)S(1)}, bf16[12,128,256]{2,1,0:T(8,128)(2,1)S(1)}, bf16[12,128,256]{2,1,0:T(8,128)(2,1)S(1)}) custom-call(s32[4]{0:T(128)S(1)} %pad_add_fusion.1.where, bf16[3072,16,2,128]{3,2,1,0:T(2,128)(2,1)S(1)} %copy-done.2), custom_call_target="tpu_custom_call" | custom-call | tf_op jit(solution)/shard_map/pack/pallas_call | solution.py:68
  86.9 47.9 %collective-permute-done.22.refs_1_ = bf16[12,128,256]{2,1,0:T(8,128)(2,1)S(1)} collective-permute-done((bf16[12,128,256]{2,1,0:T(8,128)(2,1)S(1)}, bf16[12,128,256]{2,1,0:T(8,128)(2,1)S(1)}, u32[]{:S(2)}, u32[]{:S(2)}) %collective-permute-start.22) | collective-permute-done | bytes 786464 | tf_op jit(solution)/shard_map/ppermute | solution.py:410
  138.1 4.5 %collective-permute-done.32.refs_15_ = bf16[1,4,128,256]{3,2,1,0:T(8,128)(2,1)S(1)} collective-permute-done((bf16[1,4,128,256]{3,2,1,0:T(8,128)(2,1)S(1)}, bf16[1,4,128,256]{3,2,1,0:T(8,128)(2,1)S(1)}, u32[]{:S(2)}, u32[]{:S(2)}) %collective-permute-start.32) | collective-permute-done | bytes 262176 | tf_op jit(solution)/shard_map/ppermute | solution.py:410
  145.6 4.0 %potential.2 = bf16[4,2,128,256]{3,2,1,0:T(8,128)(2,1)S(1)} custom-call(s32[8,4,12]{2,1,0:T(4,128)S(1)} %fusion.2.ids, s32[6]{0:T(128)S(1)} %stack.48.meta, bf16[12,128,256]{2,1,0:T(8,128)(2,1)} %collective-permute-done.21.refs_0_, bf16[12,128,256]{2,1,0:T(8,128)(2,1)S(1)} %collective-permute-done.22.refs_1_, ...), custom_call_target="tpu_custom_call" | custom-call | tf_op jit(solution)/shard_map/potential/pallas_call | solution.py:188
  149.6 11.4 %collective-permute-done.16.refs_11_ = bf16[1,2,128,1536]{3,2,1,0:T(8,128)(2,1)S(1)} collective-permute-done((bf16[1,2,128,1536]{3,2,1,0:T(8,128)(2,1)}, bf16[1,2,128,1536]{3,2,1,0:T(8,128)(2,1)S(1)}, u32[]{:S(2)}, u32[]{:S(2)}) %collective-permute-start.16) | collective-permute-done | bytes 786464 | tf_op jit(solution)/shard_map/ppermute | solution.py:410
  162.5 4.5 %potential.3 = bf16[4,2,128,256]{3,2,1,0:T(8,128)(2,1)S(1)} custom-call(s32[8,4,12]{2,1,0:T(4,128)S(1)} %fusion.2.ids, s32[6]{0:T(128)S(1)} %stack.48.meta, bf16[12,128,256]{2,1,0:T(8,128)(2,1)} %collective-permute-done.21.refs_0_, bf16[12,128,256]{2,1,0:T(8,128)(2,1)S(1)} %collective-permute-done.22.refs_1_, ...), custom_call_target="tpu_custom_call" | custom-call | tf_op jit(solution)/shard_map/potential/pallas_call | solution.py:188
  169.7 3.4 %collective-permute-done.33.refs_1_ = bf16[1,4,2,128,256]{4,3,2,1,0:T(8,128)(2,1)S(1)} collective-permute-done((bf16[1,4,2,128,256]{4,3,2,1,0:T(8,128)(2,1)S(1)}, bf16[1,4,2,128,256]{4,3,2,1,0:T(8,128)(2,1)S(1)}, u32[]{:S(2)}, u32[]{:S(2)}) %collective-permute-start.33) | collective-permute-done | bytes 524320 | tf_op jit(solution)/shard_map/ppermute | solution.py:410
  173.2 8.7 %collective-permute-done.36.refs_7_ = bf16[1,4,2,128,256]{4,3,2,1,0:T(8,128)(2,1)S(1)} collective-permute-done((bf16[1,4,2,128,256]{4,3,2,1,0:T(8,128)(2,1)S(1)}, bf16[1,4,2,128,256]{4,3,2,1,0:T(8,128)(2,1)S(1)}, u32[]{:S(2)}, u32[]{:S(2)}) %collective-permute-start.36) | collective-permute-done | bytes 524320 | tf_op jit(solution)/shard_map/ppermute | solution.py:410
  181.9 7.9 %collective-permute-done.39.refs_2_ = bf16[1,4,2,128,256]{4,3,2,1,0:T(8,128)(2,1)S(1)} collective-permute-done((bf16[1,4,2,128,256]{4,3,2,1,0:T(8,128)(2,1)S(1)}, bf16[1,4,2,128,256]{4,3,2,1,0:T(8,128)(2,1)S(1)}, u32[]{:S(2)}, u32[]{:S(2)}) %collective-permute-start.39) | collective-permute-done | bytes 524320 | tf_op jit(solution)/shard_map/ppermute | solution.py:410
  192.4 11.7 %collective-permute-done.34.refs_0_ = bf16[1,4,2,128,256]{4,3,2,1,0:T(8,128)(2,1)S(1)} collective-permute-done((bf16[1,4,2,128,256]{4,3,2,1,0:T(8,128)(2,1)S(1)}, bf16[1,4,2,128,256]{4,3,2,1,0:T(8,128)(2,1)S(1)}, u32[]{:S(2)}, u32[]{:S(2)}) %collective-permute-start.34) | collective-permute-done | bytes 524320 | tf_op jit(solution)/shard_map/ppermute | solution.py:410
  205.8 4.8 %pairs.1.facts = s32[8,432]{1,0:T(8,128)S(1)} custom-call(s32[8,4,12]{2,1,0:T(4,128)S(1)} %fusion.2.ids, s32[6]{0:T(128)S(1)} %stack.48.meta), custom_call_target="tpu_custom_call" | custom-call | tf_op jit(solution)/shard_map/pairs/pallas_call | solution.py:258
  210.7 6.3 %gather.1.columns = bf16[432,128,128]{2,1,0:T(8,128)(2,1)} custom-call(s32[8,432]{1,0:T(8,128)S(1)} %pairs.1.facts, bf16[1,2,128,1536]{3,2,1,0:T(8,128)(2,1)S(1)} %get-tuple-element.22.refs_0_.refs_8_, bf16[1,2,128,1536]{3,2,1,0:T(8,128)(2,1)S(1)} %collective-permute-done.7.refs_1_.refs_9_, ...), custom_call_target="tpu_custom_call" | custom-call | tf_op jit(solution)/shard_map/gather/pallas_call | solution.py:308
  217.0 10.8 %project.2.refs_4_ = f32[4,3072,128]{2,1,0:T(8,128)} custom-call(s32[8,432]{1,0:T(8,128)S(1)} %pairs.1.facts, s32[6]{0:T(128)S(1)} %stack.48.meta, bf16[432,128,128]{2,1,0:T(8,128)(2,1)} %gather.1.columns, bf16[1,4,2,128,256]{4,3,2,1,0:T(8,128)(2,1)S(1)} %bitcast.33, bf16[1,4,2,128,256]{4,3,2,1,0:T(8,128)(2,1)S(1)} %collective-permute-done.33.refs_1_, ...), custom_call_target="tpu_custom_call" | custom-call | tf_op jit(solution)/shard_map/project/pallas_call | solution.py:390
  227.9 6.0 %project.3 = f32[4,3072,128]{2,1,0:T(8,128)} custom-call(s32[8,432]{1,0:T(8,128)S(1)} %pairs.1.facts, s32[6]{0:T(128)S(1)} %stack.48.meta, bf16[432,128,128]{2,1,0:T(8,128)(2,1)S(1)} %copy-done, bf16[1,4,2,128,256]{4,3,2,1,0:T(8,128)(2,1)S(1)} %collective-permute-done.34.refs_0_, ...), custom_call_target="tpu_custom_call", output_to_operand_aliasing={{}: (7, {})} | custom-call | tf_op jit(solution)/shard_map/project/pallas_call | solution.py:390
  (134 shorter events, 44.4 us)
Async XLA Ops:
  19.0 45.2 %collective-permute-start.7 = (bf16[1,2,128,1536]{3,2,1,0:T(8,128)(2,1)S(1)}, bf16[1,2,128,1536]{3,2,1,0:T(8,128)(2,1)S(1)}, u32[]{:S(2)}, u32[]{:S(2)}) collective-permute-start(bf16[1,2,128,1536]{3,2,1,0:T(8,128)(2,1)S(1)} %get-tuple-element.22.refs_0_.refs_8_), channel_id=1, source_target_pairs={{0,8},{4,12},{8,0},{12,4},{16,24},{20,28},{24,16},{28,20},{1,9},{5... | collective-permute-start | bytes 2359304 | tf_op jit(solution)/shard_map/ppermute | solution.py:410
  20.6 43.6 %collective-permute-start.8 = (bf16[1,2,128,1536]{3,2,1,0:T(8,128)(2,1)S(1)}, bf16[1,2,128,1536]{3,2,1,0:T(8,128)(2,1)S(1)}, u32[]{:S(2)}, u32[]{:S(2)}) collective-permute-start(bf16[1,2,128,1536]{3,2,1,0:T(8,128)(2,1)S(1)} %get-tuple-element.22.refs_0_.refs_8_), channel_id=1, source_target_pairs={{0,16},{4,20},{8,24},{12,28},{16,0},{20,4},{24,8},{28,12},{1,17},{... | collective-permute-start | bytes 2359304 | tf_op jit(solution)/shard_map/ppermute | solution.py:410
  31.5 30.7 %collective-permute-start.30 = (bf16[1,4,128,256]{3,2,1,0:T(8,128)(2,1)S(1)}, bf16[1,4,128,256]{3,2,1,0:T(8,128)(2,1)S(1)}, u32[]{:S(2)}, u32[]{:S(2)}) collective-permute-start(bf16[1,4,128,256]{3,2,1,0:T(8,128)(2,1)S(1)} %fusion.1.refs_12_), channel_id=1, source_target_pairs={{0,8},{4,12},{8,0},{12,4},{16,24},{20,28},{24,16},{28,20},{1,9},{5... | collective-permute-start | bytes 786440 | tf_op jit(solution)/shard_map/ppermute | solution.py:410
  33.0 29.8 %collective-permute-start.31 = (bf16[1,4,128,256]{3,2,1,0:T(8,128)(2,1)S(1)}, bf16[1,4,128,256]{3,2,1,0:T(8,128)(2,1)S(1)}, u32[]{:S(2)}, u32[]{:S(2)}) collective-permute-start(bf16[1,4,128,256]{3,2,1,0:T(8,128)(2,1)S(1)} %fusion.1.refs_12_), channel_id=1, source_target_pairs={{0,16},{4,20},{8,24},{12,28},{16,0},{20,4},{24,8},{28,12},{1,17},{... | collective-permute-start | bytes 786440 | tf_op jit(solution)/shard_map/ppermute | solution.py:410
  62.1 20.7 %collective-permute-start.10 = (bf16[1,2,128,1536]{3,2,1,0:T(8,128)(2,1)S(1)}, bf16[1,2,128,1536]{3,2,1,0:T(8,128)(2,1)}, u32[]{:S(2)}, u32[]{:S(2)}) collective-permute-start(bf16[1,2,128,1536]{3,2,1,0:T(8,128)(2,1)S(1)} %get-tuple-element.22.refs_0_.refs_8_), channel_id=1, source_target_pairs={{0,4},{4,0},{8,12},{12,8},{16,20},{20,16},{24,28},{28,24},{1,5},{5... | collective-permute-start | bytes 2359304 | tf_op jit(solution)/shard_map/ppermute | solution.py:410
  62.3 20.6 %collective-permute-start.14 = (bf16[1,2,128,1536]{3,2,1,0:T(8,128)(2,1)S(1)}, bf16[1,2,128,1536]{3,2,1,0:T(8,128)(2,1)}, u32[]{:S(2)}, u32[]{:S(2)}) collective-permute-start(bf16[1,2,128,1536]{3,2,1,0:T(8,128)(2,1)S(1)} %get-tuple-element.21.refs_8_), channel_id=1, source_target_pairs={{0,16},{4,20},{8,24},{12,28},{16,0},{20,4},{24,8},{28,12},{1,17},{... | collective-permute-start | bytes 2359304 | tf_op jit(solution)/shard_map/ppermute | solution.py:410
  63.5 20.4 %collective-permute-start.15 = (bf16[1,2,128,1536]{3,2,1,0:T(8,128)(2,1)S(1)}, bf16[1,2,128,1536]{3,2,1,0:T(8,128)(2,1)}, u32[]{:S(2)}, u32[]{:S(2)}) collective-permute-start(bf16[1,2,128,1536]{3,2,1,0:T(8,128)(2,1)S(1)} %get-tuple-element.21.refs_8_), channel_id=1, source_target_pairs={{0,8},{4,12},{8,0},{12,4},{16,24},{20,28},{24,16},{28,20},{1,9},{5... | collective-permute-start | bytes 2359304 | tf_op jit(solution)/shard_map/ppermute | solution.py:410
  64.2 22.7 %collective-permute-start.21 = (bf16[12,128,256]{2,1,0:T(8,128)(2,1)}, bf16[12,128,256]{2,1,0:T(8,128)(2,1)}, u32[]{:S(2)}, u32[]{:S(2)}) collective-permute-start(bf16[12,128,256]{2,1,0:T(8,128)(2,1)} %pack.2), channel_id=1, source_target_pairs={{0,3},{1,2},{2,1},{3,0},{4,7},{5,6},{6,5},{7,4},{8,11},{9,10},{10,... | collective-permute-start | bytes 2359304 | tf_op jit(solution)/shard_map/ppermute | solution.py:410
  82.8 52.0 %collective-permute-start.22 = (bf16[12,128,256]{2,1,0:T(8,128)(2,1)S(1)}, bf16[12,128,256]{2,1,0:T(8,128)(2,1)S(1)}, u32[]{:S(2)}, u32[]{:S(2)}) collective-permute-start(bf16[12,128,256]{2,1,0:T(8,128)(2,1)S(1)} %get-tuple-element.16), channel_id=1, source_target_pairs={{0,2},{1,3},{2,0},{3,1},{4,6},{5,7},{6,4},{7,5},{8,10},{9,11},{10,... | collective-permute-start | bytes 2359304 | tf_op jit(solution)/shard_map/ppermute | solution.py:410
  82.9 53.4 %collective-permute-start.23 = (bf16[12,128,256]{2,1,0:T(8,128)(2,1)S(1)}, bf16[12,128,256]{2,1,0:T(8,128)(2,1)S(1)}, u32[]{:S(2)}, u32[]{:S(2)}) collective-permute-start(bf16[12,128,256]{2,1,0:T(8,128)(2,1)S(1)} %get-tuple-element.17), channel_id=1, source_target_pairs={{0,1},{1,0},{2,3},{3,2},{4,5},{5,4},{6,7},{7,6},{8,9},{9,8},{10,11... | collective-permute-start | bytes 2359304 | tf_op jit(solution)/shard_map/ppermute | solution.py:410
  83.9 52.4 %collective-permute-start.27 = (bf16[12,128,256]{2,1,0:T(8,128)(2,1)S(1)}, bf16[12,128,256]{2,1,0:T(8,128)(2,1)S(1)}, u32[]{:S(2)}, u32[]{:S(2)}) collective-permute-start(bf16[12,128,256]{2,1,0:T(8,128)(2,1)S(1)} %get-tuple-element.18.refs_3_), channel_id=1, source_target_pairs={{0,4},{4,0},{8,12},{12,8},{16,20},{20,16},{24,28},{28,24},{1,5},{5... | collective-permute-start | bytes 2359304 | tf_op jit(solution)/shard_map/ppermute | solution.py:410
  84.0 60.4 %collective-permute-start.9 = (bf16[1,2,128,1536]{3,2,1,0:T(8,128)(2,1)S(1)}, bf16[1,2,128,1536]{3,2,1,0:T(8,128)(2,1)S(1)}, u32[]{:S(2)}, u32[]{:S(2)}) collective-permute-start(bf16[1,2,128,1536]{3,2,1,0:T(8,128)(2,1)S(1)} %collective-permute-done.7.refs_1_.refs_9_), channel_id=1, source_target_pairs={{0,16},{4,20},{8,24},{12,28},{16,0},{20,4},{24,8},{28,12},{1,17},{... | collective-permute-start | bytes 2359304 | tf_op jit(solution)/shard_map/ppermute | solution.py:410
  86.9 57.6 %collective-permute-start.24 = (bf16[12,128,256]{2,1,0:T(8,128)(2,1)}, bf16[12,128,256]{2,1,0:T(8,128)(2,1)S(1)}, u32[]{:S(2)}, u32[]{:S(2)}) collective-permute-start(bf16[12,128,256]{2,1,0:T(8,128)(2,1)} %collective-permute-done.21.refs_0_), channel_id=1, source_target_pairs={{0,4},{4,0},{8,12},{12,8},{16,20},{20,16},{24,28},{28,24},{1,5},{5... | collective-permute-start | bytes 2359304 | tf_op jit(solution)/shard_map/ppermute | solution.py:410
  144.4 22.6 %collective-permute-start.11 = (bf16[1,2,128,1536]{3,2,1,0:T(8,128)(2,1)S(1)}, bf16[1,2,128,1536]{3,2,1,0:T(8,128)(2,1)S(1)}, u32[]{:S(2)}, u32[]{:S(2)}) collective-permute-start(bf16[1,2,128,1536]{3,2,1,0:T(8,128)(2,1)S(1)} %collective-permute-done.7.refs_1_.refs_9_), channel_id=1, source_target_pairs={{0,4},{4,0},{8,12},{12,8},{16,20},{20,16},{24,28},{28,24},{1,5},{5... | collective-permute-start | bytes 2359304 | tf_op jit(solution)/shard_map/ppermute | solution.py:410
  144.5 24.1 %collective-permute-start.12 = (bf16[1,2,128,1536]{3,2,1,0:T(8,128)(2,1)S(1)}, bf16[1,2,128,1536]{3,2,1,0:T(8,128)(2,1)S(1)}, u32[]{:S(2)}, u32[]{:S(2)}) collective-permute-start(bf16[1,2,128,1536]{3,2,1,0:T(8,128)(2,1)S(1)} %collective-permute-done.8.refs_2_.refs_10_), channel_id=1, source_target_pairs={{0,4},{4,0},{8,12},{12,8},{16,20},{20,16},{24,28},{28,24},{1,5},{5... | collective-permute-start | bytes 2359304 | tf_op jit(solution)/shard_map/ppermute | solution.py:410
  145.0 24.1 %collective-permute-start.18 = (bf16[1,2,128,1536]{3,2,1,0:T(8,128)(2,1)}, bf16[1,2,128,1536]{3,2,1,0:T(8,128)(2,1)S(1)}, u32[]{:S(2)}, u32[]{:S(2)}) collective-permute-start(bf16[1,2,128,1536]{3,2,1,0:T(8,128)(2,1)} %collective-permute-done.14.refs_9_), channel_id=1, source_target_pairs={{0,4},{4,0},{8,12},{12,8},{16,20},{20,16},{24,28},{28,24},{1,5},{5... | collective-permute-start | bytes 2359304 | tf_op jit(solution)/shard_map/ppermute | solution.py:410
  145.2 23.9 %collective-permute-start.19 = (bf16[1,2,128,1536]{3,2,1,0:T(8,128)(2,1)}, bf16[1,2,128,1536]{3,2,1,0:T(8,128)(2,1)S(1)}, u32[]{:S(2)}, u32[]{:S(2)}) collective-permute-start(bf16[1,2,128,1536]{3,2,1,0:T(8,128)(2,1)} %collective-permute-done.15.refs_10_), channel_id=1, source_target_pairs={{0,4},{4,0},{8,12},{12,8},{16,20},{20,16},{24,28},{28,24},{1,5},{5... | collective-permute-start | bytes 2359304 | tf_op jit(solution)/shard_map/ppermute | solution.py:410
  168.6 21.1 %collective-permute-start.39 = (bf16[1,4,2,128,256]{4,3,2,1,0:T(8,128)(2,1)S(1)}, bf16[1,4,2,128,256]{4,3,2,1,0:T(8,128)(2,1)S(1)}, u32[]{:S(2)}, u32[]{:S(2)}) collective-permute-start(bf16[1,4,2,128,256]{4,3,2,1,0:T(8,128)(2,1)S(1)} %bitcast.31), channel_id=1, source_target_pairs={{0,16},{4,20},{8,24},{12,28},{16,0},{20,4},{24,8},{28,12},{1,17},{... | collective-permute-start | bytes 1572872 | tf_op jit(solution)/shard_map/ppermute | solution.py:410
  169.1 20.6 %collective-permute-start.40 = (bf16[1,4,2,128,256]{4,3,2,1,0:T(8,128)(2,1)S(1)}, bf16[1,4,2,128,256]{4,3,2,1,0:T(8,128)(2,1)S(1)}, u32[]{:S(2)}, u32[]{:S(2)}) collective-permute-start(bf16[1,4,2,128,256]{4,3,2,1,0:T(8,128)(2,1)S(1)} %bitcast.32), channel_id=1, source_target_pairs={{0,4},{4,0},{8,12},{12,8},{16,20},{20,16},{24,28},{28,24},{1,5},{5... | collective-permute-start | bytes 1572872 | tf_op jit(solution)/shard_map/ppermute | solution.py:410
  169.1 22.1 %collective-permute-start.43 = (bf16[1,4,2,128,256]{4,3,2,1,0:T(8,128)(2,1)S(1)}, bf16[1,4,2,128,256]{4,3,2,1,0:T(8,128)(2,1)S(1)}, u32[]{:S(2)}, u32[]{:S(2)}) collective-permute-start(bf16[1,4,2,128,256]{4,3,2,1,0:T(8,128)(2,1)S(1)} %bitcast.35), channel_id=1, source_target_pairs={{0,8},{4,12},{8,0},{12,4},{16,24},{20,28},{24,16},{28,20},{1,9},{5... | collective-permute-start | bytes 1572872 | tf_op jit(solution)/shard_map/ppermute | solution.py:410
  191.8 25.1 %collective-permute-start.45 = (bf16[1,4,2,128,256]{4,3,2,1,0:T(8,128)(2,1)S(1)}, bf16[1,4,2,128,256]{4,3,2,1,0:T(8,128)(2,1)S(1)}, u32[]{:S(2)}, u32[]{:S(2)}) collective-permute-start(bf16[1,4,2,128,256]{4,3,2,1,0:T(8,128)(2,1)S(1)} %collective-permute-done.36.refs_7_), channel_id=1, source_target_pairs={{0,4},{4,0},{8,12},{12,8},{16,20},{20,16},{24,28},{28,24},{1,5},{5... | collective-permute-start | bytes 1572872 | tf_op jit(solution)/shard_map/ppermute | solution.py:410
  192.3 24.6 %collective-permute-start.42 = (bf16[1,4,2,128,256]{4,3,2,1,0:T(8,128)(2,1)S(1)}, bf16[1,4,2,128,256]{4,3,2,1,0:T(8,128)(2,1)S(1)}, u32[]{:S(2)}, u32[]{:S(2)}) collective-permute-start(bf16[1,4,2,128,256]{4,3,2,1,0:T(8,128)(2,1)S(1)} %collective-permute-done.39.refs_2_), channel_id=1, source_target_pairs={{0,4},{4,0},{8,12},{12,8},{16,20},{20,16},{24,28},{28,24},{1,5},{5... | collective-permute-start | bytes 1572872 | tf_op jit(solution)/shard_map/ppermute | solution.py:410
  205.3 22.5 %collective-permute-start.35 = (bf16[1,4,2,128,256]{4,3,2,1,0:T(8,128)(2,1)S(1)}, bf16[1,4,2,128,256]{4,3,2,1,0:T(8,128)(2,1)S(1)}, u32[]{:S(2)}, u32[]{:S(2)}) collective-permute-start(bf16[1,4,2,128,256]{4,3,2,1,0:T(8,128)(2,1)S(1)} %collective-permute-done.34.refs_0_), channel_id=1, source_target_pairs={{0,4},{4,0},{8,12},{12,8},{16,20},{20,16},{24,28},{28,24},{1,5},{5... | collective-permute-start | bytes 1572872 | tf_op jit(solution)/shard_map/ppermute | solution.py:410
  205.3 22.5 %collective-permute-start.38 = (bf16[1,4,2,128,256]{4,3,2,1,0:T(8,128)(2,1)S(1)}, bf16[1,4,2,128,256]{4,3,2,1,0:T(8,128)(2,1)S(1)}, u32[]{:S(2)}, u32[]{:S(2)}) collective-permute-start(bf16[1,4,2,128,256]{4,3,2,1,0:T(8,128)(2,1)S(1)} %collective-permute-done.37.refs_2_), channel_id=1, source_target_pairs={{0,4},{4,0},{8,12},{12,8},{16,20},{20,16},{24,28},{28,24},{1,5},{5... | collective-permute-start | bytes 1572872 | tf_op jit(solution)/shard_map/ppermute | solution.py:410
  (39 other events, 422.2 us)
where the time goes:
time: 239 us; the launch traced here: 234 us
  waiting for transfers between devices  126 us (53%)
  Pallas kernels  49.3 us (21%)
  starting transfers between devices  33.2 us (14%)
  local copies, waits for them, and re-layouts  21.5 us (9%)
  other arithmetic  3.06 us (1%)
    ppermute x47, waiting for transfers between devices, swap(): return lax.ppermute(array, axis, [(i, i ^ bit) for i in range(size)])  126 us
    ppermute x47, starting transfers between devices, swap(): return lax.ppermute(array, axis, [(i, i ^ bit) for i in range(size)])  33.2 us
    unnamed x38, local copies, waits for them, and re-layouts  21.3 us
    pallas_call x2, Pallas kernels, project(): pl.pallas_call(functools.partial(project_kernel, (nchunk, emasks, rank, g...  16.8 us
    pallas_call x2, Pallas kernels, pack(): pl.pallas_call(pack_kernel, out_shape=(jax.ShapeDtypeStruct((nb, blk, 2 *...  10.5 us
    pallas_call x2, Pallas kernels, potential(): pl.pallas_call(functools.partial(potential_kernel, sizes), out_shape=jax....  8.47 us
    pallas_call x1, Pallas kernels, gather(): pl.pallas_call(functools.partial(gather_kernel, group, nlist), out_shape=...  6.28 us
    pallas_call x1, Pallas kernels, pair_list(): pl.pallas_call(functools.partial(list_kernel, sizes), out_shape=jax.Shape...  4.83 us
  transfers between devices with their start and end apart: 47, of which 18 were waited for; matrix products, arithmetic and copies ran while one was open for 1% of the time, Pallas kernels for 17%

commit v1 on v0

--- a/solution.py
+++ b/solution.py
@@ -21,7 +21,6 @@
 SMEM = pl.BlockSpec(memory_space=pltpu.SMEM)
 VMEM = pl.BlockSpec(memory_space=pltpu.VMEM)
 ANY = pl.BlockSpec(memory_space=pl.ANY)
-HBM = pl.BlockSpec(memory_space=pltpu.HBM)
 
 
 def kernel_matrix(points, quad):
@@ -68,10 +67,10 @@
     return pl.pallas_call(
         pack_kernel,
         out_shape=(jax.ShapeDtypeStruct((nb, blk, 2 * nocc), BF16),) * planes,
-        in_specs=[SMEM, HBM],
+        in_specs=[SMEM, ANY],
         out_specs=(VMEM,) * planes,
         scratch_shapes=[pltpu.VMEM((planes, nb, blk, 2, nocc), BF16), pltpu.SemaphoreType.DMA((planes, nb))],
-        compiler_params=params(((planes, nb, blk, 4 * nocc), 2), ((planes, nb, blk, 2 * nocc), 2)),
+        compiler_params=pltpu.CompilerParams(vmem_limit_bytes=52 * MIB),
         name="pack",
     )(where, trial)
 

time: 239 us -> 233 us (0.975)
  the two profiles are of different devices: /device:TPU:0 before, /device:TPU:1 now
where the time goes in v1:
time: 233 us
  waiting for transfers between devices  110 us (47%)
  starting transfers between devices  58.9 us (25%)
  Pallas kernels  54.8 us (24%)
  local copies, waits for them, and re-layouts  4.51 us (2%)
  other arithmetic  3.82 us (2%)
    ppermute x47, waiting for transfers between devices, swap(): return lax.ppermute(array, axis, [(i, i ^ bit) for i in range(size)])  110 us
    ppermute x47, starting transfers between devices, swap(): return lax.ppermute(array, axis, [(i, i ^ bit) for i in range(size)])  58.9 us
    pallas_call x2, Pallas kernels, project(): pl.pallas_call(functools.partial(project_kernel, (nchunk, emasks, rank, g...  21.2 us
    pallas_call x2, Pallas kernels, pack(): pl.pallas_call(pack_kernel, out_shape=(jax.ShapeDtypeStruct((nb, blk, 2 *...  10.9 us
    pallas_call x2, Pallas kernels, potential(): pl.pallas_call(functools.partial(potential_kernel, sizes), out_shape=jax....  8.44 us
    pallas_call x1, Pallas kernels, gather(): pl.pallas_call(functools.partial(gather_kernel, group, nlist), out_shape=...  6.99 us
    pallas_call x1, Pallas kernels, pair_list(): pl.pallas_call(functools.partial(list_kernel, sizes), out_shape=jax.Shape...  4.83 us
  transfers between devices with their start and end apart: 47, of which 17 were waited for; matrix products, arithmetic and copies ran while one was open for 1% of the time, Pallas kernels for 19%

profile of v1, /device:TPU:1, one launch (start us, length us, event | category | flops | bytes accessed | tf_op | source)
XLA Modules:
  0.0 233.0 jit_solution(16141989717285876741)
XLA Ops:
  3.6 2.4 %occupied.2 = (f32[4,128,256]{2,1,0:T(8,128)S(1)}, bf16[4,128,256]{2,1,0:T(8,128)(2,1)S(1)}) custom-call(s32[4,12]{1,0:T(4,128)S(1)} %copy-done.10, s32[6]{0:T(128)S(1)} %stack.48.meta, bf16[3072,2,128]{2,1,0:T(2,128)(2,1)S(1)} %copy-done.5, bf16[4,128,1536]{2,1,0:T(8,128)(2,1)S(1)} %copy-done.1), custom_call_target="tpu_custom_call" | custom-call | tf_op jit(solution)/shard_map/occupied/pallas_call | solution.py:107
  8.2 6.0 %collective-permute-done.28 = bf16[4,128,256]{2,1,0:T(8,128)(2,1)S(1)} collective-permute-done((bf16[4,128,256]{2,1,0:T(8,128)(2,1)S(1)}, bf16[4,128,256]{2,1,0:T(8,128)(2,1)S(1)}, u32[]{:S(2)}, u32[]{:S(2)}) %collective-permute-start.28) | collective-permute-done | bytes 262176 | tf_op jit(solution)/shard_map/ppermute | solution.py:409
  15.0 2.2 collective-permute-start.29
  19.8 9.3 %collective-permute-done.29 = bf16[4,128,256]{2,1,0:T(8,128)(2,1)} collective-permute-done((bf16[4,128,256]{2,1,0:T(8,128)(2,1)}, bf16[4,128,256]{2,1,0:T(8,128)(2,1)}, u32[]{:S(2)}, u32[]{:S(2)}) %collective-permute-start.29) | collective-permute-done | bytes 262176 | tf_op jit(solution)/shard_map/ppermute | solution.py:409
  32.8 3.9 %pack.2 = bf16[12,128,256]{2,1,0:T(8,128)(2,1)} custom-call(s32[2]{0:T(128)S(1)} %pad_add_fusion.where, bf16[3072,16,2,128]{3,2,1,0:T(2,128)(2,1)} %trial.3), custom_call_target="tpu_custom_call" | custom-call | tf_op jit(solution)/shard_map/pack/pallas_call | solution.py:67
  37.1 3.5 %collective-permute-done = f32[1,4,5,128]{3,1,0,2:T(4,128)S(1)} collective-permute-done((f32[1,4,5,128]{3,1,0,2:T(4,128)S(1)}, f32[1,4,5,128]{3,1,0,2:T(4,128)S(1)}, u32[]{:S(2)}, u32[]{:S(2)}) %collective-permute-start) | collective-permute-done | bytes 10272 | tf_op jit(solution)/shard_map/ppermute | solution.py:409
  43.5 3.4 %collective-permute-start.3 = (f32[1,4,5,128]{3,1,0,2:T(4,128)S(1)}, f32[1,4,5,128]{3,1,0,2:T(4,128)S(1)}, u32[]{:S(2)}, u32[]{:S(2)}) collective-permute-start(f32[1,4,5,128]{3,1,0,2:T(4,128)S(1)} %maximum_bitcast_fusion), channel_id=1, source_target_pairs={{0,4},{4,0},{8,12},{12,8},{16,20},{20,16},{24,28},{28,24},{1,5},{5... | collective-permute-start | bytes 30728 | tf_op jit(solution)/shard_map/ppermute | solution.py:409
  60.3 7.0 %pack.3 = (bf16[12,128,256]{2,1,0:T(8,128)(2,1)S(1)}, bf16[12,128,256]{2,1,0:T(8,128)(2,1)S(1)}, bf16[12,128,256]{2,1,0:T(8,128)(2,1)}) custom-call(s32[4]{0:T(128)S(1)} %pad_add_fusion.1.where, bf16[3072,16,2,128]{3,2,1,0:T(2,128)(2,1)} %trial.3), custom_call_target="tpu_custom_call" | custom-call | tf_op jit(solution)/shard_map/pack/pallas_call | solution.py:67
  68.8 5.5 %collective-permute-done.14.refs_9_ = bf16[1,2,128,1536]{3,2,1,0:T(8,128)(2,1)} collective-permute-done((bf16[1,2,128,1536]{3,2,1,0:T(8,128)(2,1)S(1)}, bf16[1,2,128,1536]{3,2,1,0:T(8,128)(2,1)}, u32[]{:S(2)}, u32[]{:S(2)}) %collective-permute-start.14) | collective-permute-done | bytes 786464 | tf_op jit(solution)/shard_map/ppermute | solution.py:409
  81.9 48.0 %collective-permute-done.22.refs_1_ = bf16[12,128,256]{2,1,0:T(8,128)(2,1)S(1)} collective-permute-done((bf16[12,128,256]{2,1,0:T(8,128)(2,1)S(1)}, bf16[12,128,256]{2,1,0:T(8,128)(2,1)S(1)}, u32[]{:S(2)}, u32[]{:S(2)}) %collective-permute-start.22) | collective-permute-done | bytes 786464 | tf_op jit(solution)/shard_map/ppermute | solution.py:409
  132.7 4.2 %collective-permute-done.32.refs_15_ = bf16[1,4,128,256]{3,2,1,0:T(8,128)(2,1)S(1)} collective-permute-done((bf16[1,4,128,256]{3,2,1,0:T(8,128)(2,1)S(1)}, bf16[1,4,128,256]{3,2,1,0:T(8,128)(2,1)S(1)}, u32[]{:S(2)}, u32[]{:S(2)}) %collective-permute-start.32) | collective-permute-done | bytes 262176 | tf_op jit(solution)/shard_map/ppermute | solution.py:409
  140.4 3.9 %potential.2 = bf16[4,2,128,256]{3,2,1,0:T(8,128)(2,1)S(1)} custom-call(s32[8,4,12]{2,1,0:T(4,128)S(1)} %fusion.2.ids, s32[6]{0:T(128)S(1)} %stack.48.meta, bf16[12,128,256]{2,1,0:T(8,128)(2,1)} %collective-permute-done.21.refs_0_, bf16[12,128,256]{2,1,0:T(8,128)(2,1)S(1)} %collective-permute-done.22.refs_1_, ...), custom_call_target="tpu_custom_call" | custom-call | tf_op jit(solution)/shard_map/potential/pallas_call | solution.py:187
  144.3 10.1 %collective-permute-done.16.refs_11_ = bf16[1,2,128,1536]{3,2,1,0:T(8,128)(2,1)S(1)} collective-permute-done((bf16[1,2,128,1536]{3,2,1,0:T(8,128)(2,1)}, bf16[1,2,128,1536]{3,2,1,0:T(8,128)(2,1)S(1)}, u32[]{:S(2)}, u32[]{:S(2)}) %collective-permute-start.16) | collective-permute-done | bytes 786464 | tf_op jit(solution)/shard_map/ppermute | solution.py:409
  154.7 4.5 %potential.3 = bf16[4,2,128,256]{3,2,1,0:T(8,128)(2,1)S(1)} custom-call(s32[8,4,12]{2,1,0:T(4,128)S(1)} %fusion.2.ids, s32[6]{0:T(128)S(1)} %stack.48.meta, bf16[12,128,256]{2,1,0:T(8,128)(2,1)} %collective-permute-done.21.refs_0_, bf16[12,128,256]{2,1,0:T(8,128)(2,1)S(1)} %collective-permute-done.22.refs_1_, ...), custom_call_target="tpu_custom_call" | custom-call | tf_op jit(solution)/shard_map/potential/pallas_call | solution.py:187
  160.7 3.5 %collective-permute-start.40 = (bf16[1,4,2,128,256]{4,3,2,1,0:T(8,128)(2,1)S(1)}, bf16[1,4,2,128,256]{4,3,2,1,0:T(8,128)(2,1)S(1)}, u32[]{:S(2)}, u32[]{:S(2)}) collective-permute-start(bf16[1,4,2,128,256]{4,3,2,1,0:T(8,128)(2,1)S(1)} %bitcast.32), channel_id=1, source_target_pairs={{0,4},{4,0},{8,12},{12,8},{16,20},{20,16},{24,28},{28,24},{1,5},{5... | collective-permute-start | bytes 1572872 | tf_op jit(solution)/shard_map/ppermute | solution.py:409
  165.4 4.7 %collective-permute-start.44 = (bf16[1,4,2,128,256]{4,3,2,1,0:T(8,128)(2,1)S(1)}, bf16[1,4,2,128,256]{4,3,2,1,0:T(8,128)(2,1)S(1)}, u32[]{:S(2)}, u32[]{:S(2)}) collective-permute-start(bf16[1,4,2,128,256]{4,3,2,1,0:T(8,128)(2,1)S(1)} %bitcast.36), channel_id=1, source_target_pairs={{0,4},{4,0},{8,12},{12,8},{16,20},{20,16},{24,28},{28,24},{1,5},{5... | collective-permute-start | bytes 1572872 | tf_op jit(solution)/shard_map/ppermute | solution.py:409
  170.2 6.8 %collective-permute-start.13 = (bf16[1,2,128,1536]{3,2,1,0:T(8,128)(2,1)S(1)}, bf16[1,2,128,1536]{3,2,1,0:T(8,128)(2,1)S(1)}, u32[]{:S(2)}, u32[]{:S(2)}) collective-permute-start(bf16[1,2,128,1536]{3,2,1,0:T(8,128)(2,1)S(1)} %collective-permute-done.9.refs_3_.refs_11_), channel_id=1, source_target_pairs={{0,4},{4,0},{8,12},{12,8},{16,20},{20,16},{24,28},{28,24},{1,5},{5... | collective-permute-start | bytes 2359304 | tf_op jit(solution)/shard_map/ppermute | solution.py:409
  177.0 4.1 %collective-permute-done.39.refs_2_ = bf16[1,4,2,128,256]{4,3,2,1,0:T(8,128)(2,1)S(1)} collective-permute-done((bf16[1,4,2,128,256]{4,3,2,1,0:T(8,128)(2,1)S(1)}, bf16[1,4,2,128,256]{4,3,2,1,0:T(8,128)(2,1)S(1)}, u32[]{:S(2)}, u32[]{:S(2)}) %collective-permute-start.39) | collective-permute-done | bytes 524320 | tf_op jit(solution)/shard_map/ppermute | solution.py:409
  181.1 3.8 %collective-permute-start.20 = (bf16[1,2,128,1536]{3,2,1,0:T(8,128)(2,1)S(1)}, bf16[1,2,128,1536]{3,2,1,0:T(8,128)(2,1)S(1)}, u32[]{:S(2)}, u32[]{:S(2)}) collective-permute-start(bf16[1,2,128,1536]{3,2,1,0:T(8,128)(2,1)S(1)} %collective-permute-done.16.refs_11_), channel_id=1, source_target_pairs={{0,4},{4,0},{8,12},{12,8},{16,20},{20,16},{24,28},{28,24},{1,5},{5... | collective-permute-start | bytes 2359304 | tf_op jit(solution)/shard_map/ppermute | solution.py:409
  187.4 11.0 %collective-permute-done.34.refs_0_ = bf16[1,4,2,128,256]{4,3,2,1,0:T(8,128)(2,1)S(1)} collective-permute-done((bf16[1,4,2,128,256]{4,3,2,1,0:T(8,128)(2,1)S(1)}, bf16[1,4,2,128,256]{4,3,2,1,0:T(8,128)(2,1)S(1)}, u32[]{:S(2)}, u32[]{:S(2)}) %collective-permute-start.34) | collective-permute-done | bytes 524320 | tf_op jit(solution)/shard_map/ppermute | solution.py:409
  199.7 4.8 %pairs.1.facts = s32[8,432]{1,0:T(8,128)S(1)} custom-call(s32[8,4,12]{2,1,0:T(4,128)S(1)} %fusion.2.ids, s32[6]{0:T(128)S(1)} %stack.48.meta), custom_call_target="tpu_custom_call" | custom-call | tf_op jit(solution)/shard_map/pairs/pallas_call | solution.py:257
  204.5 7.0 %gather.1.columns = bf16[432,128,128]{2,1,0:T(8,128)(2,1)} custom-call(s32[8,432]{1,0:T(8,128)S(1)} %pairs.1.facts, bf16[1,2,128,1536]{3,2,1,0:T(8,128)(2,1)S(1)} %get-tuple-element.22.refs_0_.refs_8_, bf16[1,2,128,1536]{3,2,1,0:T(8,128)(2,1)S(1)} %collective-permute-done.7.refs_1_.refs_9_, ...), custom_call_target="tpu_custom_call" | custom-call | tf_op jit(solution)/shard_map/gather/pallas_call | solution.py:307
  211.6 13.5 %project.2.refs_4_ = f32[4,3072,128]{2,1,0:T(8,128)} custom-call(s32[8,432]{1,0:T(8,128)S(1)} %pairs.1.facts, s32[6]{0:T(128)S(1)} %stack.48.meta, bf16[432,128,128]{2,1,0:T(8,128)(2,1)} %gather.1.columns, bf16[1,4,2,128,256]{4,3,2,1,0:T(8,128)(2,1)S(1)} %bitcast.33, bf16[1,4,2,128,256]{4,3,2,1,0:T(8,128)(2,1)S(1)} %collective-permute-done.33.refs_1_, ...), custom_call_target="tpu_custom_call" | custom-call | tf_op jit(solution)/shard_map/project/pallas_call | solution.py:389
  225.1 7.7 %project.3 = f32[4,3072,128]{2,1,0:T(8,128)} custom-call(s32[8,432]{1,0:T(8,128)S(1)} %pairs.1.facts, s32[6]{0:T(128)S(1)} %stack.48.meta, bf16[432,128,128]{2,1,0:T(8,128)(2,1)S(1)} %copy-done, bf16[1,4,2,128,256]{4,3,2,1,0:T(8,128)(2,1)S(1)} %collective-permute-done.34.refs_0_, ...), custom_call_target="tpu_custom_call", output_to_operand_aliasing={{}: (7, {})} | custom-call | tf_op jit(solution)/shard_map/project/pallas_call | solution.py:389
  (132 shorter events, 51.7 us)
Async XLA Ops:
  17.3 41.1 %collective-permute-start.7 = (bf16[1,2,128,1536]{3,2,1,0:T(8,128)(2,1)S(1)}, bf16[1,2,128,1536]{3,2,1,0:T(8,128)(2,1)S(1)}, u32[]{:S(2)}, u32[]{:S(2)}) collective-permute-start(bf16[1,2,128,1536]{3,2,1,0:T(8,128)(2,1)S(1)} %get-tuple-element.22.refs_0_.refs_8_), channel_id=1, source_target_pairs={{0,8},{4,12},{8,0},{12,4},{16,24},{20,28},{24,16},{28,20},{1,9},{5... | collective-permute-start | bytes 2359304 | tf_op jit(solution)/shard_map/ppermute | solution.py:409
  18.6 40.5 %collective-permute-start.8 = (bf16[1,2,128,1536]{3,2,1,0:T(8,128)(2,1)S(1)}, bf16[1,2,128,1536]{3,2,1,0:T(8,128)(2,1)S(1)}, u32[]{:S(2)}, u32[]{:S(2)}) collective-permute-start(bf16[1,2,128,1536]{3,2,1,0:T(8,128)(2,1)S(1)} %get-tuple-element.22.refs_0_.refs_8_), channel_id=1, source_target_pairs={{0,16},{4,20},{8,24},{12,28},{16,0},{20,4},{24,8},{28,12},{1,17},{... | collective-permute-start | bytes 2359304 | tf_op jit(solution)/shard_map/ppermute | solution.py:409
  30.5 24.8 %collective-permute-start.30 = (bf16[1,4,128,256]{3,2,1,0:T(8,128)(2,1)S(1)}, bf16[1,4,128,256]{3,2,1,0:T(8,128)(2,1)S(1)}, u32[]{:S(2)}, u32[]{:S(2)}) collective-permute-start(bf16[1,4,128,256]{3,2,1,0:T(8,128)(2,1)S(1)} %fusion.1.refs_12_), channel_id=1, source_target_pairs={{0,8},{4,12},{8,0},{12,4},{16,24},{20,28},{24,16},{28,20},{1,9},{5... | collective-permute-start | bytes 786440 | tf_op jit(solution)/shard_map/ppermute | solution.py:409
  31.5 24.9 %collective-permute-start.31 = (bf16[1,4,128,256]{3,2,1,0:T(8,128)(2,1)S(1)}, bf16[1,4,128,256]{3,2,1,0:T(8,128)(2,1)S(1)}, u32[]{:S(2)}, u32[]{:S(2)}) collective-permute-start(bf16[1,4,128,256]{3,2,1,0:T(8,128)(2,1)S(1)} %fusion.1.refs_12_), channel_id=1, source_target_pairs={{0,16},{4,20},{8,24},{12,28},{16,0},{20,4},{24,8},{28,12},{1,17},{... | collective-permute-start | bytes 786440 | tf_op jit(solution)/shard_map/ppermute | solution.py:409
  55.2 19.0 %collective-permute-start.14 = (bf16[1,2,128,1536]{3,2,1,0:T(8,128)(2,1)S(1)}, bf16[1,2,128,1536]{3,2,1,0:T(8,128)(2,1)}, u32[]{:S(2)}, u32[]{:S(2)}) collective-permute-start(bf16[1,2,128,1536]{3,2,1,0:T(8,128)(2,1)S(1)} %get-tuple-element.21.refs_8_), channel_id=1, source_target_pairs={{0,16},{4,20},{8,24},{12,28},{16,0},{20,4},{24,8},{28,12},{1,17},{... | collective-permute-start | bytes 2359304 | tf_op jit(solution)/shard_map/ppermute | solution.py:409
  58.4 18.9 %collective-permute-start.17 = (bf16[1,2,128,1536]{3,2,1,0:T(8,128)(2,1)S(1)}, bf16[1,2,128,1536]{3,2,1,0:T(8,128)(2,1)}, u32[]{:S(2)}, u32[]{:S(2)}) collective-permute-start(bf16[1,2,128,1536]{3,2,1,0:T(8,128)(2,1)S(1)} %get-tuple-element.21.refs_8_), channel_id=1, source_target_pairs={{0,4},{4,0},{8,12},{12,8},{16,20},{20,16},{24,28},{28,24},{1,5},{5... | collective-permute-start | bytes 2359304 | tf_op jit(solution)/shard_map/ppermute | solution.py:409
  59.1 21.2 %collective-permute-start.21 = (bf16[12,128,256]{2,1,0:T(8,128)(2,1)}, bf16[12,128,256]{2,1,0:T(8,128)(2,1)}, u32[]{:S(2)}, u32[]{:S(2)}) collective-permute-start(bf16[12,128,256]{2,1,0:T(8,128)(2,1)} %pack.2), channel_id=1, source_target_pairs={{0,3},{1,2},{2,1},{3,0},{4,7},{5,6},{6,5},{7,4},{8,11},{9,10},{10,... | collective-permute-start | bytes 2359304 | tf_op jit(solution)/shard_map/ppermute | solution.py:409
  67.4 62.6 %collective-permute-start.22 = (bf16[12,128,256]{2,1,0:T(8,128)(2,1)S(1)}, bf16[12,128,256]{2,1,0:T(8,128)(2,1)S(1)}, u32[]{:S(2)}, u32[]{:S(2)}) collective-permute-start(bf16[12,128,256]{2,1,0:T(8,128)(2,1)S(1)} %get-tuple-element.16), channel_id=1, source_target_pairs={{0,2},{1,3},{2,0},{3,1},{4,6},{5,7},{6,4},{7,5},{8,10},{9,11},{10,... | collective-permute-start | bytes 2359304 | tf_op jit(solution)/shard_map/ppermute | solution.py:409
  74.3 55.9 %collective-permute-start.23 = (bf16[12,128,256]{2,1,0:T(8,128)(2,1)S(1)}, bf16[12,128,256]{2,1,0:T(8,128)(2,1)S(1)}, u32[]{:S(2)}, u32[]{:S(2)}) collective-permute-start(bf16[12,128,256]{2,1,0:T(8,128)(2,1)S(1)} %get-tuple-element.17), channel_id=1, source_target_pairs={{0,1},{1,0},{2,3},{3,2},{4,5},{5,4},{6,7},{7,6},{8,9},{9,8},{10,11... | collective-permute-start | bytes 2359304 | tf_op jit(solution)/shard_map/ppermute | solution.py:409
  76.0 55.4 %collective-permute-start.27 = (bf16[12,128,256]{2,1,0:T(8,128)(2,1)}, bf16[12,128,256]{2,1,0:T(8,128)(2,1)S(1)}, u32[]{:S(2)}, u32[]{:S(2)}) collective-permute-start(bf16[12,128,256]{2,1,0:T(8,128)(2,1)} %get-tuple-element.18.refs_3_), channel_id=1, source_target_pairs={{0,4},{4,0},{8,12},{12,8},{16,20},{20,16},{24,28},{28,24},{1,5},{5... | collective-permute-start | bytes 2359304 | tf_op jit(solution)/shard_map/ppermute | solution.py:409
  77.3 60.2 %collective-permute-start.9 = (bf16[1,2,128,1536]{3,2,1,0:T(8,128)(2,1)S(1)}, bf16[1,2,128,1536]{3,2,1,0:T(8,128)(2,1)S(1)}, u32[]{:S(2)}, u32[]{:S(2)}) collective-permute-start(bf16[1,2,128,1536]{3,2,1,0:T(8,128)(2,1)S(1)} %collective-permute-done.7.refs_1_.refs_9_), channel_id=1, source_target_pairs={{0,16},{4,20},{8,24},{12,28},{16,0},{20,4},{24,8},{28,12},{1,17},{... | collective-permute-start | bytes 2359304 | tf_op jit(solution)/shard_map/ppermute | solution.py:409
  80.4 59.3 %collective-permute-start.24 = (bf16[12,128,256]{2,1,0:T(8,128)(2,1)}, bf16[12,128,256]{2,1,0:T(8,128)(2,1)S(1)}, u32[]{:S(2)}, u32[]{:S(2)}) collective-permute-start(bf16[12,128,256]{2,1,0:T(8,128)(2,1)} %collective-permute-done.21.refs_0_), channel_id=1, source_target_pairs={{0,4},{4,0},{8,12},{12,8},{16,20},{20,16},{24,28},{28,24},{1,5},{5... | collective-permute-start | bytes 2359304 | tf_op jit(solution)/shard_map/ppermute | solution.py:409
  137.5 21.7 %collective-permute-start.11 = (bf16[1,2,128,1536]{3,2,1,0:T(8,128)(2,1)S(1)}, bf16[1,2,128,1536]{3,2,1,0:T(8,128)(2,1)S(1)}, u32[]{:S(2)}, u32[]{:S(2)}) collective-permute-start(bf16[1,2,128,1536]{3,2,1,0:T(8,128)(2,1)S(1)} %collective-permute-done.7.refs_1_.refs_9_), channel_id=1, source_target_pairs={{0,4},{4,0},{8,12},{12,8},{16,20},{20,16},{24,28},{28,24},{1,5},{5... | collective-permute-start | bytes 2359304 | tf_op jit(solution)/shard_map/ppermute | solution.py:409
  139.6 19.9 %collective-permute-start.12 = (bf16[1,2,128,1536]{3,2,1,0:T(8,128)(2,1)S(1)}, bf16[1,2,128,1536]{3,2,1,0:T(8,128)(2,1)S(1)}, u32[]{:S(2)}, u32[]{:S(2)}) collective-permute-start(bf16[1,2,128,1536]{3,2,1,0:T(8,128)(2,1)S(1)} %collective-permute-done.8.refs_2_.refs_10_), channel_id=1, source_target_pairs={{0,4},{4,0},{8,12},{12,8},{16,20},{20,16},{24,28},{28,24},{1,5},{5... | collective-permute-start | bytes 2359304 | tf_op jit(solution)/shard_map/ppermute | solution.py:409
  139.7 21.0 %collective-permute-start.18 = (bf16[1,2,128,1536]{3,2,1,0:T(8,128)(2,1)}, bf16[1,2,128,1536]{3,2,1,0:T(8,128)(2,1)S(1)}, u32[]{:S(2)}, u32[]{:S(2)}) collective-permute-start(bf16[1,2,128,1536]{3,2,1,0:T(8,128)(2,1)} %collective-permute-done.14.refs_9_), channel_id=1, source_target_pairs={{0,4},{4,0},{8,12},{12,8},{16,20},{20,16},{24,28},{28,24},{1,5},{5... | collective-permute-start | bytes 2359304 | tf_op jit(solution)/shard_map/ppermute | solution.py:409
  140.2 24.0 %collective-permute-start.19 = (bf16[1,2,128,1536]{3,2,1,0:T(8,128)(2,1)}, bf16[1,2,128,1536]{3,2,1,0:T(8,128)(2,1)S(1)}, u32[]{:S(2)}, u32[]{:S(2)}) collective-permute-start(bf16[1,2,128,1536]{3,2,1,0:T(8,128)(2,1)} %collective-permute-done.15.refs_10_), channel_id=1, source_target_pairs={{0,4},{4,0},{8,12},{12,8},{16,20},{20,16},{24,28},{28,24},{1,5},{5... | collective-permute-start | bytes 2359304 | tf_op jit(solution)/shard_map/ppermute | solution.py:409
  159.5 21.6 %collective-permute-start.39 = (bf16[1,4,2,128,256]{4,3,2,1,0:T(8,128)(2,1)S(1)}, bf16[1,4,2,128,256]{4,3,2,1,0:T(8,128)(2,1)S(1)}, u32[]{:S(2)}, u32[]{:S(2)}) collective-permute-start(bf16[1,4,2,128,256]{4,3,2,1,0:T(8,128)(2,1)S(1)} %bitcast.31), channel_id=1, source_target_pairs={{0,16},{4,20},{8,24},{12,28},{16,0},{20,4},{24,8},{28,12},{1,17},{... | collective-permute-start | bytes 1572872 | tf_op jit(solution)/shard_map/ppermute | solution.py:409
  160.7 24.1 %collective-permute-start.40 = (bf16[1,4,2,128,256]{4,3,2,1,0:T(8,128)(2,1)S(1)}, bf16[1,4,2,128,256]{4,3,2,1,0:T(8,128)(2,1)S(1)}, u32[]{:S(2)}, u32[]{:S(2)}) collective-permute-start(bf16[1,4,2,128,256]{4,3,2,1,0:T(8,128)(2,1)S(1)} %bitcast.32), channel_id=1, source_target_pairs={{0,4},{4,0},{8,12},{12,8},{16,20},{20,16},{24,28},{28,24},{1,5},{5... | collective-permute-start | bytes 1572872 | tf_op jit(solution)/shard_map/ppermute | solution.py:409
  164.2 20.9 %collective-permute-start.43 = (bf16[1,4,2,128,256]{4,3,2,1,0:T(8,128)(2,1)S(1)}, bf16[1,4,2,128,256]{4,3,2,1,0:T(8,128)(2,1)S(1)}, u32[]{:S(2)}, u32[]{:S(2)}) collective-permute-start(bf16[1,4,2,128,256]{4,3,2,1,0:T(8,128)(2,1)S(1)} %bitcast.35), channel_id=1, source_target_pairs={{0,8},{4,12},{8,0},{12,4},{16,24},{20,28},{24,16},{28,20},{1,9},{5... | collective-permute-start | bytes 1572872 | tf_op jit(solution)/shard_map/ppermute | solution.py:409
  165.4 20.9 %collective-permute-start.44 = (bf16[1,4,2,128,256]{4,3,2,1,0:T(8,128)(2,1)S(1)}, bf16[1,4,2,128,256]{4,3,2,1,0:T(8,128)(2,1)S(1)}, u32[]{:S(2)}, u32[]{:S(2)}) collective-permute-start(bf16[1,4,2,128,256]{4,3,2,1,0:T(8,128)(2,1)S(1)} %bitcast.36), channel_id=1, source_target_pairs={{0,4},{4,0},{8,12},{12,8},{16,20},{20,16},{24,28},{28,24},{1,5},{5... | collective-permute-start | bytes 1572872 | tf_op jit(solution)/shard_map/ppermute | solution.py:409
  186.8 24.7 %collective-permute-start.45 = (bf16[1,4,2,128,256]{4,3,2,1,0:T(8,128)(2,1)S(1)}, bf16[1,4,2,128,256]{4,3,2,1,0:T(8,128)(2,1)S(1)}, u32[]{:S(2)}, u32[]{:S(2)}) collective-permute-start(bf16[1,4,2,128,256]{4,3,2,1,0:T(8,128)(2,1)S(1)} %collective-permute-done.36.refs_7_), channel_id=1, source_target_pairs={{0,4},{4,0},{8,12},{12,8},{16,20},{20,16},{24,28},{28,24},{1,5},{5... | collective-permute-start | bytes 1572872 | tf_op jit(solution)/shard_map/ppermute | solution.py:409
  186.9 24.6 %collective-permute-start.42 = (bf16[1,4,2,128,256]{4,3,2,1,0:T(8,128)(2,1)S(1)}, bf16[1,4,2,128,256]{4,3,2,1,0:T(8,128)(2,1)S(1)}, u32[]{:S(2)}, u32[]{:S(2)}) collective-permute-start(bf16[1,4,2,128,256]{4,3,2,1,0:T(8,128)(2,1)S(1)} %collective-permute-done.39.refs_2_), channel_id=1, source_target_pairs={{0,4},{4,0},{8,12},{12,8},{16,20},{20,16},{24,28},{28,24},{1,5},{5... | collective-permute-start | bytes 1572872 | tf_op jit(solution)/shard_map/ppermute | solution.py:409
  199.2 25.9 %collective-permute-start.35 = (bf16[1,4,2,128,256]{4,3,2,1,0:T(8,128)(2,1)S(1)}, bf16[1,4,2,128,256]{4,3,2,1,0:T(8,128)(2,1)S(1)}, u32[]{:S(2)}, u32[]{:S(2)}) collective-permute-start(bf16[1,4,2,128,256]{4,3,2,1,0:T(8,128)(2,1)S(1)} %collective-permute-done.34.refs_0_), channel_id=1, source_target_pairs={{0,4},{4,0},{8,12},{12,8},{16,20},{20,16},{24,28},{28,24},{1,5},{5... | collective-permute-start | bytes 1572872 | tf_op jit(solution)/shard_map/ppermute | solution.py:409
  199.4 25.7 %collective-permute-start.38 = (bf16[1,4,2,128,256]{4,3,2,1,0:T(8,128)(2,1)S(1)}, bf16[1,4,2,128,256]{4,3,2,1,0:T(8,128)(2,1)S(1)}, u32[]{:S(2)}, u32[]{:S(2)}) collective-permute-start(bf16[1,4,2,128,256]{4,3,2,1,0:T(8,128)(2,1)S(1)} %collective-permute-done.37.refs_2_), channel_id=1, source_target_pairs={{0,4},{4,0},{8,12},{12,8},{16,20},{20,16},{24,28},{28,24},{1,5},{5... | collective-permute-start | bytes 1572872 | tf_op jit(solution)/shard_map/ppermute | solution.py:409
  (38 other events, 497.9 us)

commit v2 on v1

--- a/solution.py
+++ b/solution.py
@@ -93,17 +93,24 @@
 
     for b in range(batches):
         total = jnp.zeros(keep.shape[1:], F32)
+        half, inner = divmod(b, keep.shape[0])
         for s in range(0, sig, 2):
             two = jnp.concatenate([block(b, s), block(b, s + 1)], axis=0)
             total += jnp.dot(values[b, :, s * blk : (s + 2) * blk], two, preferred_element_type=F32)
-        keep[b] = total
-        send[b] = total.astype(BF16)
+
+        @pl.when(meta[1] == half)
+        def _(total=total, inner=inner):
+            keep[inner] = total
+
+        @pl.when(meta[1] != half)
+        def _(total=total, inner=inner):
+            send[inner] = total.astype(BF16)
 
 
 def occupied_part(occupied, colloc, blocks, meta, blk):
     batches, npts, _ = colloc.shape
     nocc = occupied.shape[2]
-    shape = (batches, npts, 2 * nocc)
+    shape = (batches // 2, npts, 2 * nocc)
     return pl.pallas_call(
         occupied_kernel,
         out_shape=(jax.ShapeDtypeStruct(shape, F32), jax.ShapeDtypeStruct(shape, BF16)),
@@ -144,7 +151,7 @@
 
     def turn_of(mask, b):
         piece, row = where[mask]
-        og = occ[piece][row, b]
+        og = occ[piece][row, meta[1] ^ (b // count), b % count]
         half = width // 2
         return jnp.concatenate([og, jnp.concatenate([-og[:, half:], og[:, :half]], axis=1)], axis=0)
 
@@ -438,7 +445,7 @@
     count = batches // 2
     ao, grid = lax.axis_index("ao"), lax.axis_index("grid")
     vector, side = grid // rank, grid % parts
-    meta = jnp.stack([ao * nlocal, ao * 0, grid * nown, ao, side, vector]).astype(jnp.int32)
+    meta = jnp.stack([ao * nlocal, ao & 1, grid * nown, ao, side, vector]).astype(jnp.int32)
     high_bits = [rank << b for b in range(nv.bit_length() - 1)]
     low_bits = [1 << b for b in range(rank.bit_length() - 1)]
     part_bits = [1 << b for b in range(parts.bit_length() - 1)]
@@ -464,7 +471,8 @@
         got = swap(send, "ao", 1 << s)
         held = held + got.astype(F32)
         send = held.astype(BF16)
-        whole = send[None]
+    other = swap(send, "ao", 1)
+    whole = jnp.stack([send, other])[None]
     occ = across(whole, high_bits)
 
     numbers = jnp.pad(blocks.astype(F32), ((0, 0), (0, npts - sig)))

time: 233 us -> 243 us (1.043)
  waiting for transfers between devices: 110 us -> 118 us
  local copies, waits for them, and re-layouts: 4.51 us -> 8.21 us
    ppermute x47 -> x48, waiting for transfers between devices: 110 us -> 118 us  [swap(): return lax.ppermute(array, axis, [(i, i ^ bit) for i in range(size)])]
    unnamed x36 -> x40, local copies, waits for them, and re-layouts: 4.3 us -> 7.99 us
    ppermute x47 -> x48, starting transfers between devices: 58.9 us -> 56.7 us  [swap(): return lax.ppermute(array, axis, [(i, i ^ bit) for i in range(size)])]
  transfers between devices with their start and end apart: 47 -> 48, of which waited for: 17 -> 19; matrix products, arithmetic and copies ran while one was open for 1% -> 1% of each run, Pallas kernels for 19% -> 18%
where the time goes in v2:
time: 243 us; the launch traced here: 242 us
  waiting for transfers between devices  118 us (49%)
  starting transfers between devices  56.7 us (23%)
  Pallas kernels  55.6 us (23%)
  local copies, waits for them, and re-layouts  8.21 us (3%)
  other arithmetic  2.74 us (1%)
    ppermute x48, waiting for transfers between devices, swap(): return lax.ppermute(array, axis, [(i, i ^ bit) for i in range(size)])  118 us
    ppermute x48, starting transfers between devices, swap(): return lax.ppermute(array, axis, [(i, i ^ bit) for i in range(size)])  56.7 us
    pallas_call x2, Pallas kernels, project(): pl.pallas_call(functools.partial(project_kernel, (nchunk, emasks, rank, g...  21.1 us
    pallas_call x2, Pallas kernels, pack(): pl.pallas_call(pack_kernel, out_shape=(jax.ShapeDtypeStruct((nb, blk, 2 *...  10.9 us
    pallas_call x2, Pallas kernels, potential(): pl.pallas_call(functools.partial(potential_kernel, sizes), out_shape=jax....  8.46 us
    unnamed x40, local copies, waits for them, and re-layouts  7.99 us
    pallas_call x1, Pallas kernels, gather(): pl.pallas_call(functools.partial(gather_kernel, group, nlist), out_shape=...  7 us
  transfers between devices with their start and end apart: 48, of which 19 were waited for; matrix products, arithmetic and copies ran while one was open for 1% of the time, Pallas kernels for 18%

profile of v2, /device:TPU:1, one launch (start us, length us, event | category | flops | bytes accessed | tf_op | source)
XLA Modules:
  0.0 242.2 jit_solution(5931253200732106059)
XLA Ops:
  3.6 3.3 %occupied.2 = (f32[2,128,256]{2,1,0:T(8,128)S(1)}, bf16[2,128,256]{2,1,0:T(8,128)(2,1)S(1)}) custom-call(s32[4,12]{1,0:T(4,128)S(1)} %copy-done.13, s32[6]{0:T(128)S(1)} %stack.61.meta, bf16[3072,2,128]{2,1,0:T(2,128)(2,1)S(1)} %copy-done.4, bf16[4,128,1536]{2,1,0:T(8,128)(2,1)S(1)} %copy-done.1), custom_call_target="tpu_custom_call" | custom-call | tf_op jit(solution)/shard_map/occupied/pallas_call | solution.py:114
  9.0 3.2 %collective-permute-done.28 = bf16[2,128,256]{2,1,0:T(8,128)(2,1)S(1)} collective-permute-done((bf16[2,128,256]{2,1,0:T(8,128)(2,1)S(1)}, bf16[2,128,256]{2,1,0:T(8,128)(2,1)S(1)}, u32[]{:S(2)}, u32[]{:S(2)}) %collective-permute-start.28) | collective-permute-done | bytes 131104 | tf_op jit(solution)/shard_map/ppermute | solution.py:416
  14.5 6.0 %collective-permute-done.29 = bf16[2,128,256]{2,1,0:T(8,128)(2,1)S(1)} collective-permute-done((bf16[2,128,256]{2,1,0:T(8,128)(2,1)S(1)}, bf16[2,128,256]{2,1,0:T(8,128)(2,1)S(1)}, u32[]{:S(2)}, u32[]{:S(2)}) %collective-permute-start.29) | collective-permute-done | bytes 131104 | tf_op jit(solution)/shard_map/ppermute | solution.py:416
  27.3 3.9 %pack.2 = bf16[12,128,256]{2,1,0:T(8,128)(2,1)} custom-call(s32[2]{0:T(128)S(1)} %pad_add_fusion.where, bf16[3072,16,2,128]{3,2,1,0:T(2,128)(2,1)} %trial.3), custom_call_target="tpu_custom_call" | custom-call | tf_op jit(solution)/shard_map/pack/pallas_call | solution.py:67
  31.5 13.5 %collective-permute-done = f32[1,4,5,128]{3,1,0,2:T(4,128)S(1)} collective-permute-done((f32[1,4,5,128]{3,1,0,2:T(4,128)S(1)}, f32[1,4,5,128]{3,1,0,2:T(4,128)S(1)}, u32[]{:S(2)}, u32[]{:S(2)}) %collective-permute-start) | collective-permute-done | bytes 10272 | tf_op jit(solution)/shard_map/ppermute | solution.py:416
  47.9 3.0 %collective-permute-start.3 = (f32[1,4,5,128]{3,1,0,2:T(4,128)S(1)}, f32[1,4,5,128]{3,1,0,2:T(4,128)S(1)}, u32[]{:S(2)}, u32[]{:S(2)}) collective-permute-start(f32[1,4,5,128]{3,1,0,2:T(4,128)S(1)} %maximum_bitcast_fusion.1), channel_id=1, source_target_pairs={{0,4},{4,0},{8,12},{12,8},{16,20},{20,16},{24,28},{28,24},{1,5},{5... | collective-permute-start | bytes 30728 | tf_op jit(solution)/shard_map/ppermute | solution.py:416
  63.2 2.8 %collective-permute-start.21 = (bf16[12,128,256]{2,1,0:T(8,128)(2,1)}, bf16[12,128,256]{2,1,0:T(8,128)(2,1)}, u32[]{:S(2)}, u32[]{:S(2)}) collective-permute-start(bf16[12,128,256]{2,1,0:T(8,128)(2,1)} %pack.2), channel_id=1, source_target_pairs={{0,3},{1,2},{2,1},{3,0},{4,7},{5,6},{6,5},{7,4},{8,11},{9,10},{10,... | collective-permute-start | bytes 2359304 | tf_op jit(solution)/shard_map/ppermute | solution.py:416
  66.1 7.0 %pack.3 = (bf16[12,128,256]{2,1,0:T(8,128)(2,1)S(1)}, bf16[12,128,256]{2,1,0:T(8,128)(2,1)S(1)}, bf16[12,128,256]{2,1,0:T(8,128)(2,1)}) custom-call(s32[4]{0:T(128)S(1)} %pad_add_fusion.1.where, bf16[3072,16,2,128]{3,2,1,0:T(2,128)(2,1)} %trial.3), custom_call_target="tpu_custom_call" | custom-call | tf_op jit(solution)/shard_map/pack/pallas_call | solution.py:67
  73.5 4.8 %collective-permute-done.14.refs_9_ = bf16[1,2,128,1536]{3,2,1,0:T(8,128)(2,1)} collective-permute-done((bf16[1,2,128,1536]{3,2,1,0:T(8,128)(2,1)S(1)}, bf16[1,2,128,1536]{3,2,1,0:T(8,128)(2,1)}, u32[]{:S(2)}, u32[]{:S(2)}) %collective-permute-start.14) | collective-permute-done | bytes 786464 | tf_op jit(solution)/shard_map/ppermute | solution.py:416
  86.0 48.9 %collective-permute-done.22.refs_1_ = bf16[12,128,256]{2,1,0:T(8,128)(2,1)S(1)} collective-permute-done((bf16[12,128,256]{2,1,0:T(8,128)(2,1)S(1)}, bf16[12,128,256]{2,1,0:T(8,128)(2,1)S(1)}, u32[]{:S(2)}, u32[]{:S(2)}) %collective-permute-start.22) | collective-permute-done | bytes 786464 | tf_op jit(solution)/shard_map/ppermute | solution.py:416
  137.4 4.7 %collective-permute-done.33.refs_15_ = bf16[1,2,2,128,256]{4,3,2,1,0:T(8,128)(2,1)S(1)} collective-permute-done((bf16[1,2,2,128,256]{4,3,2,1,0:T(8,128)(2,1)S(1)}, bf16[1,2,2,128,256]{4,3,2,1,0:T(8,128)(2,1)S(1)}, u32[]{:S(2)}, u32[]{:S(2)}) %collective-permute-start.33) | collective-permute-done | bytes 262176 | tf_op jit(solution)/shard_map/ppermute | solution.py:416
  145.3 4.0 %potential.2 = bf16[4,2,128,256]{3,2,1,0:T(8,128)(2,1)S(1)} custom-call(s32[8,4,12]{2,1,0:T(4,128)S(1)} %fusion.1.ids, s32[6]{0:T(128)S(1)} %stack.61.meta, bf16[12,128,256]{2,1,0:T(8,128)(2,1)} %collective-permute-done.21.refs_0_, bf16[12,128,256]{2,1,0:T(8,128)(2,1)S(1)} %collective-permute-done.22.refs_1_, ...), custom_call_target="tpu_custom_call" | custom-call | tf_op jit(solution)/shard_map/potential/pallas_call | solution.py:194
  149.3 10.7 %collective-permute-done.16.refs_11_ = bf16[1,2,128,1536]{3,2,1,0:T(8,128)(2,1)S(1)} collective-permute-done((bf16[1,2,128,1536]{3,2,1,0:T(8,128)(2,1)}, bf16[1,2,128,1536]{3,2,1,0:T(8,128)(2,1)S(1)}, u32[]{:S(2)}, u32[]{:S(2)}) %collective-permute-start.16) | collective-permute-done | bytes 786464 | tf_op jit(solution)/shard_map/ppermute | solution.py:416
  160.2 4.5 %potential.3 = bf16[4,2,128,256]{3,2,1,0:T(8,128)(2,1)S(1)} custom-call(s32[8,4,12]{2,1,0:T(4,128)S(1)} %fusion.1.ids, s32[6]{0:T(128)S(1)} %stack.61.meta, bf16[12,128,256]{2,1,0:T(8,128)(2,1)} %collective-permute-done.21.refs_0_, bf16[12,128,256]{2,1,0:T(8,128)(2,1)S(1)} %collective-permute-done.22.refs_1_, ...), custom_call_target="tpu_custom_call" | custom-call | tf_op jit(solution)/shard_map/potential/pallas_call | solution.py:194
  166.3 3.2 %collective-permute-start.41 = (bf16[1,4,2,128,256]{4,3,2,1,0:T(8,128)(2,1)S(1)}, bf16[1,4,2,128,256]{4,3,2,1,0:T(8,128)(2,1)S(1)}, u32[]{:S(2)}, u32[]{:S(2)}) collective-permute-start(bf16[1,4,2,128,256]{4,3,2,1,0:T(8,128)(2,1)S(1)} %bitcast.35), channel_id=1, source_target_pairs={{0,4},{4,0},{8,12},{12,8},{16,20},{20,16},{24,28},{28,24},{1,5},{5... | collective-permute-start | bytes 1572872 | tf_op jit(solution)/shard_map/ppermute | solution.py:416
  171.1 4.9 %collective-permute-start.45 = (bf16[1,4,2,128,256]{4,3,2,1,0:T(8,128)(2,1)S(1)}, bf16[1,4,2,128,256]{4,3,2,1,0:T(8,128)(2,1)S(1)}, u32[]{:S(2)}, u32[]{:S(2)}) collective-permute-start(bf16[1,4,2,128,256]{4,3,2,1,0:T(8,128)(2,1)S(1)} %bitcast.39), channel_id=1, source_target_pairs={{0,4},{4,0},{8,12},{12,8},{16,20},{20,16},{24,28},{28,24},{1,5},{5... | collective-permute-start | bytes 1572872 | tf_op jit(solution)/shard_map/ppermute | solution.py:416
  176.0 6.3 %collective-permute-start.13 = (bf16[1,2,128,1536]{3,2,1,0:T(8,128)(2,1)S(1)}, bf16[1,2,128,1536]{3,2,1,0:T(8,128)(2,1)S(1)}, u32[]{:S(2)}, u32[]{:S(2)}) collective-permute-start(bf16[1,2,128,1536]{3,2,1,0:T(8,128)(2,1)S(1)} %collective-permute-done.9.refs_3_.refs_11_), channel_id=1, source_target_pairs={{0,4},{4,0},{8,12},{12,8},{16,20},{20,16},{24,28},{28,24},{1,5},{5... | collective-permute-start | bytes 2359304 | tf_op jit(solution)/shard_map/ppermute | solution.py:416
  182.3 4.6 %collective-permute-done.40.refs_2_ = bf16[1,4,2,128,256]{4,3,2,1,0:T(8,128)(2,1)S(1)} collective-permute-done((bf16[1,4,2,128,256]{4,3,2,1,0:T(8,128)(2,1)S(1)}, bf16[1,4,2,128,256]{4,3,2,1,0:T(8,128)(2,1)S(1)}, u32[]{:S(2)}, u32[]{:S(2)}) %collective-permute-start.40) | collective-permute-done | bytes 524320 | tf_op jit(solution)/shard_map/ppermute | solution.py:416
  186.9 3.5 %collective-permute-start.20 = (bf16[1,2,128,1536]{3,2,1,0:T(8,128)(2,1)S(1)}, bf16[1,2,128,1536]{3,2,1,0:T(8,128)(2,1)S(1)}, u32[]{:S(2)}, u32[]{:S(2)}) collective-permute-start(bf16[1,2,128,1536]{3,2,1,0:T(8,128)(2,1)S(1)} %collective-permute-done.16.refs_11_), channel_id=1, source_target_pairs={{0,4},{4,0},{8,12},{12,8},{16,20},{20,16},{24,28},{28,24},{1,5},{5... | collective-permute-start | bytes 2359304 | tf_op jit(solution)/shard_map/ppermute | solution.py:416
  192.9 10.9 %collective-permute-done.35.refs_0_ = bf16[1,4,2,128,256]{4,3,2,1,0:T(8,128)(2,1)S(1)} collective-permute-done((bf16[1,4,2,128,256]{4,3,2,1,0:T(8,128)(2,1)S(1)}, bf16[1,4,2,128,256]{4,3,2,1,0:T(8,128)(2,1)S(1)}, u32[]{:S(2)}, u32[]{:S(2)}) %collective-permute-start.35) | collective-permute-done | bytes 524320 | tf_op jit(solution)/shard_map/ppermute | solution.py:416
  205.3 4.8 %pairs.1.facts = s32[8,432]{1,0:T(8,128)S(1)} custom-call(s32[8,4,12]{2,1,0:T(4,128)S(1)} %fusion.1.ids, s32[6]{0:T(128)S(1)} %stack.61.meta), custom_call_target="tpu_custom_call" | custom-call | tf_op jit(solution)/shard_map/pairs/pallas_call | solution.py:264
  210.1 7.0 %gather.1.columns = bf16[432,128,128]{2,1,0:T(8,128)(2,1)} custom-call(s32[8,432]{1,0:T(8,128)S(1)} %pairs.1.facts, bf16[1,2,128,1536]{3,2,1,0:T(8,128)(2,1)S(1)} %get-tuple-element.22.refs_0_.refs_8_, bf16[1,2,128,1536]{3,2,1,0:T(8,128)(2,1)S(1)} %collective-permute-done.7.refs_1_.refs_9_, ...), custom_call_target="tpu_custom_call" | custom-call | tf_op jit(solution)/shard_map/gather/pallas_call | solution.py:314
  220.8 13.4 %project.2.refs_4_ = f32[4,3072,128]{2,1,0:T(8,128)} custom-call(s32[8,432]{1,0:T(8,128)S(1)} %pairs.1.facts, s32[6]{0:T(128)S(1)} %stack.61.meta, bf16[432,128,128]{2,1,0:T(8,128)(2,1)} %gather.1.columns, bf16[1,4,2,128,256]{4,3,2,1,0:T(8,128)(2,1)S(1)} %bitcast.36, bf16[1,4,2,128,256]{4,3,2,1,0:T(8,128)(2,1)S(1)} %collective-permute-done.34.refs_1_, ...), custom_call_target="tpu_custom_call" | custom-call | tf_op jit(solution)/shard_map/project/pallas_call | solution.py:396
  234.3 7.7 %project.3 = f32[4,3072,128]{2,1,0:T(8,128)} custom-call(s32[8,432]{1,0:T(8,128)S(1)} %pairs.1.facts, s32[6]{0:T(128)S(1)} %stack.61.meta, bf16[432,128,128]{2,1,0:T(8,128)(2,1)S(1)} %copy-done, bf16[1,4,2,128,256]{4,3,2,1,0:T(8,128)(2,1)S(1)} %collective-permute-done.35.refs_0_, ...), custom_call_target="tpu_custom_call", output_to_operand_aliasing={{}: (7, {})} | custom-call | tf_op jit(solution)/shard_map/project/pallas_call | solution.py:396
  (139 shorter events, 54.9 us)
Async XLA Ops:
  21.4 41.1 %collective-permute-start.7 = (bf16[1,2,128,1536]{3,2,1,0:T(8,128)(2,1)S(1)}, bf16[1,2,128,1536]{3,2,1,0:T(8,128)(2,1)S(1)}, u32[]{:S(2)}, u32[]{:S(2)}) collective-permute-start(bf16[1,2,128,1536]{3,2,1,0:T(8,128)(2,1)S(1)} %get-tuple-element.22.refs_0_.refs_8_), channel_id=1, source_target_pairs={{0,8},{4,12},{8,0},{12,4},{16,24},{20,28},{24,16},{28,20},{1,9},{5... | collective-permute-start | bytes 2359304 | tf_op jit(solution)/shard_map/ppermute | solution.py:416
  22.7 40.5 %collective-permute-start.8 = (bf16[1,2,128,1536]{3,2,1,0:T(8,128)(2,1)S(1)}, bf16[1,2,128,1536]{3,2,1,0:T(8,128)(2,1)S(1)}, u32[]{:S(2)}, u32[]{:S(2)}) collective-permute-start(bf16[1,2,128,1536]{3,2,1,0:T(8,128)(2,1)S(1)} %get-tuple-element.22.refs_0_.refs_8_), channel_id=1, source_target_pairs={{0,16},{4,20},{8,24},{12,28},{16,0},{20,4},{24,8},{28,12},{1,17},{... | collective-permute-start | bytes 2359304 | tf_op jit(solution)/shard_map/ppermute | solution.py:416
  25.5 33.8 %collective-permute-start.31 = (bf16[1,2,2,128,256]{4,3,2,1,0:T(8,128)(2,1)S(1)}, bf16[1,2,2,128,256]{4,3,2,1,0:T(8,128)(2,1)S(1)}, u32[]{:S(2)}, u32[]{:S(2)}) collective-permute-start(bf16[1,2,2,128,256]{4,3,2,1,0:T(8,128)(2,1)S(1)} %maximum_bitcast_fusion.refs_12_), channel_id=1, source_target_pairs={{0,8},{4,12},{8,0},{12,4},{16,24},{20,28},{24,16},{28,20},{1,9},{5... | collective-permute-start | bytes 786440 | tf_op jit(solution)/shard_map/ppermute | solution.py:416
  26.0 34.6 %collective-permute-start.32 = (bf16[1,2,2,128,256]{4,3,2,1,0:T(8,128)(2,1)S(1)}, bf16[1,2,2,128,256]{4,3,2,1,0:T(8,128)(2,1)S(1)}, u32[]{:S(2)}, u32[]{:S(2)}) collective-permute-start(bf16[1,2,2,128,256]{4,3,2,1,0:T(8,128)(2,1)S(1)} %maximum_bitcast_fusion.refs_12_), channel_id=1, source_target_pairs={{0,16},{4,20},{8,24},{12,28},{16,0},{20,4},{24,8},{28,12},{1,17},{... | collective-permute-start | bytes 786440 | tf_op jit(solution)/shard_map/ppermute | solution.py:416
  59.3 19.0 %collective-permute-start.14 = (bf16[1,2,128,1536]{3,2,1,0:T(8,128)(2,1)S(1)}, bf16[1,2,128,1536]{3,2,1,0:T(8,128)(2,1)}, u32[]{:S(2)}, u32[]{:S(2)}) collective-permute-start(bf16[1,2,128,1536]{3,2,1,0:T(8,128)(2,1)S(1)} %get-tuple-element.21.refs_8_), channel_id=1, source_target_pairs={{0,16},{4,20},{8,24},{12,28},{16,0},{20,4},{24,8},{28,12},{1,17},{... | collective-permute-start | bytes 2359304 | tf_op jit(solution)/shard_map/ppermute | solution.py:416
  62.5 18.9 %collective-permute-start.17 = (bf16[1,2,128,1536]{3,2,1,0:T(8,128)(2,1)S(1)}, bf16[1,2,128,1536]{3,2,1,0:T(8,128)(2,1)}, u32[]{:S(2)}, u32[]{:S(2)}) collective-permute-start(bf16[1,2,128,1536]{3,2,1,0:T(8,128)(2,1)S(1)} %get-tuple-element.21.refs_8_), channel_id=1, source_target_pairs={{0,4},{4,0},{8,12},{12,8},{16,20},{20,16},{24,28},{28,24},{1,5},{5... | collective-permute-start | bytes 2359304 | tf_op jit(solution)/shard_map/ppermute | solution.py:416
  63.2 21.2 %collective-permute-start.21 = (bf16[12,128,256]{2,1,0:T(8,128)(2,1)}, bf16[12,128,256]{2,1,0:T(8,128)(2,1)}, u32[]{:S(2)}, u32[]{:S(2)}) collective-permute-start(bf16[12,128,256]{2,1,0:T(8,128)(2,1)} %pack.2), channel_id=1, source_target_pairs={{0,3},{1,2},{2,1},{3,0},{4,7},{5,6},{6,5},{7,4},{8,11},{9,10},{10,... | collective-permute-start | bytes 2359304 | tf_op jit(solution)/shard_map/ppermute | solution.py:416
  73.2 61.7 %collective-permute-start.22 = (bf16[12,128,256]{2,1,0:T(8,128)(2,1)S(1)}, bf16[12,128,256]{2,1,0:T(8,128)(2,1)S(1)}, u32[]{:S(2)}, u32[]{:S(2)}) collective-permute-start(bf16[12,128,256]{2,1,0:T(8,128)(2,1)S(1)} %get-tuple-element.16), channel_id=1, source_target_pairs={{0,2},{1,3},{2,0},{3,1},{4,6},{5,7},{6,4},{7,5},{8,10},{9,11},{10,... | collective-permute-start | bytes 2359304 | tf_op jit(solution)/shard_map/ppermute | solution.py:416
  78.3 56.8 %collective-permute-start.23 = (bf16[12,128,256]{2,1,0:T(8,128)(2,1)S(1)}, bf16[12,128,256]{2,1,0:T(8,128)(2,1)S(1)}, u32[]{:S(2)}, u32[]{:S(2)}) collective-permute-start(bf16[12,128,256]{2,1,0:T(8,128)(2,1)S(1)} %get-tuple-element.17), channel_id=1, source_target_pairs={{0,1},{1,0},{2,3},{3,2},{4,5},{5,4},{6,7},{7,6},{8,9},{9,8},{10,11... | collective-permute-start | bytes 2359304 | tf_op jit(solution)/shard_map/ppermute | solution.py:416
  80.0 56.1 %collective-permute-start.27 = (bf16[12,128,256]{2,1,0:T(8,128)(2,1)}, bf16[12,128,256]{2,1,0:T(8,128)(2,1)S(1)}, u32[]{:S(2)}, u32[]{:S(2)}) collective-permute-start(bf16[12,128,256]{2,1,0:T(8,128)(2,1)} %get-tuple-element.18.refs_3_), channel_id=1, source_target_pairs={{0,4},{4,0},{8,12},{12,8},{16,20},{20,16},{24,28},{28,24},{1,5},{5... | collective-permute-start | bytes 2359304 | tf_op jit(solution)/shard_map/ppermute | solution.py:416
  81.4 61.3 %collective-permute-start.9 = (bf16[1,2,128,1536]{3,2,1,0:T(8,128)(2,1)S(1)}, bf16[1,2,128,1536]{3,2,1,0:T(8,128)(2,1)S(1)}, u32[]{:S(2)}, u32[]{:S(2)}) collective-permute-start(bf16[1,2,128,1536]{3,2,1,0:T(8,128)(2,1)S(1)} %collective-permute-done.7.refs_1_.refs_9_), channel_id=1, source_target_pairs={{0,16},{4,20},{8,24},{12,28},{16,0},{20,4},{24,8},{28,12},{1,17},{... | collective-permute-start | bytes 2359304 | tf_op jit(solution)/shard_map/ppermute | solution.py:416
  84.4 60.2 %collective-permute-start.24 = (bf16[12,128,256]{2,1,0:T(8,128)(2,1)}, bf16[12,128,256]{2,1,0:T(8,128)(2,1)S(1)}, u32[]{:S(2)}, u32[]{:S(2)}) collective-permute-start(bf16[12,128,256]{2,1,0:T(8,128)(2,1)} %collective-permute-done.21.refs_0_), channel_id=1, source_target_pairs={{0,4},{4,0},{8,12},{12,8},{16,20},{20,16},{24,28},{28,24},{1,5},{5... | collective-permute-start | bytes 2359304 | tf_op jit(solution)/shard_map/ppermute | solution.py:416
  142.8 22.0 %collective-permute-start.11 = (bf16[1,2,128,1536]{3,2,1,0:T(8,128)(2,1)S(1)}, bf16[1,2,128,1536]{3,2,1,0:T(8,128)(2,1)S(1)}, u32[]{:S(2)}, u32[]{:S(2)}) collective-permute-start(bf16[1,2,128,1536]{3,2,1,0:T(8,128)(2,1)S(1)} %collective-permute-done.7.refs_1_.refs_9_), channel_id=1, source_target_pairs={{0,4},{4,0},{8,12},{12,8},{16,20},{20,16},{24,28},{28,24},{1,5},{5... | collective-permute-start | bytes 2359304 | tf_op jit(solution)/shard_map/ppermute | solution.py:416
  144.6 20.4 %collective-permute-start.12 = (bf16[1,2,128,1536]{3,2,1,0:T(8,128)(2,1)S(1)}, bf16[1,2,128,1536]{3,2,1,0:T(8,128)(2,1)S(1)}, u32[]{:S(2)}, u32[]{:S(2)}) collective-permute-start(bf16[1,2,128,1536]{3,2,1,0:T(8,128)(2,1)S(1)} %collective-permute-done.8.refs_2_.refs_10_), channel_id=1, source_target_pairs={{0,4},{4,0},{8,12},{12,8},{16,20},{20,16},{24,28},{28,24},{1,5},{5... | collective-permute-start | bytes 2359304 | tf_op jit(solution)/shard_map/ppermute | solution.py:416
  144.7 21.6 %collective-permute-start.18 = (bf16[1,2,128,1536]{3,2,1,0:T(8,128)(2,1)}, bf16[1,2,128,1536]{3,2,1,0:T(8,128)(2,1)S(1)}, u32[]{:S(2)}, u32[]{:S(2)}) collective-permute-start(bf16[1,2,128,1536]{3,2,1,0:T(8,128)(2,1)} %collective-permute-done.14.refs_9_), channel_id=1, source_target_pairs={{0,4},{4,0},{8,12},{12,8},{16,20},{20,16},{24,28},{28,24},{1,5},{5... | collective-permute-start | bytes 2359304 | tf_op jit(solution)/shard_map/ppermute | solution.py:416
  145.2 24.3 %collective-permute-start.19 = (bf16[1,2,128,1536]{3,2,1,0:T(8,128)(2,1)}, bf16[1,2,128,1536]{3,2,1,0:T(8,128)(2,1)S(1)}, u32[]{:S(2)}, u32[]{:S(2)}) collective-permute-start(bf16[1,2,128,1536]{3,2,1,0:T(8,128)(2,1)} %collective-permute-done.15.refs_10_), channel_id=1, source_target_pairs={{0,4},{4,0},{8,12},{12,8},{16,20},{20,16},{24,28},{28,24},{1,5},{5... | collective-permute-start | bytes 2359304 | tf_op jit(solution)/shard_map/ppermute | solution.py:416
  165.1 21.8 %collective-permute-start.40 = (bf16[1,4,2,128,256]{4,3,2,1,0:T(8,128)(2,1)S(1)}, bf16[1,4,2,128,256]{4,3,2,1,0:T(8,128)(2,1)S(1)}, u32[]{:S(2)}, u32[]{:S(2)}) collective-permute-start(bf16[1,4,2,128,256]{4,3,2,1,0:T(8,128)(2,1)S(1)} %bitcast.34), channel_id=1, source_target_pairs={{0,16},{4,20},{8,24},{12,28},{16,0},{20,4},{24,8},{28,12},{1,17},{... | collective-permute-start | bytes 1572872 | tf_op jit(solution)/shard_map/ppermute | solution.py:416
  166.3 24.1 %collective-permute-start.41 = (bf16[1,4,2,128,256]{4,3,2,1,0:T(8,128)(2,1)S(1)}, bf16[1,4,2,128,256]{4,3,2,1,0:T(8,128)(2,1)S(1)}, u32[]{:S(2)}, u32[]{:S(2)}) collective-permute-start(bf16[1,4,2,128,256]{4,3,2,1,0:T(8,128)(2,1)S(1)} %bitcast.35), channel_id=1, source_target_pairs={{0,4},{4,0},{8,12},{12,8},{16,20},{20,16},{24,28},{28,24},{1,5},{5... | collective-permute-start | bytes 1572872 | tf_op jit(solution)/shard_map/ppermute | solution.py:416
  169.5 21.1 %collective-permute-start.44 = (bf16[1,4,2,128,256]{4,3,2,1,0:T(8,128)(2,1)S(1)}, bf16[1,4,2,128,256]{4,3,2,1,0:T(8,128)(2,1)S(1)}, u32[]{:S(2)}, u32[]{:S(2)}) collective-permute-start(bf16[1,4,2,128,256]{4,3,2,1,0:T(8,128)(2,1)S(1)} %bitcast.38), channel_id=1, source_target_pairs={{0,8},{4,12},{8,0},{12,4},{16,24},{20,28},{24,16},{28,20},{1,9},{5... | collective-permute-start | bytes 1572872 | tf_op jit(solution)/shard_map/ppermute | solution.py:416
  171.1 20.8 %collective-permute-start.45 = (bf16[1,4,2,128,256]{4,3,2,1,0:T(8,128)(2,1)S(1)}, bf16[1,4,2,128,256]{4,3,2,1,0:T(8,128)(2,1)S(1)}, u32[]{:S(2)}, u32[]{:S(2)}) collective-permute-start(bf16[1,4,2,128,256]{4,3,2,1,0:T(8,128)(2,1)S(1)} %bitcast.39), channel_id=1, source_target_pairs={{0,4},{4,0},{8,12},{12,8},{16,20},{20,16},{24,28},{28,24},{1,5},{5... | collective-permute-start | bytes 1572872 | tf_op jit(solution)/shard_map/ppermute | solution.py:416
  192.4 25.5 %collective-permute-start.46 = (bf16[1,4,2,128,256]{4,3,2,1,0:T(8,128)(2,1)S(1)}, bf16[1,4,2,128,256]{4,3,2,1,0:T(8,128)(2,1)S(1)}, u32[]{:S(2)}, u32[]{:S(2)}) collective-permute-start(bf16[1,4,2,128,256]{4,3,2,1,0:T(8,128)(2,1)S(1)} %collective-permute-done.37.refs_7_), channel_id=1, source_target_pairs={{0,4},{4,0},{8,12},{12,8},{16,20},{20,16},{24,28},{28,24},{1,5},{5... | collective-permute-start | bytes 1572872 | tf_op jit(solution)/shard_map/ppermute | solution.py:416
  192.5 24.6 %collective-permute-start.43 = (bf16[1,4,2,128,256]{4,3,2,1,0:T(8,128)(2,1)S(1)}, bf16[1,4,2,128,256]{4,3,2,1,0:T(8,128)(2,1)S(1)}, u32[]{:S(2)}, u32[]{:S(2)}) collective-permute-start(bf16[1,4,2,128,256]{4,3,2,1,0:T(8,128)(2,1)S(1)} %collective-permute-done.40.refs_2_), channel_id=1, source_target_pairs={{0,4},{4,0},{8,12},{12,8},{16,20},{20,16},{24,28},{28,24},{1,5},{5... | collective-permute-start | bytes 1572872 | tf_op jit(solution)/shard_map/ppermute | solution.py:416
  204.7 29.5 %collective-permute-start.36 = (bf16[1,4,2,128,256]{4,3,2,1,0:T(8,128)(2,1)S(1)}, bf16[1,4,2,128,256]{4,3,2,1,0:T(8,128)(2,1)S(1)}, u32[]{:S(2)}, u32[]{:S(2)}) collective-permute-start(bf16[1,4,2,128,256]{4,3,2,1,0:T(8,128)(2,1)S(1)} %collective-permute-done.35.refs_0_), channel_id=1, source_target_pairs={{0,4},{4,0},{8,12},{12,8},{16,20},{20,16},{24,28},{28,24},{1,5},{5... | collective-permute-start | bytes 1572872 | tf_op jit(solution)/shard_map/ppermute | solution.py:416
  205.0 29.3 %collective-permute-start.39 = (bf16[1,4,2,128,256]{4,3,2,1,0:T(8,128)(2,1)S(1)}, bf16[1,4,2,128,256]{4,3,2,1,0:T(8,128)(2,1)S(1)}, u32[]{:S(2)}, u32[]{:S(2)}) collective-permute-start(bf16[1,4,2,128,256]{4,3,2,1,0:T(8,128)(2,1)S(1)} %collective-permute-done.38.refs_2_), channel_id=1, source_target_pairs={{0,4},{4,0},{8,12},{12,8},{16,20},{20,16},{24,28},{28,24},{1,5},{5... | collective-permute-start | bytes 1572872 | tf_op jit(solution)/shard_map/ppermute | solution.py:416
  (41 other events, 505.4 us)

commit v3 on v2

--- a/solution.py
+++ b/solution.py
@@ -123,12 +123,13 @@
 
 
 def potential_kernel(sizes, ids, meta, *refs):
-    tmasks, xmasks, omasks, fmasks, nlocal, rank, first = sizes
+    tmasks, xmasks, omasks, fmasks, nlocal, rank, nchunk = sizes
     panels, refs = refs[: len(tmasks)], refs[len(tmasks) :]
     values, refs = refs[: len(xmasks)], refs[len(xmasks) :]
     occ, refs = refs[: len(omasks)], refs[len(omasks) :]
     kern, refs = refs[0], refs[1:]
-    out, table, x, left, m, tsems, xsems = refs
+    outs, (table, x, left, m, tsems, xsems) = refs[:nchunk], refs[nchunk:]
+    groups = len(values) // nchunk
     nb, blk, width = panels[0].shape
     count, npts = x.shape[1], x.shape[2]
     sig = ids.shape[2]
@@ -142,7 +143,7 @@
     for i, piece in enumerate(values):
         loads.append(pltpu.make_async_copy(piece, x.at[pl.ds(at, piece.shape[0])], xsems.at[i]))
         for j, mask in enumerate(xmasks[i]):
-            todo += [(i, at + j, mask, b) for b in range(count)]
+            todo += [(i, i // groups, at + j, mask, b) for b in range(count)]
         at += piece.shape[0]
     for c in copies + loads:
         c.start()
@@ -158,44 +159,46 @@
     for c in copies:
         c.wait()
     seen = -1
-    for i, (piece, row, mask, b) in enumerate(todo):
+    for i, (piece, chunk, row, mask, b) in enumerate(todo):
         if piece != seen:
             loads[piece].wait()
             seen = piece
         f = fmasks.index(mask)
         dens = jnp.zeros((npts, width), F32)
         for s in range(0, sig, 2):
-            two = [table[ids[f, first + b, s + t]] for t in range(2)]
+            two = [table[ids[f, chunk * count + b, s + t]] for t in range(2)]
             dens += jnp.dot(
                 x[row, b, :, s * blk : (s + 2) * blk], jnp.concatenate(two, axis=0), preferred_element_type=F32
             )
         left[i] = dens.astype(BF16)
-    for i, (_, _, mask, b) in enumerate(todo):
-        rho = lax.dot_general(left[i], turn_of(mask, first + b), dims, preferred_element_type=F32)
-        weight = kern[fmasks.index(mask), first + b]
+    for i, (_, chunk, _, mask, b) in enumerate(todo):
+        rho = lax.dot_general(left[i], turn_of(mask, chunk * count + b), dims, preferred_element_type=F32)
+        weight = kern[fmasks.index(mask), chunk * count + b]
         m[i] = (rho * jnp.concatenate([weight, weight], axis=1)).astype(BF16)
-    for i, (_, _, mask, b) in enumerate(todo):
-        e = jnp.dot(m[i], turn_of(mask, first + b), preferred_element_type=F32)
-        out[meta[5] ^ (mask // rank), b] = e.astype(BF16)
-
-
-def potential(panels, values, occ, kern, ids, fmasks, meta, nlocal, rank, chunk):
+    for i, (_, chunk, _, mask, b) in enumerate(todo):
+        e = jnp.dot(m[i], turn_of(mask, chunk * count + b), preferred_element_type=F32)
+        outs[chunk][meta[5] ^ (mask // rank), b] = e.astype(BF16)
+
+
+def potential(panels, chunks, occ, kern, ids, fmasks, meta, nlocal, rank):
     tmasks = tuple(m for _, m in panels)
+    nchunk = len(chunks)
+    values = [piece for pieces in chunks for piece in pieces]
     xmasks = tuple(tuple(m) for _, m in values)
     omasks = tuple(tuple(m) for _, m in occ)
     count, npts, span = values[0][0].shape[1:]
     nb, blk, width = panels[0][0].shape
     nsrc = sum(len(m) for m in xmasks)
-    sizes = (tmasks, xmasks, omasks, tuple(fmasks), nlocal, rank, chunk * count)
+    sizes = (tmasks, xmasks, omasks, tuple(fmasks), nlocal, rank, nchunk)
     table = (len(panels) * nb, blk, width)
     x = (nsrc, count, npts, span)
     left = (nsrc * count, npts, width)
     m = (nsrc * count, npts, 2 * npts)
     return pl.pallas_call(
         functools.partial(potential_kernel, sizes),
-        out_shape=jax.ShapeDtypeStruct((nsrc, count, npts, width), BF16),
+        out_shape=(jax.ShapeDtypeStruct((nsrc // nchunk, count, npts, width), BF16),) * nchunk,
         in_specs=[SMEM, SMEM] + [VMEM] * len(panels) + [ANY] * len(values) + [VMEM] * (len(occ) + 1),
-        out_specs=VMEM,
+        out_specs=(VMEM,) * nchunk,
         scratch_shapes=[
             pltpu.VMEM(table, BF16),
             pltpu.VMEM(x, BF16),
@@ -456,7 +459,7 @@
         where = jnp.stack([side * nb] + [(ao ^ over) * nv + vector for over in planes]).astype(jnp.int32)
         rows = pack(trial, where, len(planes), nb, blk)
         if not panels:
-            rows, coords, weights = lax.optimization_barrier((rows, coords, weights))
+            rows, coords, weights, occupied = lax.optimization_barrier((rows, coords, weights, occupied))
         for over, one in zip(planes, rows, strict=True):
             panels.append((swap(one, "ao", over) if over else one, (over, 0)))
 
@@ -490,10 +493,10 @@
     for bit in part_bits:
         panels = panels + [(swap(a, "grid", bit), (over, m ^ bit)) for a, (over, m) in panels]
     columns = gather(far, facts, blk, group, 2 * rank)
+    parts = potential(panels, near, occ, kern, ids, fmasks, meta, nlocal, rank)
     early, late = [], []
     for chunk in range(2):
-        e = potential(panels, near[chunk], occ, kern, ids, fmasks, meta, nlocal, rank, chunk)
-        pieces = across(e[None], high_bits[::-1] if chunk else high_bits)
+        pieces = across(parts[chunk][None], high_bits[::-1] if chunk else high_bits)
         early += [(chunk, a, m) for a, m in within(pieces[:-1], low_bits)]
         late += [(chunk, a, m) for a, m in within(pieces[-1:], low_bits)]
     total = project(early, facts, columns, meta, None, rank, nown, group)

time: 243 us -> 243 us (level)
  the two profiles are of different devices: /device:TPU:1 before, /device:TPU:0 now
where the time goes in v3:
time: 243 us; the launch traced here: 238 us
  waiting for transfers between devices  149 us (61%)
  Pallas kernels  48.4 us (20%)
  starting transfers between devices  37.2 us (15%)
    ppermute x48, waiting for transfers between devices, swap(): return lax.ppermute(array, axis, [(i, i ^ bit) for i in range(size)])  149 us
    ppermute x48, starting transfers between devices, swap(): return lax.ppermute(array, axis, [(i, i ^ bit) for i in range(size)])  37.2 us
    pallas_call x2, Pallas kernels, project(): pl.pallas_call(functools.partial(project_kernel, (nchunk, emasks, rank, g...  17 us
    pallas_call x2, Pallas kernels, pack(): pl.pallas_call(pack_kernel, out_shape=(jax.ShapeDtypeStruct((nb, blk, 2 *...  11.2 us
    pallas_call x1, Pallas kernels, potential(): pl.pallas_call(functools.partial(potential_kernel, sizes), out_shape=(jax...  6.13 us
    pallas_call x1, Pallas kernels, gather(): pl.pallas_call(functools.partial(gather_kernel, group, nlist), out_shape=...  6.05 us
  transfers between devices with their start and end apart: 48, of which 21 were waited for; matrix products, arithmetic and copies ran while one was open for 1% of the time, Pallas kernels for 15%

profile of v3, /device:TPU:0, one launch (start us, length us, event | category | flops | bytes accessed | tf_op | source)
XLA Modules:
  0.0 238.0 jit_solution(11963764803573590813)
XLA Ops:
  0.1 4.1 %pack.2 = bf16[12,128,256]{2,1,0:T(8,128)(2,1)} custom-call(s32[2]{0:T(128)S(1)} %pad_add_fusion.where, bf16[3072,16,2,128]{3,2,1,0:T(2,128)(2,1)} %trial.3), custom_call_target="tpu_custom_call" | custom-call | tf_op jit(solution)/shard_map/pack/pallas_call | solution.py:67
  4.3 3.2 %occupied.1 = (f32[2,128,256]{2,1,0:T(8,128)S(1)}, bf16[2,128,256]{2,1,0:T(8,128)(2,1)S(1)}) custom-call(s32[4,12]{1,0:T(4,128)S(1)} %copy-done.8, s32[6]{0:T(128)S(1)} %stack.61.meta, bf16[3072,2,128]{2,1,0:T(2,128)(2,1)S(1)} %copy-done.2, bf16[4,128,1536]{2,1,0:T(8,128)(2,1)S(1)} %copy-done.1), custom_call_target="tpu_custom_call" | custom-call | tf_op jit(solution)/shard_map/occupied/pallas_call | solution.py:114
  7.6 3.1 %collective-permute-start.28 = (bf16[2,128,256]{2,1,0:T(8,128)(2,1)S(1)}, bf16[2,128,256]{2,1,0:T(8,128)(2,1)S(1)}, u32[]{:S(2)}, u32[]{:S(2)}) collective-permute-start(bf16[2,128,256]{2,1,0:T(8,128)(2,1)S(1)} %get-tuple-element.24), channel_id=1, source_target_pairs={{0,1},{1,0},{2,3},{3,2},{4,5},{5,4},{6,7},{7,6},{8,9},{9,8},{10,11... | collective-permute-start | bytes 393224 | tf_op jit(solution)/shard_map/ppermute | solution.py:419
  10.7 3.5 %collective-permute-done.28 = bf16[2,128,256]{2,1,0:T(8,128)(2,1)S(1)} collective-permute-done((bf16[2,128,256]{2,1,0:T(8,128)(2,1)S(1)}, bf16[2,128,256]{2,1,0:T(8,128)(2,1)S(1)}, u32[]{:S(2)}, u32[]{:S(2)}) %collective-permute-start.28) | collective-permute-done | bytes 131104 | tf_op jit(solution)/shard_map/ppermute | solution.py:419
  14.3 2.8 %collective-permute-start.29 = (bf16[2,128,256]{2,1,0:T(8,128)(2,1)S(1)}, bf16[2,128,256]{2,1,0:T(8,128)(2,1)S(1)}, u32[]{:S(2)}, u32[]{:S(2)}) collective-permute-start(bf16[2,128,256]{2,1,0:T(8,128)(2,1)S(1)} %fusion), channel_id=1, source_target_pairs={{0,2},{1,3},{2,0},{3,1},{4,6},{5,7},{6,4},{7,5},{8,10},{9,11},{10,... | collective-permute-start | bytes 393224 | tf_op jit(solution)/shard_map/ppermute | solution.py:419
  17.1 5.6 %collective-permute-done.29 = bf16[2,128,256]{2,1,0:T(8,128)(2,1)S(1)} collective-permute-done((bf16[2,128,256]{2,1,0:T(8,128)(2,1)S(1)}, bf16[2,128,256]{2,1,0:T(8,128)(2,1)S(1)}, u32[]{:S(2)}, u32[]{:S(2)}) %collective-permute-start.29) | collective-permute-done | bytes 131104 | tf_op jit(solution)/shard_map/ppermute | solution.py:419
  30.0 18.0 %collective-permute-done = f32[1,4,5,128]{3,1,0,2:T(4,128)S(1)} collective-permute-done((f32[1,4,5,128]{3,1,0,2:T(4,128)S(1)}, f32[1,4,5,128]{3,1,0,2:T(4,128)S(1)}, u32[]{:S(2)}, u32[]{:S(2)}) %collective-permute-start) | collective-permute-done | bytes 10272 | tf_op jit(solution)/shard_map/ppermute | solution.py:419
  49.5 2.2 collective-permute-done.1
  62.1 7.1 %collective-permute-done.32.refs_18_ = bf16[1,2,2,128,256]{4,3,2,1,0:T(8,128)(2,1)S(1)} collective-permute-done((bf16[1,2,2,128,256]{4,3,2,1,0:T(8,128)(2,1)S(1)}, bf16[1,2,2,128,256]{4,3,2,1,0:T(8,128)(2,1)S(1)}, u32[]{:S(2)}, u32[]{:S(2)}) %collective-permute-start.32) | collective-permute-done | bytes 262176 | tf_op jit(solution)/shard_map/ppermute | solution.py:419
  71.4 3.1 %collective-permute-start.21 = (bf16[12,128,256]{2,1,0:T(8,128)(2,1)}, bf16[12,128,256]{2,1,0:T(8,128)(2,1)}, u32[]{:S(2)}, u32[]{:S(2)}) collective-permute-start(bf16[12,128,256]{2,1,0:T(8,128)(2,1)} %pack.2), channel_id=1, source_target_pairs={{0,3},{1,2},{2,1},{3,0},{4,7},{5,6},{6,5},{7,4},{8,11},{9,10},{10,... | collective-permute-start | bytes 2359304 | tf_op jit(solution)/shard_map/ppermute | solution.py:419
  74.6 7.0 %pack.3 = (bf16[12,128,256]{2,1,0:T(8,128)(2,1)S(1)}, bf16[12,128,256]{2,1,0:T(8,128)(2,1)S(1)}, bf16[12,128,256]{2,1,0:T(8,128)(2,1)}) custom-call(s32[4]{0:T(128)S(1)} %pad_add_fusion.1.where, bf16[3072,16,2,128]{3,2,1,0:T(2,128)(2,1)} %trial.3), custom_call_target="tpu_custom_call" | custom-call | tf_op jit(solution)/shard_map/pack/pallas_call | solution.py:67
  83.0 2.4 collective-permute-done.14.refs_9_.refs_13_
  85.4 2.6 %collective-permute-done.15.refs_10_.refs_14_ = bf16[1,2,128,1536]{3,2,1,0:T(8,128)(2,1)} collective-permute-done((bf16[1,2,128,1536]{3,2,1,0:T(8,128)(2,1)S(1)}, bf16[1,2,128,1536]{3,2,1,0:T(8,128)(2,1)}, u32[]{:S(2)}, u32[]{:S(2)}) %collective-permute-start.15) | collective-permute-done | bytes 786464 | tf_op jit(solution)/shard_map/ppermute | solution.py:419
  89.5 4.5 %collective-permute-done.21.refs_0_ = bf16[12,128,256]{2,1,0:T(8,128)(2,1)} collective-permute-done((bf16[12,128,256]{2,1,0:T(8,128)(2,1)}, bf16[12,128,256]{2,1,0:T(8,128)(2,1)}, u32[]{:S(2)}, u32[]{:S(2)}) %collective-permute-start.21) | collective-permute-done | bytes 786464 | tf_op jit(solution)/shard_map/ppermute | solution.py:419
  95.6 45.9 %collective-permute-done.22.refs_1_ = bf16[12,128,256]{2,1,0:T(8,128)(2,1)S(1)} collective-permute-done((bf16[12,128,256]{2,1,0:T(8,128)(2,1)S(1)}, bf16[12,128,256]{2,1,0:T(8,128)(2,1)S(1)}, u32[]{:S(2)}, u32[]{:S(2)}) %collective-permute-start.22) | collective-permute-done | bytes 786464 | tf_op jit(solution)/shard_map/ppermute | solution.py:419
  144.8 16.2 %collective-permute-done.16.refs_11_.refs_15_ = bf16[1,2,128,1536]{3,2,1,0:T(8,128)(2,1)S(1)} collective-permute-done((bf16[1,2,128,1536]{3,2,1,0:T(8,128)(2,1)}, bf16[1,2,128,1536]{3,2,1,0:T(8,128)(2,1)S(1)}, u32[]{:S(2)}, u32[]{:S(2)}) %collective-permute-start.16) | collective-permute-done | bytes 786464 | tf_op jit(solution)/shard_map/ppermute | solution.py:419
  162.2 6.1 %potential.1 = (bf16[4,2,128,256]{3,2,1,0:T(8,128)(2,1)S(1)}, bf16[4,2,128,256]{3,2,1,0:T(8,128)(2,1)S(1)}) custom-call(s32[8,4,12]{2,1,0:T(4,128)S(1)} %fusion.1.ids, s32[6]{0:T(128)S(1)} %stack.61.meta, bf16[12,128,256]{2,1,0:T(8,128)(2,1)} %collective-permute-done.21.refs_0_, bf16[12,128,256]{2,1,0:T(8,128)(2,1)S(1)} %collective-permute-done.22.refs_1_, ...), custom_call_target="tpu_custom_call" | custom-call | tf_op jit(solution)/shard_map/potential/pallas_call | solution.py:197
  172.5 10.7 %collective-permute-done.34.refs_1_ = bf16[1,4,2,128,256]{4,3,2,1,0:T(8,128)(2,1)S(1)} collective-permute-done((bf16[1,4,2,128,256]{4,3,2,1,0:T(8,128)(2,1)S(1)}, bf16[1,4,2,128,256]{4,3,2,1,0:T(8,128)(2,1)S(1)}, u32[]{:S(2)}, u32[]{:S(2)}) %collective-permute-start.34) | collective-permute-done | bytes 524320 | tf_op jit(solution)/shard_map/ppermute | solution.py:419
  183.7 10.1 %collective-permute-done.40.refs_2_ = bf16[1,4,2,128,256]{4,3,2,1,0:T(8,128)(2,1)S(1)} collective-permute-done((bf16[1,4,2,128,256]{4,3,2,1,0:T(8,128)(2,1)S(1)}, bf16[1,4,2,128,256]{4,3,2,1,0:T(8,128)(2,1)S(1)}, u32[]{:S(2)}, u32[]{:S(2)}) %collective-permute-start.40) | collective-permute-done | bytes 524320 | tf_op jit(solution)/shard_map/ppermute | solution.py:419
  197.4 10.7 %collective-permute-done.35.refs_0_ = bf16[1,4,2,128,256]{4,3,2,1,0:T(8,128)(2,1)S(1)} collective-permute-done((bf16[1,4,2,128,256]{4,3,2,1,0:T(8,128)(2,1)S(1)}, bf16[1,4,2,128,256]{4,3,2,1,0:T(8,128)(2,1)S(1)}, u32[]{:S(2)}, u32[]{:S(2)}) %collective-permute-start.35) | collective-permute-done | bytes 524320 | tf_op jit(solution)/shard_map/ppermute | solution.py:419
  209.9 4.8 %pairs.1.facts = s32[8,432]{1,0:T(8,128)S(1)} custom-call(s32[8,4,12]{2,1,0:T(4,128)S(1)} %fusion.1.ids, s32[6]{0:T(128)S(1)} %stack.61.meta), custom_call_target="tpu_custom_call" | custom-call | tf_op jit(solution)/shard_map/pairs/pallas_call | solution.py:267
  214.7 6.1 %gather.1.columns = bf16[432,128,128]{2,1,0:T(8,128)(2,1)} custom-call(s32[8,432]{1,0:T(8,128)S(1)} %pairs.1.facts, bf16[1,2,128,1536]{3,2,1,0:T(8,128)(2,1)S(1)} %get-tuple-element.28.refs_0_.refs_8_, bf16[1,2,128,1536]{3,2,1,0:T(8,128)(2,1)S(1)} %collective-permute-done.7.refs_1_.refs_9_, ...), custom_call_target="tpu_custom_call" | custom-call | tf_op jit(solution)/shard_map/gather/pallas_call | solution.py:317
  220.8 10.9 %project.2.refs_4_ = f32[4,3072,128]{2,1,0:T(8,128)} custom-call(s32[8,432]{1,0:T(8,128)S(1)} %pairs.1.facts, s32[6]{0:T(128)S(1)} %stack.61.meta, bf16[432,128,128]{2,1,0:T(8,128)(2,1)} %gather.1.columns, bf16[1,4,2,128,256]{4,3,2,1,0:T(8,128)(2,1)S(1)} %bitcast.36, bf16[1,4,2,128,256]{4,3,2,1,0:T(8,128)(2,1)S(1)} %collective-permute-done.34.refs_1_, ...), custom_call_target="tpu_custom_call" | custom-call | tf_op jit(solution)/shard_map/project/pallas_call | solution.py:399
  231.7 6.1 %project.3 = f32[4,3072,128]{2,1,0:T(8,128)} custom-call(s32[8,432]{1,0:T(8,128)S(1)} %pairs.1.facts, s32[6]{0:T(128)S(1)} %stack.61.meta, bf16[432,128,128]{2,1,0:T(8,128)(2,1)S(1)} %copy-done, bf16[1,4,2,128,256]{4,3,2,1,0:T(8,128)(2,1)S(1)} %collective-permute-done.35.refs_0_, ...), custom_call_target="tpu_custom_call", output_to_operand_aliasing={{}: (7, {})} | custom-call | tf_op jit(solution)/shard_map/project/pallas_call | solution.py:399
  (126 shorter events, 40.6 us)
Async XLA Ops:
  23.5 47.9 %collective-permute-start.7 = (bf16[1,2,128,1536]{3,2,1,0:T(8,128)(2,1)S(1)}, bf16[1,2,128,1536]{3,2,1,0:T(8,128)(2,1)S(1)}, u32[]{:S(2)}, u32[]{:S(2)}) collective-permute-start(bf16[1,2,128,1536]{3,2,1,0:T(8,128)(2,1)S(1)} %get-tuple-element.28.refs_0_.refs_8_), channel_id=1, source_target_pairs={{0,8},{4,12},{8,0},{12,4},{16,24},{20,28},{24,16},{28,20},{1,9},{5... | collective-permute-start | bytes 2359304 | tf_op jit(solution)/shard_map/ppermute | solution.py:419
  25.0 56.6 %collective-permute-start.8 = (bf16[1,2,128,1536]{3,2,1,0:T(8,128)(2,1)S(1)}, bf16[1,2,128,1536]{3,2,1,0:T(8,128)(2,1)S(1)}, u32[]{:S(2)}, u32[]{:S(2)}) collective-permute-start(bf16[1,2,128,1536]{3,2,1,0:T(8,128)(2,1)S(1)} %get-tuple-element.28.refs_0_.refs_8_), channel_id=1, source_target_pairs={{0,16},{4,20},{8,24},{12,28},{16,0},{20,4},{24,8},{28,12},{1,17},{... | collective-permute-start | bytes 2359304 | tf_op jit(solution)/shard_map/ppermute | solution.py:419
  26.6 55.5 %collective-permute-start.10 = (bf16[1,2,128,1536]{3,2,1,0:T(8,128)(2,1)S(1)}, bf16[1,2,128,1536]{3,2,1,0:T(8,128)(2,1)}, u32[]{:S(2)}, u32[]{:S(2)}) collective-permute-start(bf16[1,2,128,1536]{3,2,1,0:T(8,128)(2,1)S(1)} %get-tuple-element.28.refs_0_.refs_8_), channel_id=1, source_target_pairs={{0,4},{4,0},{8,12},{12,8},{16,20},{20,16},{24,28},{28,24},{1,5},{5... | collective-permute-start | bytes 2359304 | tf_op jit(solution)/shard_map/ppermute | solution.py:419
  27.8 33.7 %collective-permute-start.31 = (bf16[1,2,2,128,256]{4,3,2,1,0:T(8,128)(2,1)S(1)}, bf16[1,2,2,128,256]{4,3,2,1,0:T(8,128)(2,1)S(1)}, u32[]{:S(2)}, u32[]{:S(2)}) collective-permute-start(bf16[1,2,2,128,256]{4,3,2,1,0:T(8,128)(2,1)S(1)} %maximum_bitcast_fusion.refs_16_), channel_id=1, source_target_pairs={{0,8},{4,12},{8,0},{12,4},{16,24},{20,28},{24,16},{28,20},{1,9},{5... | collective-permute-start | bytes 786440 | tf_op jit(solution)/shard_map/ppermute | solution.py:419
  29.3 18.7 %collective-permute-start = (f32[1,4,5,128]{3,1,0,2:T(4,128)S(1)}, f32[1,4,5,128]{3,1,0,2:T(4,128)S(1)}, u32[]{:S(2)}, u32[]{:S(2)}) collective-permute-start(f32[1,4,5,128]{3,1,0,2:T(4,128)S(1)} %maximum_bitcast_fusion.1), channel_id=1, source_target_pairs={{0,8},{4,12},{8,0},{12,4},{16,24},{20,28},{24,16},{28,20},{1,9},{5... | collective-permute-start | bytes 30728 | tf_op jit(solution)/shard_map/ppermute | solution.py:419
  61.6 23.8 %collective-permute-start.14 = (bf16[1,2,128,1536]{3,2,1,0:T(8,128)(2,1)S(1)}, bf16[1,2,128,1536]{3,2,1,0:T(8,128)(2,1)}, u32[]{:S(2)}, u32[]{:S(2)}) collective-permute-start(bf16[1,2,128,1536]{3,2,1,0:T(8,128)(2,1)S(1)} %get-tuple-element.27.refs_8_.refs_12_), channel_id=1, source_target_pairs={{0,16},{4,20},{8,24},{12,28},{16,0},{20,4},{24,8},{28,12},{1,17},{... | collective-permute-start | bytes 2359304 | tf_op jit(solution)/shard_map/ppermute | solution.py:419
  71.4 22.6 %collective-permute-start.21 = (bf16[12,128,256]{2,1,0:T(8,128)(2,1)}, bf16[12,128,256]{2,1,0:T(8,128)(2,1)}, u32[]{:S(2)}, u32[]{:S(2)}) collective-permute-start(bf16[12,128,256]{2,1,0:T(8,128)(2,1)} %pack.2), channel_id=1, source_target_pairs={{0,3},{1,2},{2,1},{3,0},{4,7},{5,6},{6,5},{7,4},{8,11},{9,10},{10,... | collective-permute-start | bytes 2359304 | tf_op jit(solution)/shard_map/ppermute | solution.py:419
  81.7 59.8 %collective-permute-start.22 = (bf16[12,128,256]{2,1,0:T(8,128)(2,1)S(1)}, bf16[12,128,256]{2,1,0:T(8,128)(2,1)S(1)}, u32[]{:S(2)}, u32[]{:S(2)}) collective-permute-start(bf16[12,128,256]{2,1,0:T(8,128)(2,1)S(1)} %get-tuple-element.19), channel_id=1, source_target_pairs={{0,2},{1,3},{2,0},{3,1},{4,6},{5,7},{6,4},{7,5},{8,10},{9,11},{10,... | collective-permute-start | bytes 2359304 | tf_op jit(solution)/shard_map/ppermute | solution.py:419
  82.0 60.0 %collective-permute-start.23 = (bf16[12,128,256]{2,1,0:T(8,128)(2,1)S(1)}, bf16[12,128,256]{2,1,0:T(8,128)(2,1)S(1)}, u32[]{:S(2)}, u32[]{:S(2)}) collective-permute-start(bf16[12,128,256]{2,1,0:T(8,128)(2,1)S(1)} %get-tuple-element.20), channel_id=1, source_target_pairs={{0,1},{1,0},{2,3},{3,2},{4,5},{5,4},{6,7},{7,6},{8,9},{9,8},{10,11... | collective-permute-start | bytes 2359304 | tf_op jit(solution)/shard_map/ppermute | solution.py:419
  85.4 56.7 %collective-permute-start.27 = (bf16[12,128,256]{2,1,0:T(8,128)(2,1)}, bf16[12,128,256]{2,1,0:T(8,128)(2,1)S(1)}, u32[]{:S(2)}, u32[]{:S(2)}) collective-permute-start(bf16[12,128,256]{2,1,0:T(8,128)(2,1)} %get-tuple-element.21.refs_3_), channel_id=1, source_target_pairs={{0,4},{4,0},{8,12},{12,8},{16,20},{20,16},{24,28},{28,24},{1,5},{5... | collective-permute-start | bytes 2359304 | tf_op jit(solution)/shard_map/ppermute | solution.py:419
  88.0 56.0 %collective-permute-start.9 = (bf16[1,2,128,1536]{3,2,1,0:T(8,128)(2,1)S(1)}, bf16[1,2,128,1536]{3,2,1,0:T(8,128)(2,1)S(1)}, u32[]{:S(2)}, u32[]{:S(2)}) collective-permute-start(bf16[1,2,128,1536]{3,2,1,0:T(8,128)(2,1)S(1)} %collective-permute-done.7.refs_1_.refs_9_), channel_id=1, source_target_pairs={{0,16},{4,20},{8,24},{12,28},{16,0},{20,4},{24,8},{28,12},{1,17},{... | collective-permute-start | bytes 2359304 | tf_op jit(solution)/shard_map/ppermute | solution.py:419
  94.0 48.6 %collective-permute-start.33 = (bf16[1,2,2,128,256]{4,3,2,1,0:T(8,128)(2,1)S(1)}, bf16[1,2,2,128,256]{4,3,2,1,0:T(8,128)(2,1)S(1)}, u32[]{:S(2)}, u32[]{:S(2)}) collective-permute-start(bf16[1,2,2,128,256]{4,3,2,1,0:T(8,128)(2,1)S(1)} %copy-done.5), channel_id=1, source_target_pairs={{0,16},{4,20},{8,24},{12,28},{16,0},{20,4},{24,8},{28,12},{1,17},{... | collective-permute-start | bytes 786440 | tf_op jit(solution)/shard_map/ppermute | solution.py:419
  141.5 19.5 %collective-permute-start.16 = (bf16[1,2,128,1536]{3,2,1,0:T(8,128)(2,1)}, bf16[1,2,128,1536]{3,2,1,0:T(8,128)(2,1)S(1)}, u32[]{:S(2)}, u32[]{:S(2)}) collective-permute-start(bf16[1,2,128,1536]{3,2,1,0:T(8,128)(2,1)} %collective-permute-done.14.refs_9_.refs_13_), channel_id=1, source_target_pairs={{0,8},{4,12},{8,0},{12,4},{16,24},{20,28},{24,16},{28,20},{1,9},{5... | collective-permute-start | bytes 2359304 | tf_op jit(solution)/shard_map/ppermute | solution.py:419
  142.0 19.0 %collective-permute-start.24 = (bf16[12,128,256]{2,1,0:T(8,128)(2,1)}, bf16[12,128,256]{2,1,0:T(8,128)(2,1)S(1)}, u32[]{:S(2)}, u32[]{:S(2)}) collective-permute-start(bf16[12,128,256]{2,1,0:T(8,128)(2,1)} %collective-permute-done.21.refs_0_), channel_id=1, source_target_pairs={{0,4},{4,0},{8,12},{12,8},{16,20},{20,16},{24,28},{28,24},{1,5},{5... | collective-permute-start | bytes 2359304 | tf_op jit(solution)/shard_map/ppermute | solution.py:419
  142.1 19.5 %collective-permute-start.25 = (bf16[12,128,256]{2,1,0:T(8,128)(2,1)S(1)}, bf16[12,128,256]{2,1,0:T(8,128)(2,1)S(1)}, u32[]{:S(2)}, u32[]{:S(2)}) collective-permute-start(bf16[12,128,256]{2,1,0:T(8,128)(2,1)S(1)} %collective-permute-done.22.refs_1_), channel_id=1, source_target_pairs={{0,4},{4,0},{8,12},{12,8},{16,20},{20,16},{24,28},{28,24},{1,5},{5... | collective-permute-start | bytes 2359304 | tf_op jit(solution)/shard_map/ppermute | solution.py:419
  142.6 19.0 %collective-permute-start.26 = (bf16[12,128,256]{2,1,0:T(8,128)(2,1)S(1)}, bf16[12,128,256]{2,1,0:T(8,128)(2,1)S(1)}, u32[]{:S(2)}, u32[]{:S(2)}) collective-permute-start(bf16[12,128,256]{2,1,0:T(8,128)(2,1)S(1)} %collective-permute-done.23.refs_2_), channel_id=1, source_target_pairs={{0,4},{4,0},{8,12},{12,8},{16,20},{20,16},{24,28},{28,24},{1,5},{5... | collective-permute-start | bytes 2359304 | tf_op jit(solution)/shard_map/ppermute | solution.py:419
  144.0 24.3 %collective-permute-start.17 = (bf16[1,2,128,1536]{3,2,1,0:T(8,128)(2,1)S(1)}, bf16[1,2,128,1536]{3,2,1,0:T(8,128)(2,1)S(1)}, u32[]{:S(2)}, u32[]{:S(2)}) collective-permute-start(bf16[1,2,128,1536]{3,2,1,0:T(8,128)(2,1)S(1)} %get-tuple-element.27.refs_8_.refs_12_), channel_id=1, source_target_pairs={{0,4},{4,0},{8,12},{12,8},{16,20},{20,16},{24,28},{28,24},{1,5},{5... | collective-permute-start | bytes 2359304 | tf_op jit(solution)/shard_map/ppermute | solution.py:419
  170.4 23.3 %collective-permute-start.40 = (bf16[1,4,2,128,256]{4,3,2,1,0:T(8,128)(2,1)S(1)}, bf16[1,4,2,128,256]{4,3,2,1,0:T(8,128)(2,1)S(1)}, u32[]{:S(2)}, u32[]{:S(2)}) collective-permute-start(bf16[1,4,2,128,256]{4,3,2,1,0:T(8,128)(2,1)S(1)} %bitcast.34), channel_id=1, source_target_pairs={{0,16},{4,20},{8,24},{12,28},{16,0},{20,4},{24,8},{28,12},{1,17},{... | collective-permute-start | bytes 1572872 | tf_op jit(solution)/shard_map/ppermute | solution.py:419
  171.0 22.8 %collective-permute-start.41 = (bf16[1,4,2,128,256]{4,3,2,1,0:T(8,128)(2,1)S(1)}, bf16[1,4,2,128,256]{4,3,2,1,0:T(8,128)(2,1)S(1)}, u32[]{:S(2)}, u32[]{:S(2)}) collective-permute-start(bf16[1,4,2,128,256]{4,3,2,1,0:T(8,128)(2,1)S(1)} %bitcast.35), channel_id=1, source_target_pairs={{0,4},{4,0},{8,12},{12,8},{16,20},{20,16},{24,28},{28,24},{1,5},{5... | collective-permute-start | bytes 1572872 | tf_op jit(solution)/shard_map/ppermute | solution.py:419
  171.0 24.4 %collective-permute-start.44 = (bf16[1,4,2,128,256]{4,3,2,1,0:T(8,128)(2,1)S(1)}, bf16[1,4,2,128,256]{4,3,2,1,0:T(8,128)(2,1)S(1)}, u32[]{:S(2)}, u32[]{:S(2)}) collective-permute-start(bf16[1,4,2,128,256]{4,3,2,1,0:T(8,128)(2,1)S(1)} %bitcast.38), channel_id=1, source_target_pairs={{0,8},{4,12},{8,0},{12,4},{16,24},{20,28},{24,16},{28,20},{1,9},{5... | collective-permute-start | bytes 1572872 | tf_op jit(solution)/shard_map/ppermute | solution.py:419
  196.8 24.0 %collective-permute-start.46 = (bf16[1,4,2,128,256]{4,3,2,1,0:T(8,128)(2,1)S(1)}, bf16[1,4,2,128,256]{4,3,2,1,0:T(8,128)(2,1)S(1)}, u32[]{:S(2)}, u32[]{:S(2)}) collective-permute-start(bf16[1,4,2,128,256]{4,3,2,1,0:T(8,128)(2,1)S(1)} %collective-permute-done.37.refs_7_), channel_id=1, source_target_pairs={{0,4},{4,0},{8,12},{12,8},{16,20},{20,16},{24,28},{28,24},{1,5},{5... | collective-permute-start | bytes 1572872 | tf_op jit(solution)/shard_map/ppermute | solution.py:419
  197.3 23.5 %collective-permute-start.43 = (bf16[1,4,2,128,256]{4,3,2,1,0:T(8,128)(2,1)S(1)}, bf16[1,4,2,128,256]{4,3,2,1,0:T(8,128)(2,1)S(1)}, u32[]{:S(2)}, u32[]{:S(2)}) collective-permute-start(bf16[1,4,2,128,256]{4,3,2,1,0:T(8,128)(2,1)S(1)} %collective-permute-done.40.refs_2_), channel_id=1, source_target_pairs={{0,4},{4,0},{8,12},{12,8},{16,20},{20,16},{24,28},{28,24},{1,5},{5... | collective-permute-start | bytes 1572872 | tf_op jit(solution)/shard_map/ppermute | solution.py:419
  209.4 22.4 %collective-permute-start.36 = (bf16[1,4,2,128,256]{4,3,2,1,0:T(8,128)(2,1)S(1)}, bf16[1,4,2,128,256]{4,3,2,1,0:T(8,128)(2,1)S(1)}, u32[]{:S(2)}, u32[]{:S(2)}) collective-permute-start(bf16[1,4,2,128,256]{4,3,2,1,0:T(8,128)(2,1)S(1)} %collective-permute-done.35.refs_0_), channel_id=1, source_target_pairs={{0,4},{4,0},{8,12},{12,8},{16,20},{20,16},{24,28},{28,24},{1,5},{5... | collective-permute-start | bytes 1572872 | tf_op jit(solution)/shard_map/ppermute | solution.py:419
  209.4 22.4 %collective-permute-start.39 = (bf16[1,4,2,128,256]{4,3,2,1,0:T(8,128)(2,1)S(1)}, bf16[1,4,2,128,256]{4,3,2,1,0:T(8,128)(2,1)S(1)}, u32[]{:S(2)}, u32[]{:S(2)}) collective-permute-start(bf16[1,4,2,128,256]{4,3,2,1,0:T(8,128)(2,1)S(1)} %collective-permute-done.38.refs_2_), channel_id=1, source_target_pairs={{0,4},{4,0},{8,12},{12,8},{16,20},{20,16},{24,28},{28,24},{1,5},{5... | collective-permute-start | bytes 1572872 | tf_op jit(solution)/shard_map/ppermute | solution.py:419
  (35 other events, 467.0 us)

commit v4 on v3

--- a/solution.py
+++ b/solution.py
@@ -275,9 +275,9 @@
     )(ids, meta)
 
 
-def gather_kernel(group, nlist, facts, *refs):
-    values, (columns, x, rows, xsems, osems) = refs[:-5], refs[-5:]
-    blk = rows.shape[1]
+def gather_kernel(nlist, facts, *refs):
+    values, (columns, x, xsems) = refs[:-3], refs[-3:]
+    blk = columns.shape[1]
     copies = []
     at = 0
     for i, piece in enumerate(values):
@@ -287,74 +287,43 @@
         c.start()
     for c in copies:
         c.wait()
-    n = facts[5, nlist]
 
     def one(i, carry):
         for t in range(4):
             row = facts[3, 4 * i + t]
             start = pl.multiple_of(facts[4, 4 * i + t] * blk, blk)
             column = x[jnp.maximum(row, 0), facts[2, 4 * i + t], :, pl.ds(start, blk)]
-            rows[4 * i + t] = jnp.where(row >= 0, column, jnp.zeros_like(column)).T
+            columns[4 * i + t] = jnp.where(row >= 0, column, jnp.zeros_like(column)).T
         return carry
 
-    lax.fori_loop(0, lax.div(n, 4), one, 0)
-    outs = [
-        pltpu.make_async_copy(rows.at[pl.ds(i * group, group)], columns.at[pl.ds(i * group, group)], osems.at[i])
-        for i in range(columns.shape[0] // group)
-    ]
-    for act in ("start", "wait"):
-        for i, c in enumerate(outs):
-
-            @pl.when(i * group < n)
-            def _(c=c, act=act):
-                getattr(c, act)()
-
-
-def gather(values, facts, blk, group, nlist):
+    lax.fori_loop(0, lax.div(facts[5, nlist], 4), one, 0)
+
+
+def gather(values, facts, blk, nlist):
     flat = [a for pieces in values for a, _ in pieces]
     count, npts, span = flat[0].shape[1:]
     most = facts.shape[1]
-    return pl.pallas_call(
-        functools.partial(gather_kernel, group, nlist),
+    x = (sum(a.shape[0] for a in flat), count, npts, span)
+    large = most * blk * npts * 2 > 16 * MIB
+    return pl.pallas_call(
+        functools.partial(gather_kernel, nlist),
         out_shape=jax.ShapeDtypeStruct((most, blk, npts), BF16),
         in_specs=[SMEM] + [ANY] * len(flat),
-        out_specs=ANY,
-        scratch_shapes=[
-            pltpu.VMEM((sum(a.shape[0] for a in flat), count, npts, span), BF16),
-            pltpu.VMEM((most, blk, npts), BF16),
-            pltpu.SemaphoreType.DMA((len(flat),)),
-            pltpu.SemaphoreType.DMA((most // group,)),
-        ],
-        compiler_params=params(((most, blk, npts), 2), ((sum(a.shape[0] for a in flat), count, npts, span), 2)),
+        out_specs=VMEM,
+        scratch_shapes=[pltpu.VMEM(x, BF16), pltpu.SemaphoreType.DMA((len(flat),))],
+        compiler_params=params((x, 2), ((most if large else 0, blk, npts), 2)),
         name="gather",
     )(facts, *flat)
 
 
 def project_kernel(sizes, facts, meta, columns, *refs):
-    nchunk, emasks, rank, group, nown, again = sizes
+    nchunk, emasks, rank, nown, again = sizes
     ne = len(emasks)
     potentials, refs = refs[:ne], refs[ne + again :]
-    out, x, staged, total, xsems, osems = refs
-    blk = x.shape[1]
+    out, staged, total, osems = refs
+    blk = columns.shape[1]
     offsets = sorted({mask // rank for _, masks in emasks for mask in masks})
-    n = facts[5, nchunk * rank]
-    xcopies = [
-        pltpu.make_async_copy(columns.at[pl.ds(i * group, group)], x.at[pl.ds(i * group, group)], xsems.at[i])
-        for i in range(columns.shape[0] // group)
-    ]
-    for i, c in enumerate(xcopies):
-
-        @pl.when(i * group < n)
-        def _(c=c):
-            c.start()
-
     total[...] = jnp.zeros_like(total)
-    for i, c in enumerate(xcopies):
-
-        @pl.when(i * group < n)
-        def _(c=c):
-            c.wait()
-
     for t in range(nchunk * rank):
         mine = [
             (i, j, offsets.index(mask // rank))
@@ -367,7 +336,7 @@
             for at in range(4):
                 own, source, b = [facts[f, 4 * p + at] for f in range(3)]
                 for i, j, k in mine:
-                    total[k, own] += jnp.dot(x[4 * p + at], potentials[i][j, source, b], preferred_element_type=F32)
+                    total[k, own] += jnp.dot(columns[4 * p + at], potentials[i][j, source, b], preferred_element_type=F32)
             return carry
 
         lax.fori_loop(lax.div(facts[5, t], 4), lax.div(facts[5, t + 1], 4), one, 0)
@@ -384,7 +353,7 @@
         c.wait()
 
 
-def project(potentials, facts, columns, meta, before, rank, nown, group):
+def project(potentials, facts, columns, meta, before, rank, nown):
     emasks = tuple((chunk, tuple(m)) for chunk, _, m in potentials)
     nchunk = 1 + max(chunk for chunk, _, _ in potentials)
     nv, _, _, width = potentials[0][1].shape[1:]
@@ -397,16 +366,14 @@
     total = (nk, nown, blk, width)
     arrays = [(a.shape, 2) for _, a, _ in potentials]
     return pl.pallas_call(
-        functools.partial(project_kernel, (nchunk, emasks, rank, group, nown, int(again))),
+        functools.partial(project_kernel, (nchunk, emasks, rank, nown, int(again))),
         out_shape=jax.ShapeDtypeStruct((nv, nown * blk * 2, width // 2), F32),
-        in_specs=[SMEM] * 2 + [ANY] + [VMEM] * ne + [ANY] * int(again),
+        in_specs=[SMEM] * 2 + [VMEM] * (1 + ne) + [ANY] * int(again),
         out_specs=ANY,
         input_output_aliases={3 + ne: 0} if again else {},
         scratch_shapes=[
-            pltpu.VMEM(columns.shape, BF16),
             pltpu.VMEM(staged, F32),
             pltpu.VMEM(total, F32),
-            pltpu.SemaphoreType.DMA((columns.shape[0] // group,)),
             pltpu.SemaphoreType.DMA((nk,)),
         ],
         compiler_params=params((columns.shape, 2), (staged, 4), (total, 4), *arrays),
@@ -492,15 +459,17 @@
 
     for bit in part_bits:
         panels = panels + [(swap(a, "grid", bit), (over, m ^ bit)) for a, (over, m) in panels]
-    columns = gather(far, facts, blk, group, 2 * rank)
     parts = potential(panels, near, occ, kern, ids, fmasks, meta, nlocal, rank)
-    early, late = [], []
+    stages = [[], [], []]
     for chunk in range(2):
         pieces = across(parts[chunk][None], high_bits[::-1] if chunk else high_bits)
-        early += [(chunk, a, m) for a, m in within(pieces[:-1], low_bits)]
-        late += [(chunk, a, m) for a, m in within(pieces[-1:], low_bits)]
-    total = project(early, facts, columns, meta, None, rank, nown, group)
-    total = project(late, facts, columns, meta, total, rank, nown, group)
+        for stage, some in enumerate((pieces[:1], pieces[1:-1], pieces[-1:])):
+            stages[stage] += [(chunk, a, m) for a, m in within(some, low_bits)]
+    columns = gather(far, facts, blk, 2 * rank)
+    total = None
+    for some in stages:
+        if some:
+            total = project(some, facts, columns, meta, total, rank, nown)
     return total.reshape(nv, nown * blk, 2, nocc)
 
 

time: 243 us -> 223 us (0.918)
  the two profiles are of different devices: /device:TPU:0 before, /device:TPU:1 now
where the time goes in v4:
time: 223 us
  waiting for transfers between devices  114 us (51%)
  starting transfers between devices  53 us (24%)
  Pallas kernels  52.3 us (23%)
    ppermute x48, waiting for transfers between devices, swap(): return lax.ppermute(array, axis, [(i, i ^ bit) for i in range(size)])  114 us
    ppermute x48, starting transfers between devices, swap(): return lax.ppermute(array, axis, [(i, i ^ bit) for i in range(size)])  53 us
    pallas_call x3, Pallas kernels, project(): pl.pallas_call(functools.partial(project_kernel, (nchunk, emasks, rank, n...  24 us
    pallas_call x2, Pallas kernels, pack(): pl.pallas_call(pack_kernel, out_shape=(jax.ShapeDtypeStruct((nb, blk, 2 *...  10.3 us
    pallas_call x1, Pallas kernels, potential(): pl.pallas_call(functools.partial(potential_kernel, sizes), out_shape=(jax...  5.9 us
    pallas_call x1, Pallas kernels, pair_list(): pl.pallas_call(functools.partial(list_kernel, sizes), out_shape=jax.Shape...  4.83 us
  transfers between devices with their start and end apart: 48, of which 12 were waited for; matrix products, arithmetic and copies ran while one was open for 1% of the time, Pallas kernels for 17%

profile of v4, /device:TPU:1, one launch (start us, length us, event | category | flops | bytes accessed | tf_op | source)
XLA Modules:
  0.0 223.0 jit_solution(2130874297202504713)
XLA Ops:
  0.1 3.3 %pack.2 = bf16[12,128,256]{2,1,0:T(8,128)(2,1)S(1)} custom-call(s32[2]{0:T(128)S(1)} %pad_add_fusion.where, bf16[3072,16,2,128]{3,2,1,0:T(2,128)(2,1)} %trial.3), custom_call_target="tpu_custom_call" | custom-call | tf_op jit(solution)/shard_map/pack/pallas_call | solution.py:67
  4.3 3.3 %occupied.1 = (f32[2,128,256]{2,1,0:T(8,128)S(1)}, bf16[2,128,256]{2,1,0:T(8,128)(2,1)S(1)}) custom-call(s32[4,12]{1,0:T(4,128)S(1)} %copy-done.5, s32[6]{0:T(128)S(1)} %stack.61.meta, bf16[3072,2,128]{2,1,0:T(2,128)(2,1)S(1)} %copy-done.1, bf16[4,128,1536]{2,1,0:T(8,128)(2,1)S(1)} %copy-done), custom_call_target="tpu_custom_call" | custom-call | tf_op jit(solution)/shard_map/occupied/pallas_call | solution.py:114
  9.8 3.2 %collective-permute-done.28 = bf16[2,128,256]{2,1,0:T(8,128)(2,1)S(1)} collective-permute-done((bf16[2,128,256]{2,1,0:T(8,128)(2,1)S(1)}, bf16[2,128,256]{2,1,0:T(8,128)(2,1)S(1)}, u32[]{:S(2)}, u32[]{:S(2)}) %collective-permute-start.28) | collective-permute-done | bytes 131104 | tf_op jit(solution)/shard_map/ppermute | solution.py:386
  13.0 2.3 %collective-permute-start.29 = (bf16[2,128,256]{2,1,0:T(8,128)(2,1)S(1)}, bf16[2,128,256]{2,1,0:T(8,128)(2,1)S(1)}, u32[]{:S(2)}, u32[]{:S(2)}) collective-permute-start(bf16[2,128,256]{2,1,0:T(8,128)(2,1)S(1)} %fusion), channel_id=1, source_target_pairs={{0,2},{1,3},{2,0},{3,1},{4,6},{5,7},{6,4},{7,5},{8,10},{9,11},{10,... | collective-permute-start | bytes 393224 | tf_op jit(solution)/shard_map/ppermute | solution.py:386
  15.3 6.0 %collective-permute-done.29 = bf16[2,128,256]{2,1,0:T(8,128)(2,1)S(1)} collective-permute-done((bf16[2,128,256]{2,1,0:T(8,128)(2,1)S(1)}, bf16[2,128,256]{2,1,0:T(8,128)(2,1)S(1)}, u32[]{:S(2)}, u32[]{:S(2)}) %collective-permute-start.29) | collective-permute-done | bytes 131104 | tf_op jit(solution)/shard_map/ppermute | solution.py:386
  22.0 3.2 %collective-permute-done.30 = bf16[2,128,256]{2,1,0:T(8,128)(2,1)S(1)} collective-permute-done((bf16[2,128,256]{2,1,0:T(8,128)(2,1)S(1)}, bf16[2,128,256]{2,1,0:T(8,128)(2,1)S(1)}, u32[]{:S(2)}, u32[]{:S(2)}) %collective-permute-start.30) | collective-permute-done | bytes 131104 | tf_op jit(solution)/shard_map/ppermute | solution.py:386
  25.8 7.1 %pack.3 = (bf16[12,128,256]{2,1,0:T(8,128)(2,1)S(1)}, bf16[12,128,256]{2,1,0:T(8,128)(2,1)S(1)}, bf16[12,128,256]{2,1,0:T(8,128)(2,1)}) custom-call(s32[4]{0:T(128)S(1)} %pad_add_fusion.1.where, bf16[3072,16,2,128]{3,2,1,0:T(2,128)(2,1)} %trial.3), custom_call_target="tpu_custom_call" | custom-call | tf_op jit(solution)/shard_map/pack/pallas_call | solution.py:67
  32.8 3.6 %collective-permute-start.22 = (bf16[12,128,256]{2,1,0:T(8,128)(2,1)S(1)}, bf16[12,128,256]{2,1,0:T(8,128)(2,1)S(1)}, u32[]{:S(2)}, u32[]{:S(2)}) collective-permute-start(bf16[12,128,256]{2,1,0:T(8,128)(2,1)S(1)} %get-tuple-element.19), channel_id=1, source_target_pairs={{0,2},{1,3},{2,0},{3,1},{4,6},{5,7},{6,4},{7,5},{8,10},{9,11},{10,... | collective-permute-start | bytes 2359304 | tf_op jit(solution)/shard_map/ppermute | solution.py:386
  38.0 2.8 %collective-permute-start.3 = (f32[1,4,5,128]{3,1,0,2:T(4,128)S(1)}, f32[1,4,5,128]{3,1,0,2:T(4,128)S(1)}, u32[]{:S(2)}, u32[]{:S(2)}) collective-permute-start(f32[1,4,5,128]{3,1,0,2:T(4,128)S(1)} %maximum_bitcast_fusion.1), channel_id=1, source_target_pairs={{0,4},{4,0},{8,12},{12,8},{16,20},{20,16},{24,28},{28,24},{1,5},{5... | collective-permute-start | bytes 30728 | tf_op jit(solution)/shard_map/ppermute | solution.py:386
  41.0 2.9 %collective-permute-start.4 = (f32[1,4,5,128]{3,1,0,2:T(4,128)S(1)}, f32[1,4,5,128]{3,1,0,2:T(4,128)S(1)}, u32[]{:S(2)}, u32[]{:S(2)}) collective-permute-start(f32[1,4,5,128]{3,1,0,2:T(4,128)S(1)} %collective-permute-done), channel_id=1, source_target_pairs={{0,4},{4,0},{8,12},{12,8},{16,20},{20,16},{24,28},{28,24},{1,5},{5... | collective-permute-start | bytes 30728 | tf_op jit(solution)/shard_map/ppermute | solution.py:386
  49.4 6.0 %collective-permute-done.32.refs_18_ = bf16[1,2,2,128,256]{4,3,2,1,0:T(8,128)(2,1)S(1)} collective-permute-done((bf16[1,2,2,128,256]{4,3,2,1,0:T(8,128)(2,1)S(1)}, bf16[1,2,2,128,256]{4,3,2,1,0:T(8,128)(2,1)S(1)}, u32[]{:S(2)}, u32[]{:S(2)}) %collective-permute-start.32) | collective-permute-done | bytes 262176 | tf_op jit(solution)/shard_map/ppermute | solution.py:386
  56.6 15.0 %collective-permute-done.22.refs_1_ = bf16[12,128,256]{2,1,0:T(8,128)(2,1)S(1)} collective-permute-done((bf16[12,128,256]{2,1,0:T(8,128)(2,1)S(1)}, bf16[12,128,256]{2,1,0:T(8,128)(2,1)S(1)}, u32[]{:S(2)}, u32[]{:S(2)}) %collective-permute-start.22) | collective-permute-done | bytes 786464 | tf_op jit(solution)/shard_map/ppermute | solution.py:386
  71.9 26.4 %collective-permute-done.23.refs_2_ = bf16[12,128,256]{2,1,0:T(8,128)(2,1)S(1)} collective-permute-done((bf16[12,128,256]{2,1,0:T(8,128)(2,1)S(1)}, bf16[12,128,256]{2,1,0:T(8,128)(2,1)S(1)}, u32[]{:S(2)}, u32[]{:S(2)}) %collective-permute-start.23) | collective-permute-done | bytes 786464 | tf_op jit(solution)/shard_map/ppermute | solution.py:386
  101.6 15.1 %collective-permute-done.15.refs_10_.refs_14_ = bf16[1,2,128,1536]{3,2,1,0:T(8,128)(2,1)S(1)} collective-permute-done((bf16[1,2,128,1536]{3,2,1,0:T(8,128)(2,1)S(1)}, bf16[1,2,128,1536]{3,2,1,0:T(8,128)(2,1)S(1)}, u32[]{:S(2)}, u32[]{:S(2)}) %collective-permute-start.15) | collective-permute-done | bytes 786464 | tf_op jit(solution)/shard_map/ppermute | solution.py:386
  127.9 11.3 %collective-permute-done.16.refs_11_.refs_15_ = bf16[1,2,128,1536]{3,2,1,0:T(8,128)(2,1)S(1)} collective-permute-done((bf16[1,2,128,1536]{3,2,1,0:T(8,128)(2,1)S(1)}, bf16[1,2,128,1536]{3,2,1,0:T(8,128)(2,1)S(1)}, u32[]{:S(2)}, u32[]{:S(2)}) %collective-permute-start.16) | collective-permute-done | bytes 786464 | tf_op jit(solution)/shard_map/ppermute | solution.py:386
  142.3 5.9 %potential.1 = (bf16[4,2,128,256]{3,2,1,0:T(8,128)(2,1)S(1)}, bf16[4,2,128,256]{3,2,1,0:T(8,128)(2,1)S(1)}) custom-call(s32[8,4,12]{2,1,0:T(4,128)S(1)} %fusion.1.ids, s32[6]{0:T(128)S(1)} %stack.61.meta, bf16[12,128,256]{2,1,0:T(8,128)(2,1)S(1)} %collective-permute-done.21.refs_0_, bf16[12,128,256]{2,1,0:T(8,128)(2,1)S(1)} %collective-permute-done.22.refs_1_, ...), custom_call_target="tpu_custom_call" | custom-call | tf_op jit(solution)/shard_map/potential/pallas_call | solution.py:197
  152.9 9.2 %collective-permute-done.34.refs_0_ = bf16[1,4,2,128,256]{4,3,2,1,0:T(8,128)(2,1)S(1)} collective-permute-done((bf16[1,4,2,128,256]{4,3,2,1,0:T(8,128)(2,1)S(1)}, bf16[1,4,2,128,256]{4,3,2,1,0:T(8,128)(2,1)S(1)}, u32[]{:S(2)}, u32[]{:S(2)}) %collective-permute-start.34) | collective-permute-done | bytes 524320 | tf_op jit(solution)/shard_map/ppermute | solution.py:386
  165.2 9.2 %collective-permute-done.37.refs_4_ = bf16[1,4,2,128,256]{4,3,2,1,0:T(8,128)(2,1)S(1)} collective-permute-done((bf16[1,4,2,128,256]{4,3,2,1,0:T(8,128)(2,1)S(1)}, bf16[1,4,2,128,256]{4,3,2,1,0:T(8,128)(2,1)S(1)}, u32[]{:S(2)}, u32[]{:S(2)}) %collective-permute-start.37) | collective-permute-done | bytes 524320 | tf_op jit(solution)/shard_map/ppermute | solution.py:386
  178.2 8.5 %collective-permute-done.35.refs_0_ = bf16[1,4,2,128,256]{4,3,2,1,0:T(8,128)(2,1)S(1)} collective-permute-done((bf16[1,4,2,128,256]{4,3,2,1,0:T(8,128)(2,1)S(1)}, bf16[1,4,2,128,256]{4,3,2,1,0:T(8,128)(2,1)S(1)}, u32[]{:S(2)}, u32[]{:S(2)}) %collective-permute-start.35) | collective-permute-done | bytes 524320 | tf_op jit(solution)/shard_map/ppermute | solution.py:386
  189.9 4.8 %pairs.1.facts = s32[8,432]{1,0:T(8,128)S(1)} custom-call(s32[8,4,12]{2,1,0:T(4,128)S(1)} %fusion.1.ids, s32[6]{0:T(128)S(1)} %stack.61.meta), custom_call_target="tpu_custom_call" | custom-call | tf_op jit(solution)/shard_map/pairs/pallas_call | solution.py:267
  194.8 4.1 %gather.1.columns = bf16[432,128,128]{2,1,0:T(8,128)(2,1)S(1)} custom-call(s32[8,432]{1,0:T(8,128)S(1)} %pairs.1.facts, bf16[1,2,128,1536]{3,2,1,0:T(8,128)(2,1)S(1)} %get-tuple-element.28.refs_0_.refs_8_, bf16[1,2,128,1536]{3,2,1,0:T(8,128)(2,1)S(1)} %collective-permute-done.7.refs_1_.refs_9_, ...), custom_call_target="tpu_custom_call" | custom-call | tf_op jit(solution)/shard_map/gather/pallas_call | solution.py:308
  198.8 7.4 %project.3.refs_8_ = f32[4,3072,128]{2,1,0:T(8,128)} custom-call(s32[8,432]{1,0:T(8,128)S(1)} %pairs.1.facts, s32[6]{0:T(128)S(1)} %stack.61.meta, bf16[432,128,128]{2,1,0:T(8,128)(2,1)S(1)} %gather.1.columns, bf16[1,4,2,128,256]{4,3,2,1,0:T(8,128)(2,1)S(1)} %bitcast.36, bf16[1,4,2,128,256]{4,3,2,1,0:T(8,128)(2,1)S(1)} %collective-permute-done.46.refs_1_, ...), custom_call_target="tpu_custom_call" | custom-call | tf_op jit(solution)/shard_map/project/pallas_call | solution.py:368
  206.3 9.2 %project.4.refs_4_ = f32[4,3072,128]{2,1,0:T(8,128)} custom-call(s32[8,432]{1,0:T(8,128)S(1)} %pairs.1.facts, s32[6]{0:T(128)S(1)} %stack.61.meta, bf16[432,128,128]{2,1,0:T(8,128)(2,1)S(1)} %gather.1.columns, bf16[1,4,2,128,256]{4,3,2,1,0:T(8,128)(2,1)S(1)} %collective-permute-done.34.refs_0_, ...), custom_call_target="tpu_custom_call", output_to_operand_aliasing={{}: (11, {})} | custom-call | tf_op jit(solution)/shard_map/project/pallas_call | solution.py:368
  215.5 7.4 %project.5 = f32[4,3072,128]{2,1,0:T(8,128)} custom-call(s32[8,432]{1,0:T(8,128)S(1)} %pairs.1.facts, s32[6]{0:T(128)S(1)} %stack.61.meta, bf16[432,128,128]{2,1,0:T(8,128)(2,1)S(1)} %gather.1.columns, bf16[1,4,2,128,256]{4,3,2,1,0:T(8,128)(2,1)S(1)} %collective-permute-done.35.refs_0_, ...), custom_call_target="tpu_custom_call", output_to_operand_aliasing={{}: (7, {})} | custom-call | tf_op jit(solution)/shard_map/project/pallas_call | solution.py:368
  (121 shorter events, 45.6 us)
Async XLA Ops:
  25.3 22.8 %collective-permute-start.31 = (bf16[1,2,2,128,256]{4,3,2,1,0:T(8,128)(2,1)S(1)}, bf16[1,2,2,128,256]{4,3,2,1,0:T(8,128)(2,1)S(1)}, u32[]{:S(2)}, u32[]{:S(2)}) collective-permute-start(bf16[1,2,2,128,256]{4,3,2,1,0:T(8,128)(2,1)S(1)} %maximum_bitcast_fusion.refs_16_), channel_id=1, source_target_pairs={{0,8},{4,12},{8,0},{12,4},{16,24},{20,28},{24,16},{28,20},{1,9},{5... | collective-permute-start | bytes 786440 | tf_op jit(solution)/shard_map/ppermute | solution.py:386
  32.8 38.8 %collective-permute-start.22 = (bf16[12,128,256]{2,1,0:T(8,128)(2,1)S(1)}, bf16[12,128,256]{2,1,0:T(8,128)(2,1)S(1)}, u32[]{:S(2)}, u32[]{:S(2)}) collective-permute-start(bf16[12,128,256]{2,1,0:T(8,128)(2,1)S(1)} %get-tuple-element.19), channel_id=1, source_target_pairs={{0,2},{1,3},{2,0},{3,1},{4,6},{5,7},{6,4},{7,5},{8,10},{9,11},{10,... | collective-permute-start | bytes 2359304 | tf_op jit(solution)/shard_map/ppermute | solution.py:386
  46.1 52.2 %collective-permute-start.23 = (bf16[12,128,256]{2,1,0:T(8,128)(2,1)S(1)}, bf16[12,128,256]{2,1,0:T(8,128)(2,1)S(1)}, u32[]{:S(2)}, u32[]{:S(2)}) collective-permute-start(bf16[12,128,256]{2,1,0:T(8,128)(2,1)S(1)} %get-tuple-element.20), channel_id=1, source_target_pairs={{0,1},{1,0},{2,3},{3,2},{4,5},{5,4},{6,7},{7,6},{8,9},{9,8},{10,11... | collective-permute-start | bytes 2359304 | tf_op jit(solution)/shard_map/ppermute | solution.py:386
  47.7 50.9 %collective-permute-start.27 = (bf16[12,128,256]{2,1,0:T(8,128)(2,1)}, bf16[12,128,256]{2,1,0:T(8,128)(2,1)S(1)}, u32[]{:S(2)}, u32[]{:S(2)}) collective-permute-start(bf16[12,128,256]{2,1,0:T(8,128)(2,1)} %get-tuple-element.21.refs_3_), channel_id=1, source_target_pairs={{0,4},{4,0},{8,12},{12,8},{16,20},{20,16},{24,28},{28,24},{1,5},{5... | collective-permute-start | bytes 2359304 | tf_op jit(solution)/shard_map/ppermute | solution.py:386
  48.0 51.8 %collective-permute-start.21 = (bf16[12,128,256]{2,1,0:T(8,128)(2,1)S(1)}, bf16[12,128,256]{2,1,0:T(8,128)(2,1)S(1)}, u32[]{:S(2)}, u32[]{:S(2)}) collective-permute-start(bf16[12,128,256]{2,1,0:T(8,128)(2,1)S(1)} %copy-done.4), channel_id=1, source_target_pairs={{0,3},{1,2},{2,1},{3,0},{4,7},{5,6},{6,5},{7,4},{8,11},{9,10},{10,... | collective-permute-start | bytes 2359304 | tf_op jit(solution)/shard_map/ppermute | solution.py:386
  55.4 45.7 %collective-permute-start.14 = (bf16[1,2,128,1536]{3,2,1,0:T(8,128)(2,1)S(1)}, bf16[1,2,128,1536]{3,2,1,0:T(8,128)(2,1)S(1)}, u32[]{:S(2)}, u32[]{:S(2)}) collective-permute-start(bf16[1,2,128,1536]{3,2,1,0:T(8,128)(2,1)S(1)} %get-tuple-element.27.refs_8_.refs_12_), channel_id=1, source_target_pairs={{0,16},{4,20},{8,24},{12,28},{16,0},{20,4},{24,8},{28,12},{1,17},{... | collective-permute-start | bytes 2359304 | tf_op jit(solution)/shard_map/ppermute | solution.py:386
  71.6 29.6 %collective-permute-start.7 = (bf16[1,2,128,1536]{3,2,1,0:T(8,128)(2,1)S(1)}, bf16[1,2,128,1536]{3,2,1,0:T(8,128)(2,1)S(1)}, u32[]{:S(2)}, u32[]{:S(2)}) collective-permute-start(bf16[1,2,128,1536]{3,2,1,0:T(8,128)(2,1)S(1)} %get-tuple-element.28.refs_0_.refs_8_), channel_id=1, source_target_pairs={{0,8},{4,12},{8,0},{12,4},{16,24},{20,28},{24,16},{28,20},{1,9},{5... | collective-permute-start | bytes 2359304 | tf_op jit(solution)/shard_map/ppermute | solution.py:386
  98.3 18.4 %collective-permute-start.15 = (bf16[1,2,128,1536]{3,2,1,0:T(8,128)(2,1)S(1)}, bf16[1,2,128,1536]{3,2,1,0:T(8,128)(2,1)S(1)}, u32[]{:S(2)}, u32[]{:S(2)}) collective-permute-start(bf16[1,2,128,1536]{3,2,1,0:T(8,128)(2,1)S(1)} %get-tuple-element.27.refs_8_.refs_12_), channel_id=1, source_target_pairs={{0,8},{4,12},{8,0},{12,4},{16,24},{20,28},{24,16},{28,20},{1,9},{5... | collective-permute-start | bytes 2359304 | tf_op jit(solution)/shard_map/ppermute | solution.py:386
  98.6 19.7 %collective-permute-start.8 = (bf16[1,2,128,1536]{3,2,1,0:T(8,128)(2,1)S(1)}, bf16[1,2,128,1536]{3,2,1,0:T(8,128)(2,1)S(1)}, u32[]{:S(2)}, u32[]{:S(2)}) collective-permute-start(bf16[1,2,128,1536]{3,2,1,0:T(8,128)(2,1)S(1)} %get-tuple-element.28.refs_0_.refs_8_), channel_id=1, source_target_pairs={{0,16},{4,20},{8,24},{12,28},{16,0},{20,4},{24,8},{28,12},{1,17},{... | collective-permute-start | bytes 2359304 | tf_op jit(solution)/shard_map/ppermute | solution.py:386
  99.8 20.2 %collective-permute-start.10 = (bf16[1,2,128,1536]{3,2,1,0:T(8,128)(2,1)S(1)}, bf16[1,2,128,1536]{3,2,1,0:T(8,128)(2,1)S(1)}, u32[]{:S(2)}, u32[]{:S(2)}) collective-permute-start(bf16[1,2,128,1536]{3,2,1,0:T(8,128)(2,1)S(1)} %get-tuple-element.28.refs_0_.refs_8_), channel_id=1, source_target_pairs={{0,4},{4,0},{8,12},{12,8},{16,20},{20,16},{24,28},{28,24},{1,5},{5... | collective-permute-start | bytes 2359304 | tf_op jit(solution)/shard_map/ppermute | solution.py:386
  101.1 23.6 %collective-permute-start.25 = (bf16[12,128,256]{2,1,0:T(8,128)(2,1)S(1)}, bf16[12,128,256]{2,1,0:T(8,128)(2,1)S(1)}, u32[]{:S(2)}, u32[]{:S(2)}) collective-permute-start(bf16[12,128,256]{2,1,0:T(8,128)(2,1)S(1)} %collective-permute-done.22.refs_1_), channel_id=1, source_target_pairs={{0,4},{4,0},{8,12},{12,8},{16,20},{20,16},{24,28},{28,24},{1,5},{5... | collective-permute-start | bytes 2359304 | tf_op jit(solution)/shard_map/ppermute | solution.py:386
  101.2 21.0 %collective-permute-start.33 = (bf16[1,2,2,128,256]{4,3,2,1,0:T(8,128)(2,1)S(1)}, bf16[1,2,2,128,256]{4,3,2,1,0:T(8,128)(2,1)S(1)}, u32[]{:S(2)}, u32[]{:S(2)}) collective-permute-start(bf16[1,2,2,128,256]{4,3,2,1,0:T(8,128)(2,1)S(1)} %collective-permute-done.31.refs_17_), channel_id=1, source_target_pairs={{0,16},{4,20},{8,24},{12,28},{16,0},{20,4},{24,8},{28,12},{1,17},{... | collective-permute-start | bytes 786440 | tf_op jit(solution)/shard_map/ppermute | solution.py:386
  120.0 19.2 %collective-permute-start.16 = (bf16[1,2,128,1536]{3,2,1,0:T(8,128)(2,1)S(1)}, bf16[1,2,128,1536]{3,2,1,0:T(8,128)(2,1)S(1)}, u32[]{:S(2)}, u32[]{:S(2)}) collective-permute-start(bf16[1,2,128,1536]{3,2,1,0:T(8,128)(2,1)S(1)} %collective-permute-done.14.refs_9_.refs_13_), channel_id=1, source_target_pairs={{0,8},{4,12},{8,0},{12,4},{16,24},{20,28},{24,16},{28,20},{1,9},{5... | collective-permute-start | bytes 2359304 | tf_op jit(solution)/shard_map/ppermute | solution.py:386
  124.8 23.4 %collective-permute-start.17 = (bf16[1,2,128,1536]{3,2,1,0:T(8,128)(2,1)S(1)}, bf16[1,2,128,1536]{3,2,1,0:T(8,128)(2,1)S(1)}, u32[]{:S(2)}, u32[]{:S(2)}) collective-permute-start(bf16[1,2,128,1536]{3,2,1,0:T(8,128)(2,1)S(1)} %get-tuple-element.27.refs_8_.refs_12_), channel_id=1, source_target_pairs={{0,4},{4,0},{8,12},{12,8},{16,20},{20,16},{24,28},{28,24},{1,5},{5... | collective-permute-start | bytes 2359304 | tf_op jit(solution)/shard_map/ppermute | solution.py:386
  127.3 21.0 %collective-permute-start.11 = (bf16[1,2,128,1536]{3,2,1,0:T(8,128)(2,1)S(1)}, bf16[1,2,128,1536]{3,2,1,0:T(8,128)(2,1)S(1)}, u32[]{:S(2)}, u32[]{:S(2)}) collective-permute-start(bf16[1,2,128,1536]{3,2,1,0:T(8,128)(2,1)S(1)} %collective-permute-done.7.refs_1_.refs_9_), channel_id=1, source_target_pairs={{0,4},{4,0},{8,12},{12,8},{16,20},{20,16},{24,28},{28,24},{1,5},{5... | collective-permute-start | bytes 2359304 | tf_op jit(solution)/shard_map/ppermute | solution.py:386
  127.4 21.4 %collective-permute-start.18 = (bf16[1,2,128,1536]{3,2,1,0:T(8,128)(2,1)S(1)}, bf16[1,2,128,1536]{3,2,1,0:T(8,128)(2,1)S(1)}, u32[]{:S(2)}, u32[]{:S(2)}) collective-permute-start(bf16[1,2,128,1536]{3,2,1,0:T(8,128)(2,1)S(1)} %collective-permute-done.14.refs_9_.refs_13_), channel_id=1, source_target_pairs={{0,4},{4,0},{8,12},{12,8},{16,20},{20,16},{24,28},{28,24},{1,5},{5... | collective-permute-start | bytes 2359304 | tf_op jit(solution)/shard_map/ppermute | solution.py:386
  151.2 23.1 %collective-permute-start.37 = (bf16[1,4,2,128,256]{4,3,2,1,0:T(8,128)(2,1)S(1)}, bf16[1,4,2,128,256]{4,3,2,1,0:T(8,128)(2,1)S(1)}, u32[]{:S(2)}, u32[]{:S(2)}) collective-permute-start(bf16[1,4,2,128,256]{4,3,2,1,0:T(8,128)(2,1)S(1)} %bitcast.38), channel_id=1, source_target_pairs={{0,16},{4,20},{8,24},{12,28},{16,0},{20,4},{24,8},{28,12},{1,17},{... | collective-permute-start | bytes 1572872 | tf_op jit(solution)/shard_map/ppermute | solution.py:386
  151.5 24.1 %collective-permute-start.43 = (bf16[1,4,2,128,256]{4,3,2,1,0:T(8,128)(2,1)S(1)}, bf16[1,4,2,128,256]{4,3,2,1,0:T(8,128)(2,1)S(1)}, u32[]{:S(2)}, u32[]{:S(2)}) collective-permute-start(bf16[1,4,2,128,256]{4,3,2,1,0:T(8,128)(2,1)S(1)} %bitcast.39), channel_id=1, source_target_pairs={{0,8},{4,12},{8,0},{12,4},{16,24},{20,28},{24,16},{28,20},{1,9},{5... | collective-permute-start | bytes 1572872 | tf_op jit(solution)/shard_map/ppermute | solution.py:386
  151.7 24.1 %collective-permute-start.13 = (bf16[1,2,128,1536]{3,2,1,0:T(8,128)(2,1)S(1)}, bf16[1,2,128,1536]{3,2,1,0:T(8,128)(2,1)S(1)}, u32[]{:S(2)}, u32[]{:S(2)}) collective-permute-start(bf16[1,2,128,1536]{3,2,1,0:T(8,128)(2,1)S(1)} %collective-permute-done.9.refs_3_.refs_11_), channel_id=1, source_target_pairs={{0,4},{4,0},{8,12},{12,8},{16,20},{20,16},{24,28},{28,24},{1,5},{5... | collective-permute-start | bytes 2359304 | tf_op jit(solution)/shard_map/ppermute | solution.py:386
  175.8 30.4 %collective-permute-start.44 = (bf16[1,4,2,128,256]{4,3,2,1,0:T(8,128)(2,1)S(1)}, bf16[1,4,2,128,256]{4,3,2,1,0:T(8,128)(2,1)S(1)}, u32[]{:S(2)}, u32[]{:S(2)}) collective-permute-start(bf16[1,4,2,128,256]{4,3,2,1,0:T(8,128)(2,1)S(1)} %collective-permute-done.37.refs_4_), channel_id=1, source_target_pairs={{0,4},{4,0},{8,12},{12,8},{16,20},{20,16},{24,28},{28,24},{1,5},{5... | collective-permute-start | bytes 1572872 | tf_op jit(solution)/shard_map/ppermute | solution.py:386
  177.6 28.6 %collective-permute-start.42 = (bf16[1,4,2,128,256]{4,3,2,1,0:T(8,128)(2,1)S(1)}, bf16[1,4,2,128,256]{4,3,2,1,0:T(8,128)(2,1)S(1)}, u32[]{:S(2)}, u32[]{:S(2)}) collective-permute-start(bf16[1,4,2,128,256]{4,3,2,1,0:T(8,128)(2,1)S(1)} %collective-permute-done.40.refs_1_), channel_id=1, source_target_pairs={{0,4},{4,0},{8,12},{12,8},{16,20},{20,16},{24,28},{28,24},{1,5},{5... | collective-permute-start | bytes 1572872 | tf_op jit(solution)/shard_map/ppermute | solution.py:386
  177.7 28.5 %collective-permute-start.45 = (bf16[1,4,2,128,256]{4,3,2,1,0:T(8,128)(2,1)S(1)}, bf16[1,4,2,128,256]{4,3,2,1,0:T(8,128)(2,1)S(1)}, u32[]{:S(2)}, u32[]{:S(2)}) collective-permute-start(bf16[1,4,2,128,256]{4,3,2,1,0:T(8,128)(2,1)S(1)} %collective-permute-done.43.refs_5_), channel_id=1, source_target_pairs={{0,4},{4,0},{8,12},{12,8},{16,20},{20,16},{24,28},{28,24},{1,5},{5... | collective-permute-start | bytes 1572872 | tf_op jit(solution)/shard_map/ppermute | solution.py:386
  186.6 28.9 %collective-permute-start.36 = (bf16[1,4,2,128,256]{4,3,2,1,0:T(8,128)(2,1)S(1)}, bf16[1,4,2,128,256]{4,3,2,1,0:T(8,128)(2,1)S(1)}, u32[]{:S(2)}, u32[]{:S(2)}) collective-permute-start(bf16[1,4,2,128,256]{4,3,2,1,0:T(8,128)(2,1)S(1)} %collective-permute-done.35.refs_0_), channel_id=1, source_target_pairs={{0,4},{4,0},{8,12},{12,8},{16,20},{20,16},{24,28},{28,24},{1,5},{5... | collective-permute-start | bytes 1572872 | tf_op jit(solution)/shard_map/ppermute | solution.py:386
  188.7 26.8 %collective-permute-start.39 = (bf16[1,4,2,128,256]{4,3,2,1,0:T(8,128)(2,1)S(1)}, bf16[1,4,2,128,256]{4,3,2,1,0:T(8,128)(2,1)S(1)}, u32[]{:S(2)}, u32[]{:S(2)}) collective-permute-start(bf16[1,4,2,128,256]{4,3,2,1,0:T(8,128)(2,1)S(1)} %collective-permute-done.38.refs_2_), channel_id=1, source_target_pairs={{0,4},{4,0},{8,12},{12,8},{16,20},{20,16},{24,28},{28,24},{1,5},{5... | collective-permute-start | bytes 1572872 | tf_op jit(solution)/shard_map/ppermute | solution.py:386
  (32 other events, 355.3 us)

commit v5 on v4

--- a/solution.py
+++ b/solution.py
@@ -79,12 +79,15 @@
     batches, sig = ids.shape
     blk, nocc = occupied.shape[0] // (table.shape[0] - 1), occupied.shape[2]
     nlocal = table.shape[0] - 1
-    pick = selectors(blk)
-    for j in range(nlocal):
-        both = occupied[j * blk : (j + 1) * blk].reshape(2 * blk, nocc)
-        for c in range(2):
-            split = jnp.dot(pick[c], both, preferred_element_type=F32)
-            table[j, :, c * nocc : (c + 1) * nocc] = split.astype(BF16)
+    pick = jnp.concatenate(selectors(blk), axis=0)
+    for j in range(0, nlocal, 2):
+        ahead = range(j, min(j + 2, nlocal))
+        both = jnp.concatenate([occupied[k * blk : (k + 1) * blk].reshape(2 * blk, nocc) for k in ahead], axis=1)
+        split = jnp.dot(pick, both, preferred_element_type=F32).astype(BF16)
+        for k in ahead:
+            for c in range(2):
+                piece = split[c * blk : (c + 1) * blk, (k - j) * nocc : (k - j + 1) * nocc]
+                table[k, :, c * nocc : (c + 1) * nocc] = piece
     table[nlocal] = jnp.zeros(table.shape[1:], BF16)
 
     def block(b, s):

time: 223 us -> 223 us (level)
  no operation moved by 1% of the time
where the time goes in v5:
time: 223 us
  waiting for transfers between devices  114 us (51%)
  starting transfers between devices  53 us (24%)
  Pallas kernels  52.2 us (23%)
    ppermute x48, waiting for transfers between devices, swap(): return lax.ppermute(array, axis, [(i, i ^ bit) for i in range(size)])  114 us
    ppermute x48, starting transfers between devices, swap(): return lax.ppermute(array, axis, [(i, i ^ bit) for i in range(size)])  53 us
    pallas_call x3, Pallas kernels, project(): pl.pallas_call(functools.partial(project_kernel, (nchunk, emasks, rank, n...  24 us
    pallas_call x2, Pallas kernels, pack(): pl.pallas_call(pack_kernel, out_shape=(jax.ShapeDtypeStruct((nb, blk, 2 *...  10.3 us
    pallas_call x1, Pallas kernels, potential(): pl.pallas_call(functools.partial(potential_kernel, sizes), out_shape=(jax...  5.9 us
    pallas_call x1, Pallas kernels, pair_list(): pl.pallas_call(functools.partial(list_kernel, sizes), out_shape=jax.Shape...  4.83 us
  transfers between devices with their start and end apart: 48, of which 12 were waited for; matrix products, arithmetic and copies ran while one was open for 1% of the time, Pallas kernels for 17%

profile of v5, /device:TPU:1, one launch (start us, length us, event | category | flops | bytes accessed | tf_op | source)
XLA Modules:
  0.0 222.9 jit_solution(17465659591398175390)
XLA Ops:
  0.1 3.3 %pack.2 = bf16[12,128,256]{2,1,0:T(8,128)(2,1)S(1)} custom-call(s32[2]{0:T(128)S(1)} %pad_add_fusion.where, bf16[3072,16,2,128]{3,2,1,0:T(2,128)(2,1)} %trial.3), custom_call_target="tpu_custom_call" | custom-call | tf_op jit(solution)/shard_map/pack/pallas_call | solution.py:67
  4.3 3.1 %occupied.1 = (f32[2,128,256]{2,1,0:T(8,128)S(1)}, bf16[2,128,256]{2,1,0:T(8,128)(2,1)S(1)}) custom-call(s32[4,12]{1,0:T(4,128)S(1)} %copy-done.5, s32[6]{0:T(128)S(1)} %stack.61.meta, bf16[3072,2,128]{2,1,0:T(2,128)(2,1)S(1)} %copy-done.1, bf16[4,128,1536]{2,1,0:T(8,128)(2,1)S(1)} %copy-done), custom_call_target="tpu_custom_call" | custom-call | tf_op jit(solution)/shard_map/occupied/pallas_call | solution.py:117
  9.7 3.2 %collective-permute-done.28 = bf16[2,128,256]{2,1,0:T(8,128)(2,1)S(1)} collective-permute-done((bf16[2,128,256]{2,1,0:T(8,128)(2,1)S(1)}, bf16[2,128,256]{2,1,0:T(8,128)(2,1)S(1)}, u32[]{:S(2)}, u32[]{:S(2)}) %collective-permute-start.28) | collective-permute-done | bytes 131104 | tf_op jit(solution)/shard_map/ppermute | solution.py:389
  12.9 2.3 %collective-permute-start.29 = (bf16[2,128,256]{2,1,0:T(8,128)(2,1)S(1)}, bf16[2,128,256]{2,1,0:T(8,128)(2,1)S(1)}, u32[]{:S(2)}, u32[]{:S(2)}) collective-permute-start(bf16[2,128,256]{2,1,0:T(8,128)(2,1)S(1)} %fusion), channel_id=1, source_target_pairs={{0,2},{1,3},{2,0},{3,1},{4,6},{5,7},{6,4},{7,5},{8,10},{9,11},{10,... | collective-permute-start | bytes 393224 | tf_op jit(solution)/shard_map/ppermute | solution.py:389
  15.2 6.0 %collective-permute-done.29 = bf16[2,128,256]{2,1,0:T(8,128)(2,1)S(1)} collective-permute-done((bf16[2,128,256]{2,1,0:T(8,128)(2,1)S(1)}, bf16[2,128,256]{2,1,0:T(8,128)(2,1)S(1)}, u32[]{:S(2)}, u32[]{:S(2)}) %collective-permute-start.29) | collective-permute-done | bytes 131104 | tf_op jit(solution)/shard_map/ppermute | solution.py:389
  21.9 3.2 %collective-permute-done.30 = bf16[2,128,256]{2,1,0:T(8,128)(2,1)S(1)} collective-permute-done((bf16[2,128,256]{2,1,0:T(8,128)(2,1)S(1)}, bf16[2,128,256]{2,1,0:T(8,128)(2,1)S(1)}, u32[]{:S(2)}, u32[]{:S(2)}) %collective-permute-start.30) | collective-permute-done | bytes 131104 | tf_op jit(solution)/shard_map/ppermute | solution.py:389
  25.7 7.1 %pack.3 = (bf16[12,128,256]{2,1,0:T(8,128)(2,1)S(1)}, bf16[12,128,256]{2,1,0:T(8,128)(2,1)S(1)}, bf16[12,128,256]{2,1,0:T(8,128)(2,1)}) custom-call(s32[4]{0:T(128)S(1)} %pad_add_fusion.1.where, bf16[3072,16,2,128]{3,2,1,0:T(2,128)(2,1)} %trial.3), custom_call_target="tpu_custom_call" | custom-call | tf_op jit(solution)/shard_map/pack/pallas_call | solution.py:67
  32.7 3.6 %collective-permute-start.22 = (bf16[12,128,256]{2,1,0:T(8,128)(2,1)S(1)}, bf16[12,128,256]{2,1,0:T(8,128)(2,1)S(1)}, u32[]{:S(2)}, u32[]{:S(2)}) collective-permute-start(bf16[12,128,256]{2,1,0:T(8,128)(2,1)S(1)} %get-tuple-element.19), channel_id=1, source_target_pairs={{0,2},{1,3},{2,0},{3,1},{4,6},{5,7},{6,4},{7,5},{8,10},{9,11},{10,... | collective-permute-start | bytes 2359304 | tf_op jit(solution)/shard_map/ppermute | solution.py:389
  37.9 2.8 %collective-permute-start.3 = (f32[1,4,5,128]{3,1,0,2:T(4,128)S(1)}, f32[1,4,5,128]{3,1,0,2:T(4,128)S(1)}, u32[]{:S(2)}, u32[]{:S(2)}) collective-permute-start(f32[1,4,5,128]{3,1,0,2:T(4,128)S(1)} %maximum_bitcast_fusion.1), channel_id=1, source_target_pairs={{0,4},{4,0},{8,12},{12,8},{16,20},{20,16},{24,28},{28,24},{1,5},{5... | collective-permute-start | bytes 30728 | tf_op jit(solution)/shard_map/ppermute | solution.py:389
  40.9 2.9 %collective-permute-start.4 = (f32[1,4,5,128]{3,1,0,2:T(4,128)S(1)}, f32[1,4,5,128]{3,1,0,2:T(4,128)S(1)}, u32[]{:S(2)}, u32[]{:S(2)}) collective-permute-start(f32[1,4,5,128]{3,1,0,2:T(4,128)S(1)} %collective-permute-done), channel_id=1, source_target_pairs={{0,4},{4,0},{8,12},{12,8},{16,20},{20,16},{24,28},{28,24},{1,5},{5... | collective-permute-start | bytes 30728 | tf_op jit(solution)/shard_map/ppermute | solution.py:389
  49.3 6.0 %collective-permute-done.32.refs_18_ = bf16[1,2,2,128,256]{4,3,2,1,0:T(8,128)(2,1)S(1)} collective-permute-done((bf16[1,2,2,128,256]{4,3,2,1,0:T(8,128)(2,1)S(1)}, bf16[1,2,2,128,256]{4,3,2,1,0:T(8,128)(2,1)S(1)}, u32[]{:S(2)}, u32[]{:S(2)}) %collective-permute-start.32) | collective-permute-done | bytes 262176 | tf_op jit(solution)/shard_map/ppermute | solution.py:389
  56.5 15.0 %collective-permute-done.22.refs_1_ = bf16[12,128,256]{2,1,0:T(8,128)(2,1)S(1)} collective-permute-done((bf16[12,128,256]{2,1,0:T(8,128)(2,1)S(1)}, bf16[12,128,256]{2,1,0:T(8,128)(2,1)S(1)}, u32[]{:S(2)}, u32[]{:S(2)}) %collective-permute-start.22) | collective-permute-done | bytes 786464 | tf_op jit(solution)/shard_map/ppermute | solution.py:389
  71.8 26.4 %collective-permute-done.23.refs_2_ = bf16[12,128,256]{2,1,0:T(8,128)(2,1)S(1)} collective-permute-done((bf16[12,128,256]{2,1,0:T(8,128)(2,1)S(1)}, bf16[12,128,256]{2,1,0:T(8,128)(2,1)S(1)}, u32[]{:S(2)}, u32[]{:S(2)}) %collective-permute-start.23) | collective-permute-done | bytes 786464 | tf_op jit(solution)/shard_map/ppermute | solution.py:389
  101.5 15.1 %collective-permute-done.15.refs_10_.refs_14_ = bf16[1,2,128,1536]{3,2,1,0:T(8,128)(2,1)S(1)} collective-permute-done((bf16[1,2,128,1536]{3,2,1,0:T(8,128)(2,1)S(1)}, bf16[1,2,128,1536]{3,2,1,0:T(8,128)(2,1)S(1)}, u32[]{:S(2)}, u32[]{:S(2)}) %collective-permute-start.15) | collective-permute-done | bytes 786464 | tf_op jit(solution)/shard_map/ppermute | solution.py:389
  127.8 11.3 %collective-permute-done.16.refs_11_.refs_15_ = bf16[1,2,128,1536]{3,2,1,0:T(8,128)(2,1)S(1)} collective-permute-done((bf16[1,2,128,1536]{3,2,1,0:T(8,128)(2,1)S(1)}, bf16[1,2,128,1536]{3,2,1,0:T(8,128)(2,1)S(1)}, u32[]{:S(2)}, u32[]{:S(2)}) %collective-permute-start.16) | collective-permute-done | bytes 786464 | tf_op jit(solution)/shard_map/ppermute | solution.py:389
  142.2 5.9 %potential.1 = (bf16[4,2,128,256]{3,2,1,0:T(8,128)(2,1)S(1)}, bf16[4,2,128,256]{3,2,1,0:T(8,128)(2,1)S(1)}) custom-call(s32[8,4,12]{2,1,0:T(4,128)S(1)} %fusion.1.ids, s32[6]{0:T(128)S(1)} %stack.61.meta, bf16[12,128,256]{2,1,0:T(8,128)(2,1)S(1)} %collective-permute-done.21.refs_0_, bf16[12,128,256]{2,1,0:T(8,128)(2,1)S(1)} %collective-permute-done.22.refs_1_, ...), custom_call_target="tpu_custom_call" | custom-call | tf_op jit(solution)/shard_map/potential/pallas_call | solution.py:200
  152.8 9.2 %collective-permute-done.34.refs_0_ = bf16[1,4,2,128,256]{4,3,2,1,0:T(8,128)(2,1)S(1)} collective-permute-done((bf16[1,4,2,128,256]{4,3,2,1,0:T(8,128)(2,1)S(1)}, bf16[1,4,2,128,256]{4,3,2,1,0:T(8,128)(2,1)S(1)}, u32[]{:S(2)}, u32[]{:S(2)}) %collective-permute-start.34) | collective-permute-done | bytes 524320 | tf_op jit(solution)/shard_map/ppermute | solution.py:389
  165.0 9.2 %collective-permute-done.37.refs_4_ = bf16[1,4,2,128,256]{4,3,2,1,0:T(8,128)(2,1)S(1)} collective-permute-done((bf16[1,4,2,128,256]{4,3,2,1,0:T(8,128)(2,1)S(1)}, bf16[1,4,2,128,256]{4,3,2,1,0:T(8,128)(2,1)S(1)}, u32[]{:S(2)}, u32[]{:S(2)}) %collective-permute-start.37) | collective-permute-done | bytes 524320 | tf_op jit(solution)/shard_map/ppermute | solution.py:389
  178.0 8.5 %collective-permute-done.35.refs_0_ = bf16[1,4,2,128,256]{4,3,2,1,0:T(8,128)(2,1)S(1)} collective-permute-done((bf16[1,4,2,128,256]{4,3,2,1,0:T(8,128)(2,1)S(1)}, bf16[1,4,2,128,256]{4,3,2,1,0:T(8,128)(2,1)S(1)}, u32[]{:S(2)}, u32[]{:S(2)}) %collective-permute-start.35) | collective-permute-done | bytes 524320 | tf_op jit(solution)/shard_map/ppermute | solution.py:389
  189.8 4.8 %pairs.1.facts = s32[8,432]{1,0:T(8,128)S(1)} custom-call(s32[8,4,12]{2,1,0:T(4,128)S(1)} %fusion.1.ids, s32[6]{0:T(128)S(1)} %stack.61.meta), custom_call_target="tpu_custom_call" | custom-call | tf_op jit(solution)/shard_map/pairs/pallas_call | solution.py:270
  194.7 4.1 %gather.1.columns = bf16[432,128,128]{2,1,0:T(8,128)(2,1)S(1)} custom-call(s32[8,432]{1,0:T(8,128)S(1)} %pairs.1.facts, bf16[1,2,128,1536]{3,2,1,0:T(8,128)(2,1)S(1)} %get-tuple-element.28.refs_0_.refs_8_, bf16[1,2,128,1536]{3,2,1,0:T(8,128)(2,1)S(1)} %collective-permute-done.7.refs_1_.refs_9_, ...), custom_call_target="tpu_custom_call" | custom-call | tf_op jit(solution)/shard_map/gather/pallas_call | solution.py:311
  198.7 7.4 %project.3.refs_8_ = f32[4,3072,128]{2,1,0:T(8,128)} custom-call(s32[8,432]{1,0:T(8,128)S(1)} %pairs.1.facts, s32[6]{0:T(128)S(1)} %stack.61.meta, bf16[432,128,128]{2,1,0:T(8,128)(2,1)S(1)} %gather.1.columns, bf16[1,4,2,128,256]{4,3,2,1,0:T(8,128)(2,1)S(1)} %bitcast.36, bf16[1,4,2,128,256]{4,3,2,1,0:T(8,128)(2,1)S(1)} %collective-permute-done.46.refs_1_, ...), custom_call_target="tpu_custom_call" | custom-call | tf_op jit(solution)/shard_map/project/pallas_call | solution.py:371
  206.1 9.2 %project.4.refs_4_ = f32[4,3072,128]{2,1,0:T(8,128)} custom-call(s32[8,432]{1,0:T(8,128)S(1)} %pairs.1.facts, s32[6]{0:T(128)S(1)} %stack.61.meta, bf16[432,128,128]{2,1,0:T(8,128)(2,1)S(1)} %gather.1.columns, bf16[1,4,2,128,256]{4,3,2,1,0:T(8,128)(2,1)S(1)} %collective-permute-done.34.refs_0_, ...), custom_call_target="tpu_custom_call", output_to_operand_aliasing={{}: (11, {})} | custom-call | tf_op jit(solution)/shard_map/project/pallas_call | solution.py:371
  215.4 7.4 %project.5 = f32[4,3072,128]{2,1,0:T(8,128)} custom-call(s32[8,432]{1,0:T(8,128)S(1)} %pairs.1.facts, s32[6]{0:T(128)S(1)} %stack.61.meta, bf16[432,128,128]{2,1,0:T(8,128)(2,1)S(1)} %gather.1.columns, bf16[1,4,2,128,256]{4,3,2,1,0:T(8,128)(2,1)S(1)} %collective-permute-done.35.refs_0_, ...), custom_call_target="tpu_custom_call", output_to_operand_aliasing={{}: (7, {})} | custom-call | tf_op jit(solution)/shard_map/project/pallas_call | solution.py:371
  (121 shorter events, 45.6 us)
Async XLA Ops:
  25.2 22.8 %collective-permute-start.31 = (bf16[1,2,2,128,256]{4,3,2,1,0:T(8,128)(2,1)S(1)}, bf16[1,2,2,128,256]{4,3,2,1,0:T(8,128)(2,1)S(1)}, u32[]{:S(2)}, u32[]{:S(2)}) collective-permute-start(bf16[1,2,2,128,256]{4,3,2,1,0:T(8,128)(2,1)S(1)} %maximum_bitcast_fusion.refs_16_), channel_id=1, source_target_pairs={{0,8},{4,12},{8,0},{12,4},{16,24},{20,28},{24,16},{28,20},{1,9},{5... | collective-permute-start | bytes 786440 | tf_op jit(solution)/shard_map/ppermute | solution.py:389
  32.7 38.8 %collective-permute-start.22 = (bf16[12,128,256]{2,1,0:T(8,128)(2,1)S(1)}, bf16[12,128,256]{2,1,0:T(8,128)(2,1)S(1)}, u32[]{:S(2)}, u32[]{:S(2)}) collective-permute-start(bf16[12,128,256]{2,1,0:T(8,128)(2,1)S(1)} %get-tuple-element.19), channel_id=1, source_target_pairs={{0,2},{1,3},{2,0},{3,1},{4,6},{5,7},{6,4},{7,5},{8,10},{9,11},{10,... | collective-permute-start | bytes 2359304 | tf_op jit(solution)/shard_map/ppermute | solution.py:389
  46.0 52.2 %collective-permute-start.23 = (bf16[12,128,256]{2,1,0:T(8,128)(2,1)S(1)}, bf16[12,128,256]{2,1,0:T(8,128)(2,1)S(1)}, u32[]{:S(2)}, u32[]{:S(2)}) collective-permute-start(bf16[12,128,256]{2,1,0:T(8,128)(2,1)S(1)} %get-tuple-element.20), channel_id=1, source_target_pairs={{0,1},{1,0},{2,3},{3,2},{4,5},{5,4},{6,7},{7,6},{8,9},{9,8},{10,11... | collective-permute-start | bytes 2359304 | tf_op jit(solution)/shard_map/ppermute | solution.py:389
  47.6 50.9 %collective-permute-start.27 = (bf16[12,128,256]{2,1,0:T(8,128)(2,1)}, bf16[12,128,256]{2,1,0:T(8,128)(2,1)S(1)}, u32[]{:S(2)}, u32[]{:S(2)}) collective-permute-start(bf16[12,128,256]{2,1,0:T(8,128)(2,1)} %get-tuple-element.21.refs_3_), channel_id=1, source_target_pairs={{0,4},{4,0},{8,12},{12,8},{16,20},{20,16},{24,28},{28,24},{1,5},{5... | collective-permute-start | bytes 2359304 | tf_op jit(solution)/shard_map/ppermute | solution.py:389
  47.9 51.8 %collective-permute-start.21 = (bf16[12,128,256]{2,1,0:T(8,128)(2,1)S(1)}, bf16[12,128,256]{2,1,0:T(8,128)(2,1)S(1)}, u32[]{:S(2)}, u32[]{:S(2)}) collective-permute-start(bf16[12,128,256]{2,1,0:T(8,128)(2,1)S(1)} %copy-done.4), channel_id=1, source_target_pairs={{0,3},{1,2},{2,1},{3,0},{4,7},{5,6},{6,5},{7,4},{8,11},{9,10},{10,... | collective-permute-start | bytes 2359304 | tf_op jit(solution)/shard_map/ppermute | solution.py:389
  55.3 45.7 %collective-permute-start.14 = (bf16[1,2,128,1536]{3,2,1,0:T(8,128)(2,1)S(1)}, bf16[1,2,128,1536]{3,2,1,0:T(8,128)(2,1)S(1)}, u32[]{:S(2)}, u32[]{:S(2)}) collective-permute-start(bf16[1,2,128,1536]{3,2,1,0:T(8,128)(2,1)S(1)} %get-tuple-element.27.refs_8_.refs_12_), channel_id=1, source_target_pairs={{0,16},{4,20},{8,24},{12,28},{16,0},{20,4},{24,8},{28,12},{1,17},{... | collective-permute-start | bytes 2359304 | tf_op jit(solution)/shard_map/ppermute | solution.py:389
  71.5 29.6 %collective-permute-start.7 = (bf16[1,2,128,1536]{3,2,1,0:T(8,128)(2,1)S(1)}, bf16[1,2,128,1536]{3,2,1,0:T(8,128)(2,1)S(1)}, u32[]{:S(2)}, u32[]{:S(2)}) collective-permute-start(bf16[1,2,128,1536]{3,2,1,0:T(8,128)(2,1)S(1)} %get-tuple-element.28.refs_0_.refs_8_), channel_id=1, source_target_pairs={{0,8},{4,12},{8,0},{12,4},{16,24},{20,28},{24,16},{28,20},{1,9},{5... | collective-permute-start | bytes 2359304 | tf_op jit(solution)/shard_map/ppermute | solution.py:389
  98.2 18.4 %collective-permute-start.15 = (bf16[1,2,128,1536]{3,2,1,0:T(8,128)(2,1)S(1)}, bf16[1,2,128,1536]{3,2,1,0:T(8,128)(2,1)S(1)}, u32[]{:S(2)}, u32[]{:S(2)}) collective-permute-start(bf16[1,2,128,1536]{3,2,1,0:T(8,128)(2,1)S(1)} %get-tuple-element.27.refs_8_.refs_12_), channel_id=1, source_target_pairs={{0,8},{4,12},{8,0},{12,4},{16,24},{20,28},{24,16},{28,20},{1,9},{5... | collective-permute-start | bytes 2359304 | tf_op jit(solution)/shard_map/ppermute | solution.py:389
  98.5 19.7 %collective-permute-start.8 = (bf16[1,2,128,1536]{3,2,1,0:T(8,128)(2,1)S(1)}, bf16[1,2,128,1536]{3,2,1,0:T(8,128)(2,1)S(1)}, u32[]{:S(2)}, u32[]{:S(2)}) collective-permute-start(bf16[1,2,128,1536]{3,2,1,0:T(8,128)(2,1)S(1)} %get-tuple-element.28.refs_0_.refs_8_), channel_id=1, source_target_pairs={{0,16},{4,20},{8,24},{12,28},{16,0},{20,4},{24,8},{28,12},{1,17},{... | collective-permute-start | bytes 2359304 | tf_op jit(solution)/shard_map/ppermute | solution.py:389
  99.7 20.2 %collective-permute-start.10 = (bf16[1,2,128,1536]{3,2,1,0:T(8,128)(2,1)S(1)}, bf16[1,2,128,1536]{3,2,1,0:T(8,128)(2,1)S(1)}, u32[]{:S(2)}, u32[]{:S(2)}) collective-permute-start(bf16[1,2,128,1536]{3,2,1,0:T(8,128)(2,1)S(1)} %get-tuple-element.28.refs_0_.refs_8_), channel_id=1, source_target_pairs={{0,4},{4,0},{8,12},{12,8},{16,20},{20,16},{24,28},{28,24},{1,5},{5... | collective-permute-start | bytes 2359304 | tf_op jit(solution)/shard_map/ppermute | solution.py:389
  101.0 23.6 %collective-permute-start.25 = (bf16[12,128,256]{2,1,0:T(8,128)(2,1)S(1)}, bf16[12,128,256]{2,1,0:T(8,128)(2,1)S(1)}, u32[]{:S(2)}, u32[]{:S(2)}) collective-permute-start(bf16[12,128,256]{2,1,0:T(8,128)(2,1)S(1)} %collective-permute-done.22.refs_1_), channel_id=1, source_target_pairs={{0,4},{4,0},{8,12},{12,8},{16,20},{20,16},{24,28},{28,24},{1,5},{5... | collective-permute-start | bytes 2359304 | tf_op jit(solution)/shard_map/ppermute | solution.py:389
  101.1 21.1 %collective-permute-start.33 = (bf16[1,2,2,128,256]{4,3,2,1,0:T(8,128)(2,1)S(1)}, bf16[1,2,2,128,256]{4,3,2,1,0:T(8,128)(2,1)S(1)}, u32[]{:S(2)}, u32[]{:S(2)}) collective-permute-start(bf16[1,2,2,128,256]{4,3,2,1,0:T(8,128)(2,1)S(1)} %collective-permute-done.31.refs_17_), channel_id=1, source_target_pairs={{0,16},{4,20},{8,24},{12,28},{16,0},{20,4},{24,8},{28,12},{1,17},{... | collective-permute-start | bytes 786440 | tf_op jit(solution)/shard_map/ppermute | solution.py:389
  119.9 19.2 %collective-permute-start.16 = (bf16[1,2,128,1536]{3,2,1,0:T(8,128)(2,1)S(1)}, bf16[1,2,128,1536]{3,2,1,0:T(8,128)(2,1)S(1)}, u32[]{:S(2)}, u32[]{:S(2)}) collective-permute-start(bf16[1,2,128,1536]{3,2,1,0:T(8,128)(2,1)S(1)} %collective-permute-done.14.refs_9_.refs_13_), channel_id=1, source_target_pairs={{0,8},{4,12},{8,0},{12,4},{16,24},{20,28},{24,16},{28,20},{1,9},{5... | collective-permute-start | bytes 2359304 | tf_op jit(solution)/shard_map/ppermute | solution.py:389
  124.7 23.4 %collective-permute-start.17 = (bf16[1,2,128,1536]{3,2,1,0:T(8,128)(2,1)S(1)}, bf16[1,2,128,1536]{3,2,1,0:T(8,128)(2,1)S(1)}, u32[]{:S(2)}, u32[]{:S(2)}) collective-permute-start(bf16[1,2,128,1536]{3,2,1,0:T(8,128)(2,1)S(1)} %get-tuple-element.27.refs_8_.refs_12_), channel_id=1, source_target_pairs={{0,4},{4,0},{8,12},{12,8},{16,20},{20,16},{24,28},{28,24},{1,5},{5... | collective-permute-start | bytes 2359304 | tf_op jit(solution)/shard_map/ppermute | solution.py:389
  127.2 21.0 %collective-permute-start.11 = (bf16[1,2,128,1536]{3,2,1,0:T(8,128)(2,1)S(1)}, bf16[1,2,128,1536]{3,2,1,0:T(8,128)(2,1)S(1)}, u32[]{:S(2)}, u32[]{:S(2)}) collective-permute-start(bf16[1,2,128,1536]{3,2,1,0:T(8,128)(2,1)S(1)} %collective-permute-done.7.refs_1_.refs_9_), channel_id=1, source_target_pairs={{0,4},{4,0},{8,12},{12,8},{16,20},{20,16},{24,28},{28,24},{1,5},{5... | collective-permute-start | bytes 2359304 | tf_op jit(solution)/shard_map/ppermute | solution.py:389
  127.3 21.4 %collective-permute-start.18 = (bf16[1,2,128,1536]{3,2,1,0:T(8,128)(2,1)S(1)}, bf16[1,2,128,1536]{3,2,1,0:T(8,128)(2,1)S(1)}, u32[]{:S(2)}, u32[]{:S(2)}) collective-permute-start(bf16[1,2,128,1536]{3,2,1,0:T(8,128)(2,1)S(1)} %collective-permute-done.14.refs_9_.refs_13_), channel_id=1, source_target_pairs={{0,4},{4,0},{8,12},{12,8},{16,20},{20,16},{24,28},{28,24},{1,5},{5... | collective-permute-start | bytes 2359304 | tf_op jit(solution)/shard_map/ppermute | solution.py:389
  151.1 23.1 %collective-permute-start.37 = (bf16[1,4,2,128,256]{4,3,2,1,0:T(8,128)(2,1)S(1)}, bf16[1,4,2,128,256]{4,3,2,1,0:T(8,128)(2,1)S(1)}, u32[]{:S(2)}, u32[]{:S(2)}) collective-permute-start(bf16[1,4,2,128,256]{4,3,2,1,0:T(8,128)(2,1)S(1)} %bitcast.38), channel_id=1, source_target_pairs={{0,16},{4,20},{8,24},{12,28},{16,0},{20,4},{24,8},{28,12},{1,17},{... | collective-permute-start | bytes 1572872 | tf_op jit(solution)/shard_map/ppermute | solution.py:389
  151.4 24.1 %collective-permute-start.43 = (bf16[1,4,2,128,256]{4,3,2,1,0:T(8,128)(2,1)S(1)}, bf16[1,4,2,128,256]{4,3,2,1,0:T(8,128)(2,1)S(1)}, u32[]{:S(2)}, u32[]{:S(2)}) collective-permute-start(bf16[1,4,2,128,256]{4,3,2,1,0:T(8,128)(2,1)S(1)} %bitcast.39), channel_id=1, source_target_pairs={{0,8},{4,12},{8,0},{12,4},{16,24},{20,28},{24,16},{28,20},{1,9},{5... | collective-permute-start | bytes 1572872 | tf_op jit(solution)/shard_map/ppermute | solution.py:389
  151.6 24.1 %collective-permute-start.13 = (bf16[1,2,128,1536]{3,2,1,0:T(8,128)(2,1)S(1)}, bf16[1,2,128,1536]{3,2,1,0:T(8,128)(2,1)S(1)}, u32[]{:S(2)}, u32[]{:S(2)}) collective-permute-start(bf16[1,2,128,1536]{3,2,1,0:T(8,128)(2,1)S(1)} %collective-permute-done.9.refs_3_.refs_11_), channel_id=1, source_target_pairs={{0,4},{4,0},{8,12},{12,8},{16,20},{20,16},{24,28},{28,24},{1,5},{5... | collective-permute-start | bytes 2359304 | tf_op jit(solution)/shard_map/ppermute | solution.py:389
  175.7 30.4 %collective-permute-start.44 = (bf16[1,4,2,128,256]{4,3,2,1,0:T(8,128)(2,1)S(1)}, bf16[1,4,2,128,256]{4,3,2,1,0:T(8,128)(2,1)S(1)}, u32[]{:S(2)}, u32[]{:S(2)}) collective-permute-start(bf16[1,4,2,128,256]{4,3,2,1,0:T(8,128)(2,1)S(1)} %collective-permute-done.37.refs_4_), channel_id=1, source_target_pairs={{0,4},{4,0},{8,12},{12,8},{16,20},{20,16},{24,28},{28,24},{1,5},{5... | collective-permute-start | bytes 1572872 | tf_op jit(solution)/shard_map/ppermute | solution.py:389
  177.5 28.6 %collective-permute-start.42 = (bf16[1,4,2,128,256]{4,3,2,1,0:T(8,128)(2,1)S(1)}, bf16[1,4,2,128,256]{4,3,2,1,0:T(8,128)(2,1)S(1)}, u32[]{:S(2)}, u32[]{:S(2)}) collective-permute-start(bf16[1,4,2,128,256]{4,3,2,1,0:T(8,128)(2,1)S(1)} %collective-permute-done.40.refs_1_), channel_id=1, source_target_pairs={{0,4},{4,0},{8,12},{12,8},{16,20},{20,16},{24,28},{28,24},{1,5},{5... | collective-permute-start | bytes 1572872 | tf_op jit(solution)/shard_map/ppermute | solution.py:389
  177.6 28.5 %collective-permute-start.45 = (bf16[1,4,2,128,256]{4,3,2,1,0:T(8,128)(2,1)S(1)}, bf16[1,4,2,128,256]{4,3,2,1,0:T(8,128)(2,1)S(1)}, u32[]{:S(2)}, u32[]{:S(2)}) collective-permute-start(bf16[1,4,2,128,256]{4,3,2,1,0:T(8,128)(2,1)S(1)} %collective-permute-done.43.refs_5_), channel_id=1, source_target_pairs={{0,4},{4,0},{8,12},{12,8},{16,20},{20,16},{24,28},{28,24},{1,5},{5... | collective-permute-start | bytes 1572872 | tf_op jit(solution)/shard_map/ppermute | solution.py:389
  186.5 28.9 %collective-permute-start.36 = (bf16[1,4,2,128,256]{4,3,2,1,0:T(8,128)(2,1)S(1)}, bf16[1,4,2,128,256]{4,3,2,1,0:T(8,128)(2,1)S(1)}, u32[]{:S(2)}, u32[]{:S(2)}) collective-permute-start(bf16[1,4,2,128,256]{4,3,2,1,0:T(8,128)(2,1)S(1)} %collective-permute-done.35.refs_0_), channel_id=1, source_target_pairs={{0,4},{4,0},{8,12},{12,8},{16,20},{20,16},{24,28},{28,24},{1,5},{5... | collective-permute-start | bytes 1572872 | tf_op jit(solution)/shard_map/ppermute | solution.py:389
  188.6 26.8 %collective-permute-start.39 = (bf16[1,4,2,128,256]{4,3,2,1,0:T(8,128)(2,1)S(1)}, bf16[1,4,2,128,256]{4,3,2,1,0:T(8,128)(2,1)S(1)}, u32[]{:S(2)}, u32[]{:S(2)}) collective-permute-start(bf16[1,4,2,128,256]{4,3,2,1,0:T(8,128)(2,1)S(1)} %collective-permute-done.38.refs_2_), channel_id=1, source_target_pairs={{0,4},{4,0},{8,12},{12,8},{16,20},{20,16},{24,28},{28,24},{1,5},{5... | collective-permute-start | bytes 1572872 | tf_op jit(solution)/shard_map/ppermute | solution.py:389
  (32 other events, 355.3 us)

commit v6 on v5

--- a/solution.py
+++ b/solution.py
@@ -133,13 +133,15 @@
     kern, refs = refs[0], refs[1:]
     outs, (table, x, left, m, tsems, xsems) = refs[:nchunk], refs[nchunk:]
     groups = len(values) // nchunk
-    nb, blk, width = panels[0].shape
+    blk, width = panels[0].shape[1:]
+    nb = nlocal // (1 + max(side for _, side, _ in tmasks))
     count, npts = x.shape[1], x.shape[2]
     sig = ids.shape[2]
     copies = []
-    for i, (over, side) in enumerate(tmasks):
-        at = (meta[3] ^ over) * nlocal + (meta[4] ^ side) * nb
-        copies.append(pltpu.make_async_copy(panels[i], table.at[pl.ds(at, nb)], tsems.at[i]))
+    for i, (over, side, off) in enumerate(tmasks):
+        at = (meta[3] ^ over) * nlocal + (meta[4] ^ side) * nb + off
+        size = panels[i].shape[0]
+        copies.append(pltpu.make_async_copy(panels[i], table.at[pl.ds(at, size)], tsems.at[i]))
     loads = []
     todo = []
     at = 0
@@ -190,10 +192,10 @@
     xmasks = tuple(tuple(m) for _, m in values)
     omasks = tuple(tuple(m) for _, m in occ)
     count, npts, span = values[0][0].shape[1:]
-    nb, blk, width = panels[0][0].shape
+    blk, width = panels[0][0].shape[1:]
     nsrc = sum(len(m) for m in xmasks)
     sizes = (tmasks, xmasks, omasks, tuple(fmasks), nlocal, rank, nchunk)
-    table = (len(panels) * nb, blk, width)
+    table = (sum(a.shape[0] for a, _ in panels), blk, width)
     x = (nsrc, count, npts, span)
     left = (nsrc * count, npts, width)
     m = (nsrc * count, npts, 2 * npts)
@@ -425,13 +427,16 @@
 
     panels = []
     far_first = list(reversed(range(n_ao)))
-    for planes in (far_first[:1], far_first[1:]):
-        where = jnp.stack([side * nb] + [(ao ^ over) * nv + vector for over in planes]).astype(jnp.int32)
-        rows = pack(trial, where, len(planes), nb, blk)
-        if not panels:
+    early = max(1, nb // 4)
+    jobs = [(far_first[:1], 0, early), (far_first[:1], early, nb - early), (far_first[1:], 0, nb)]
+    for i, (planes, off, size) in enumerate(jobs):
+        where = jnp.stack([side * nb + off] + [(ao ^ over) * nv + vector for over in planes]).astype(jnp.int32)
+        rows = pack(trial, where, len(planes), size, blk)
+        if i == 0:
             rows, coords, weights, occupied = lax.optimization_barrier((rows, coords, weights, occupied))
         for over, one in zip(planes, rows, strict=True):
-            panels.append((swap(one, "ao", over) if over else one, (over, 0)))
+            name = str(over) if i else "f"
+            panels.append((swap(one, "ao", over) if over else one, (over, 0, off), name))
 
     near = []
     for chunk in range(2):
@@ -461,7 +466,8 @@
     facts = pair_list(xmasks, ids, fmasks, meta, rank, nown, 2, count, group)
 
     for bit in part_bits:
-        panels = panels + [(swap(a, "grid", bit), (over, m ^ bit)) for a, (over, m) in panels]
+        panels = panels + [(swap(x, "grid", bit), (over, m ^ bit, off), name) for x, (over, m, off), name in panels]
+    panels = [(x, what) for x, what, _ in panels]
     parts = potential(panels, near, occ, kern, ids, fmasks, meta, nlocal, rank)
     stages = [[], [], []]
     for chunk in range(2):

time: 223 us -> 225 us (level)
  waiting for transfers between devices: 114 us -> 106 us
  starting transfers between devices: 53 us -> 58.4 us
  Pallas kernels: 52.2 us -> 54.6 us
    ppermute x48 -> x50, waiting for transfers between devices: 114 us -> 106 us  [swap(): return lax.ppermute(array, axis, [(i, i ^ bit) for i in range(size)])]
    ppermute x48 -> x50, starting transfers between devices: 53 us -> 58.4 us  [swap(): return lax.ppermute(array, axis, [(i, i ^ bit) for i in range(size)])]
    pallas_call x2 -> x3, Pallas kernels: 10.3 us -> 11.9 us  [pack(): pl.pallas_call(pack_kernel, out_shape=(jax.ShapeDtypeStruct((nb, blk, 2 *...]
  transfers between devices with their start and end apart: 48 -> 50, of which waited for: 12 -> 10; matrix products, arithmetic and copies ran while one was open for 1% -> 2% of each run, Pallas kernels for 17% -> 19%
where the time goes in v6:
time: 225 us
  waiting for transfers between devices  106 us (47%)
  starting transfers between devices  58.4 us (26%)
  Pallas kernels  54.6 us (24%)
  other arithmetic  3.38 us (2%)
    ppermute x50, waiting for transfers between devices, swap(): return lax.ppermute(array, axis, [(i, i ^ bit) for i in range(size)])  106 us
    ppermute x50, starting transfers between devices, swap(): return lax.ppermute(array, axis, [(i, i ^ bit) for i in range(size)])  58.4 us
    pallas_call x3, Pallas kernels, project(): pl.pallas_call(functools.partial(project_kernel, (nchunk, emasks, rank, n...  24 us
    pallas_call x3, Pallas kernels, pack(): pl.pallas_call(pack_kernel, out_shape=(jax.ShapeDtypeStruct((nb, blk, 2 *...  11.9 us
    pallas_call x1, Pallas kernels, potential(): pl.pallas_call(functools.partial(potential_kernel, sizes), out_shape=(jax...  6.7 us
    pallas_call x1, Pallas kernels, pair_list(): pl.pallas_call(functools.partial(list_kernel, sizes), out_shape=jax.Shape...  4.83 us
  transfers between devices with their start and end apart: 50, of which 10 were waited for; matrix products, arithmetic and copies ran while one was open for 2% of the time, Pallas kernels for 19%

profile of v6, /device:TPU:1, one launch (start us, length us, event | category | flops | bytes accessed | tf_op | source)
XLA Modules:
  0.0 224.9 jit_solution(18370788218799422228)
XLA Ops:
  3.0 3.1 %occupied.1 = (f32[2,128,256]{2,1,0:T(8,128)S(1)}, bf16[2,128,256]{2,1,0:T(8,128)(2,1)S(1)}) custom-call(s32[4,12]{1,0:T(4,128)S(1)} %copy-done.7, s32[6]{0:T(128)S(1)} %stack.68.meta, bf16[3072,2,128]{2,1,0:T(2,128)(2,1)S(1)} %copy-done.1, bf16[4,128,1536]{2,1,0:T(8,128)(2,1)S(1)} %copy-done), custom_call_target="tpu_custom_call" | custom-call | tf_op jit(solution)/shard_map/occupied/pallas_call | solution.py:117
  8.4 2.7 %pack.4 = bf16[9,128,256]{2,1,0:T(8,128)(2,1)S(1)} custom-call(s32[2]{0:T(128)S(1)} %get-tuple-element.30.where, bf16[3072,16,2,128]{3,2,1,0:T(2,128)(2,1)} %trial.5), custom_call_target="tpu_custom_call" | custom-call | tf_op jit(solution)/shard_map/pack/pallas_call | solution.py:67
  11.1 2.3 %collective-permute-start.22 = (bf16[9,128,256]{2,1,0:T(8,128)(2,1)S(1)}, bf16[9,128,256]{2,1,0:T(8,128)(2,1)S(1)}, u32[]{:S(2)}, u32[]{:S(2)}) collective-permute-start(bf16[9,128,256]{2,1,0:T(8,128)(2,1)S(1)} %pack.4), channel_id=1, source_target_pairs={{0,3},{1,2},{2,1},{3,0},{4,7},{5,6},{6,5},{7,4},{8,11},{9,10},{10,... | collective-permute-start | bytes 1769480 | tf_op jit(solution)/shard_map/ppermute | solution.py:391
  17.0 2.4 %collective-permute-start.3 = (f32[1,4,5,128]{3,1,0,2:T(4,128)S(1)}, f32[1,4,5,128]{3,1,0,2:T(4,128)S(1)}, u32[]{:S(2)}, u32[]{:S(2)}) collective-permute-start(f32[1,4,5,128]{3,1,0,2:T(4,128)S(1)} %maximum_bitcast_fusion.1), channel_id=1, source_target_pairs={{0,4},{4,0},{8,12},{12,8},{16,20},{20,16},{24,28},{28,24},{1,5},{5... | collective-permute-start | bytes 30728 | tf_op jit(solution)/shard_map/ppermute | solution.py:391
  21.1 27.8 %collective-permute-done.31 = bf16[2,128,256]{2,1,0:T(8,128)(2,1)} collective-permute-done((bf16[2,128,256]{2,1,0:T(8,128)(2,1)}, bf16[2,128,256]{2,1,0:T(8,128)(2,1)}, u32[]{:S(2)}, u32[]{:S(2)}) %collective-permute-start.31) | collective-permute-done | bytes 131104 | tf_op jit(solution)/shard_map/ppermute | solution.py:391
  51.1 2.8 %collective-permute-start.4 = (f32[1,4,5,128]{3,1,0,2:T(4,128)S(1)}, f32[1,4,5,128]{3,1,0,2:T(4,128)S(1)}, u32[]{:S(2)}, u32[]{:S(2)}) collective-permute-start(f32[1,4,5,128]{3,1,0,2:T(4,128)S(1)} %collective-permute-done), channel_id=1, source_target_pairs={{0,4},{4,0},{8,12},{12,8},{16,20},{20,16},{24,28},{28,24},{1,5},{5... | collective-permute-start | bytes 30728 | tf_op jit(solution)/shard_map/ppermute | solution.py:391
  54.8 7.0 %pack.5 = (bf16[12,128,256]{2,1,0:T(8,128)(2,1)S(1)}, bf16[12,128,256]{2,1,0:T(8,128)(2,1)S(1)}, bf16[12,128,256]{2,1,0:T(8,128)(2,1)}) custom-call(s32[4]{0:T(128)S(1)} %pad_add_fusion.2.where, bf16[3072,16,2,128]{3,2,1,0:T(2,128)(2,1)} %trial.5), custom_call_target="tpu_custom_call" | custom-call | tf_op jit(solution)/shard_map/pack/pallas_call | solution.py:67
  61.8 2.2 %collective-permute-start.23 = (bf16[12,128,256]{2,1,0:T(8,128)(2,1)S(1)}, bf16[12,128,256]{2,1,0:T(8,128)(2,1)S(1)}, u32[]{:S(2)}, u32[]{:S(2)}) collective-permute-start(bf16[12,128,256]{2,1,0:T(8,128)(2,1)S(1)} %get-tuple-element.19), channel_id=1, source_target_pairs={{0,2},{1,3},{2,0},{3,1},{4,6},{5,7},{6,4},{7,5},{8,10},{9,11},{10,... | collective-permute-start | bytes 2359304 | tf_op jit(solution)/shard_map/ppermute | solution.py:391
  69.1 5.1 %collective-permute-done.33.refs_19_ = bf16[1,2,2,128,256]{4,3,2,1,0:T(8,128)(2,1)S(1)} collective-permute-done((bf16[1,2,2,128,256]{4,3,2,1,0:T(8,128)(2,1)S(1)}, bf16[1,2,2,128,256]{4,3,2,1,0:T(8,128)(2,1)S(1)}, u32[]{:S(2)}, u32[]{:S(2)}) %collective-permute-start.33) | collective-permute-done | bytes 262176 | tf_op jit(solution)/shard_map/ppermute | solution.py:391
  76.7 21.6 %collective-permute-done.23.refs_2_ = bf16[12,128,256]{2,1,0:T(8,128)(2,1)S(1)} collective-permute-done((bf16[12,128,256]{2,1,0:T(8,128)(2,1)S(1)}, bf16[12,128,256]{2,1,0:T(8,128)(2,1)S(1)}, u32[]{:S(2)}, u32[]{:S(2)}) %collective-permute-start.23) | collective-permute-done | bytes 786464 | tf_op jit(solution)/shard_map/ppermute | solution.py:391
  103.2 12.9 %collective-permute-done.15.refs_10_.refs_16_ = bf16[1,2,128,1536]{3,2,1,0:T(8,128)(2,1)S(1)} collective-permute-done((bf16[1,2,128,1536]{3,2,1,0:T(8,128)(2,1)S(1)}, bf16[1,2,128,1536]{3,2,1,0:T(8,128)(2,1)S(1)}, u32[]{:S(2)}, u32[]{:S(2)}) %collective-permute-start.15) | collective-permute-done | bytes 786464 | tf_op jit(solution)/shard_map/ppermute | solution.py:391
  116.1 2.2 collective-permute-start.27
  118.3 3.3 %collective-permute-start.28 = (bf16[12,128,256]{2,1,0:T(8,128)(2,1)S(1)}, bf16[12,128,256]{2,1,0:T(8,128)(2,1)S(1)}, u32[]{:S(2)}, u32[]{:S(2)}) collective-permute-start(bf16[12,128,256]{2,1,0:T(8,128)(2,1)S(1)} %collective-permute-done.24.refs_3_), channel_id=1, source_target_pairs={{0,4},{4,0},{8,12},{12,8},{16,20},{20,16},{24,28},{28,24},{1,5},{5... | collective-permute-start | bytes 2359304 | tf_op jit(solution)/shard_map/ppermute | solution.py:391
  129.7 11.1 %collective-permute-done.16.refs_11_.refs_17_ = bf16[1,2,128,1536]{3,2,1,0:T(8,128)(2,1)S(1)} collective-permute-done((bf16[1,2,128,1536]{3,2,1,0:T(8,128)(2,1)S(1)}, bf16[1,2,128,1536]{3,2,1,0:T(8,128)(2,1)S(1)}, u32[]{:S(2)}, u32[]{:S(2)}) %collective-permute-start.16) | collective-permute-done | bytes 786464 | tf_op jit(solution)/shard_map/ppermute | solution.py:391
  141.7 2.4 %collective-permute-start.19 = (bf16[1,2,128,1536]{3,2,1,0:T(8,128)(2,1)S(1)}, bf16[1,2,128,1536]{3,2,1,0:T(8,128)(2,1)S(1)}, u32[]{:S(2)}, u32[]{:S(2)}) collective-permute-start(bf16[1,2,128,1536]{3,2,1,0:T(8,128)(2,1)S(1)} %collective-permute-done.15.refs_10_.refs_16_), channel_id=1, source_target_pairs={{0,4},{4,0},{8,12},{12,8},{16,20},{20,16},{24,28},{28,24},{1,5},{5... | collective-permute-start | bytes 2359304 | tf_op jit(solution)/shard_map/ppermute | solution.py:391
  144.0 6.7 %potential.1 = (bf16[4,2,128,256]{3,2,1,0:T(8,128)(2,1)S(1)}, bf16[4,2,128,256]{3,2,1,0:T(8,128)(2,1)S(1)}) custom-call(s32[8,4,12]{2,1,0:T(4,128)S(1)} %fusion.1.ids, s32[6]{0:T(128)S(1)} %stack.68.meta, bf16[3,128,256]{2,1,0:T(8,128)(2,1)S(1)} %collective-permute-done.21.refs_0_, bf16[9,128,256]{2,1,0:T(8,128)(2,1)S(1)} %collective-permute-done.22.refs_1_, ...), custom_call_target="tpu_custom_call" | custom-call | tf_op jit(solution)/shard_map/potential/pallas_call | solution.py:202
  156.3 8.4 %collective-permute-done.36.refs_0_ = bf16[1,4,2,128,256]{4,3,2,1,0:T(8,128)(2,1)S(1)} collective-permute-done((bf16[1,4,2,128,256]{4,3,2,1,0:T(8,128)(2,1)S(1)}, bf16[1,4,2,128,256]{4,3,2,1,0:T(8,128)(2,1)S(1)}, u32[]{:S(2)}, u32[]{:S(2)}) %collective-permute-start.36) | collective-permute-done | bytes 524320 | tf_op jit(solution)/shard_map/ppermute | solution.py:391
  166.8 9.2 %collective-permute-done.39.refs_4_ = bf16[1,4,2,128,256]{4,3,2,1,0:T(8,128)(2,1)S(1)} collective-permute-done((bf16[1,4,2,128,256]{4,3,2,1,0:T(8,128)(2,1)S(1)}, bf16[1,4,2,128,256]{4,3,2,1,0:T(8,128)(2,1)S(1)}, u32[]{:S(2)}, u32[]{:S(2)}) %collective-permute-start.39) | collective-permute-done | bytes 524320 | tf_op jit(solution)/shard_map/ppermute | solution.py:391
  180.9 7.3 %collective-permute-done.37.refs_0_ = bf16[1,4,2,128,256]{4,3,2,1,0:T(8,128)(2,1)S(1)} collective-permute-done((bf16[1,4,2,128,256]{4,3,2,1,0:T(8,128)(2,1)S(1)}, bf16[1,4,2,128,256]{4,3,2,1,0:T(8,128)(2,1)S(1)}, u32[]{:S(2)}, u32[]{:S(2)}) %collective-permute-start.37) | collective-permute-done | bytes 524320 | tf_op jit(solution)/shard_map/ppermute | solution.py:391
  191.8 4.8 %pairs.1.facts = s32[8,432]{1,0:T(8,128)S(1)} custom-call(s32[8,4,12]{2,1,0:T(4,128)S(1)} %fusion.1.ids, s32[6]{0:T(128)S(1)} %stack.68.meta), custom_call_target="tpu_custom_call" | custom-call | tf_op jit(solution)/shard_map/pairs/pallas_call | solution.py:272
  196.6 4.1 %gather.1.columns = bf16[432,128,128]{2,1,0:T(8,128)(2,1)S(1)} custom-call(s32[8,432]{1,0:T(8,128)S(1)} %pairs.1.facts, bf16[1,2,128,1536]{3,2,1,0:T(8,128)(2,1)S(1)} %get-tuple-element.28.refs_0_.refs_10_, bf16[1,2,128,1536]{3,2,1,0:T(8,128)(2,1)S(1)} %collective-permute-done.7.refs_1_.refs_11_, ...), custom_call_target="tpu_custom_call" | custom-call | tf_op jit(solution)/shard_map/gather/pallas_call | solution.py:313
  200.7 7.4 %project.3.refs_8_ = f32[4,3072,128]{2,1,0:T(8,128)} custom-call(s32[8,432]{1,0:T(8,128)S(1)} %pairs.1.facts, s32[6]{0:T(128)S(1)} %stack.68.meta, bf16[432,128,128]{2,1,0:T(8,128)(2,1)S(1)} %gather.1.columns, bf16[1,4,2,128,256]{4,3,2,1,0:T(8,128)(2,1)S(1)} %bitcast.37, bf16[1,4,2,128,256]{4,3,2,1,0:T(8,128)(2,1)S(1)} %collective-permute-done.48.refs_1_, ...), custom_call_target="tpu_custom_call" | custom-call | tf_op jit(solution)/shard_map/project/pallas_call | solution.py:373
  208.1 9.2 %project.4.refs_4_ = f32[4,3072,128]{2,1,0:T(8,128)} custom-call(s32[8,432]{1,0:T(8,128)S(1)} %pairs.1.facts, s32[6]{0:T(128)S(1)} %stack.68.meta, bf16[432,128,128]{2,1,0:T(8,128)(2,1)S(1)} %gather.1.columns, bf16[1,4,2,128,256]{4,3,2,1,0:T(8,128)(2,1)S(1)} %collective-permute-done.36.refs_0_, ...), custom_call_target="tpu_custom_call", output_to_operand_aliasing={{}: (11, {})} | custom-call | tf_op jit(solution)/shard_map/project/pallas_call | solution.py:373
  217.3 7.4 %project.5 = f32[4,3072,128]{2,1,0:T(8,128)} custom-call(s32[8,432]{1,0:T(8,128)S(1)} %pairs.1.facts, s32[6]{0:T(128)S(1)} %stack.68.meta, bf16[432,128,128]{2,1,0:T(8,128)(2,1)S(1)} %gather.1.columns, bf16[1,4,2,128,256]{4,3,2,1,0:T(8,128)(2,1)S(1)} %collective-permute-done.37.refs_0_, ...), custom_call_target="tpu_custom_call", output_to_operand_aliasing={{}: (7, {})} | custom-call | tf_op jit(solution)/shard_map/project/pallas_call | solution.py:373
  (130 shorter events, 51.0 us)
Async XLA Ops:
  11.1 56.7 %collective-permute-start.22 = (bf16[9,128,256]{2,1,0:T(8,128)(2,1)S(1)}, bf16[9,128,256]{2,1,0:T(8,128)(2,1)S(1)}, u32[]{:S(2)}, u32[]{:S(2)}) collective-permute-start(bf16[9,128,256]{2,1,0:T(8,128)(2,1)S(1)} %pack.4), channel_id=1, source_target_pairs={{0,3},{1,2},{2,1},{3,0},{4,7},{5,6},{6,5},{7,4},{8,11},{9,10},{10,... | collective-permute-start | bytes 1769480 | tf_op jit(solution)/shard_map/ppermute | solution.py:391
  14.0 34.9 %collective-permute-start.31 = (bf16[2,128,256]{2,1,0:T(8,128)(2,1)}, bf16[2,128,256]{2,1,0:T(8,128)(2,1)}, u32[]{:S(2)}, u32[]{:S(2)}) collective-permute-start(bf16[2,128,256]{2,1,0:T(8,128)(2,1)} %fusion), channel_id=1, source_target_pairs={{0,2},{1,3},{2,0},{3,1},{4,6},{5,7},{6,4},{7,5},{8,10},{9,11},{10,... | collective-permute-start | bytes 393224 | tf_op jit(solution)/shard_map/ppermute | solution.py:391
  15.7 35.3 %collective-permute-start.1 = (f32[1,4,5,128]{3,1,0,2:T(4,128)S(1)}, f32[1,4,5,128]{3,1,0,2:T(4,128)S(1)}, u32[]{:S(2)}, u32[]{:S(2)}) collective-permute-start(f32[1,4,5,128]{3,1,0,2:T(4,128)S(1)} %maximum_bitcast_fusion.1), channel_id=1, source_target_pairs={{0,16},{4,20},{8,24},{12,28},{16,0},{20,4},{24,8},{28,12},{1,17},{... | collective-permute-start | bytes 30728 | tf_op jit(solution)/shard_map/ppermute | solution.py:391
  17.0 36.9 %collective-permute-start.3 = (f32[1,4,5,128]{3,1,0,2:T(4,128)S(1)}, f32[1,4,5,128]{3,1,0,2:T(4,128)S(1)}, u32[]{:S(2)}, u32[]{:S(2)}) collective-permute-start(f32[1,4,5,128]{3,1,0,2:T(4,128)S(1)} %maximum_bitcast_fusion.1), channel_id=1, source_target_pairs={{0,4},{4,0},{8,12},{12,8},{16,20},{20,16},{24,28},{28,24},{1,5},{5... | collective-permute-start | bytes 30728 | tf_op jit(solution)/shard_map/ppermute | solution.py:391
  19.4 34.6 %collective-permute-start.21 = (bf16[3,128,256]{2,1,0:T(8,128)(2,1)S(1)}, bf16[3,128,256]{2,1,0:T(8,128)(2,1)S(1)}, u32[]{:S(2)}, u32[]{:S(2)}) collective-permute-start(bf16[3,128,256]{2,1,0:T(8,128)(2,1)S(1)} %copy-done.6), channel_id=1, source_target_pairs={{0,3},{1,2},{2,1},{3,0},{4,7},{5,6},{6,5},{7,4},{8,11},{9,10},{10,... | collective-permute-start | bytes 589832 | tf_op jit(solution)/shard_map/ppermute | solution.py:391
  61.8 36.5 %collective-permute-start.23 = (bf16[12,128,256]{2,1,0:T(8,128)(2,1)S(1)}, bf16[12,128,256]{2,1,0:T(8,128)(2,1)S(1)}, u32[]{:S(2)}, u32[]{:S(2)}) collective-permute-start(bf16[12,128,256]{2,1,0:T(8,128)(2,1)S(1)} %get-tuple-element.19), channel_id=1, source_target_pairs={{0,2},{1,3},{2,0},{3,1},{4,6},{5,7},{6,4},{7,5},{8,10},{9,11},{10,... | collective-permute-start | bytes 2359304 | tf_op jit(solution)/shard_map/ppermute | solution.py:391
  64.1 35.5 %collective-permute-start.24 = (bf16[12,128,256]{2,1,0:T(8,128)(2,1)S(1)}, bf16[12,128,256]{2,1,0:T(8,128)(2,1)S(1)}, u32[]{:S(2)}, u32[]{:S(2)}) collective-permute-start(bf16[12,128,256]{2,1,0:T(8,128)(2,1)S(1)} %get-tuple-element.20), channel_id=1, source_target_pairs={{0,1},{1,0},{2,3},{3,2},{4,5},{5,4},{6,7},{7,6},{8,9},{9,8},{10,11... | collective-permute-start | bytes 2359304 | tf_op jit(solution)/shard_map/ppermute | solution.py:391
  66.2 35.4 %collective-permute-start.29 = (bf16[12,128,256]{2,1,0:T(8,128)(2,1)}, bf16[12,128,256]{2,1,0:T(8,128)(2,1)S(1)}, u32[]{:S(2)}, u32[]{:S(2)}) collective-permute-start(bf16[12,128,256]{2,1,0:T(8,128)(2,1)} %get-tuple-element.21.refs_4_), channel_id=1, source_target_pairs={{0,4},{4,0},{8,12},{12,8},{16,20},{20,16},{24,28},{28,24},{1,5},{5... | collective-permute-start | bytes 2359304 | tf_op jit(solution)/shard_map/ppermute | solution.py:391
  74.3 28.5 %collective-permute-start.14 = (bf16[1,2,128,1536]{3,2,1,0:T(8,128)(2,1)S(1)}, bf16[1,2,128,1536]{3,2,1,0:T(8,128)(2,1)S(1)}, u32[]{:S(2)}, u32[]{:S(2)}) collective-permute-start(bf16[1,2,128,1536]{3,2,1,0:T(8,128)(2,1)S(1)} %get-tuple-element.27.refs_8_.refs_14_), channel_id=1, source_target_pairs={{0,16},{4,20},{8,24},{12,28},{16,0},{20,4},{24,8},{28,12},{1,17},{... | collective-permute-start | bytes 2359304 | tf_op jit(solution)/shard_map/ppermute | solution.py:391
  75.5 27.3 %collective-permute-start.7 = (bf16[1,2,128,1536]{3,2,1,0:T(8,128)(2,1)S(1)}, bf16[1,2,128,1536]{3,2,1,0:T(8,128)(2,1)S(1)}, u32[]{:S(2)}, u32[]{:S(2)}) collective-permute-start(bf16[1,2,128,1536]{3,2,1,0:T(8,128)(2,1)S(1)} %get-tuple-element.28.refs_0_.refs_10_), channel_id=1, source_target_pairs={{0,8},{4,12},{8,0},{12,4},{16,24},{20,28},{24,16},{28,20},{1,9},{5... | collective-permute-start | bytes 2359304 | tf_op jit(solution)/shard_map/ppermute | solution.py:391
  101.6 20.0 %collective-permute-start.10 = (bf16[1,2,128,1536]{3,2,1,0:T(8,128)(2,1)S(1)}, bf16[1,2,128,1536]{3,2,1,0:T(8,128)(2,1)S(1)}, u32[]{:S(2)}, u32[]{:S(2)}) collective-permute-start(bf16[1,2,128,1536]{3,2,1,0:T(8,128)(2,1)S(1)} %get-tuple-element.28.refs_0_.refs_10_), channel_id=1, source_target_pairs={{0,4},{4,0},{8,12},{12,8},{16,20},{20,16},{24,28},{28,24},{1,5},{5... | collective-permute-start | bytes 2359304 | tf_op jit(solution)/shard_map/ppermute | solution.py:391
  102.8 24.0 %collective-permute-start.26 = (bf16[9,128,256]{2,1,0:T(8,128)(2,1)S(1)}, bf16[9,128,256]{2,1,0:T(8,128)(2,1)S(1)}, u32[]{:S(2)}, u32[]{:S(2)}) collective-permute-start(bf16[9,128,256]{2,1,0:T(8,128)(2,1)S(1)} %collective-permute-done.22.refs_1_), channel_id=1, source_target_pairs={{0,4},{4,0},{8,12},{12,8},{16,20},{20,16},{24,28},{28,24},{1,5},{5... | collective-permute-start | bytes 1769480 | tf_op jit(solution)/shard_map/ppermute | solution.py:391
  102.8 21.0 %collective-permute-start.35 = (bf16[1,2,2,128,256]{4,3,2,1,0:T(8,128)(2,1)S(1)}, bf16[1,2,2,128,256]{4,3,2,1,0:T(8,128)(2,1)S(1)}, u32[]{:S(2)}, u32[]{:S(2)}) collective-permute-start(bf16[1,2,2,128,256]{4,3,2,1,0:T(8,128)(2,1)S(1)} %collective-permute-done.33.refs_19_), channel_id=1, source_target_pairs={{0,16},{4,20},{8,24},{12,28},{16,0},{20,4},{24,8},{28,12},{1,17},{... | collective-permute-start | bytes 786440 | tf_op jit(solution)/shard_map/ppermute | solution.py:391
  126.8 24.0 %collective-permute-start.17 = (bf16[1,2,128,1536]{3,2,1,0:T(8,128)(2,1)S(1)}, bf16[1,2,128,1536]{3,2,1,0:T(8,128)(2,1)S(1)}, u32[]{:S(2)}, u32[]{:S(2)}) collective-permute-start(bf16[1,2,128,1536]{3,2,1,0:T(8,128)(2,1)S(1)} %get-tuple-element.27.refs_8_.refs_14_), channel_id=1, source_target_pairs={{0,4},{4,0},{8,12},{12,8},{16,20},{20,16},{24,28},{28,24},{1,5},{5... | collective-permute-start | bytes 2359304 | tf_op jit(solution)/shard_map/ppermute | solution.py:391
  129.1 21.7 %collective-permute-start.11 = (bf16[1,2,128,1536]{3,2,1,0:T(8,128)(2,1)S(1)}, bf16[1,2,128,1536]{3,2,1,0:T(8,128)(2,1)S(1)}, u32[]{:S(2)}, u32[]{:S(2)}) collective-permute-start(bf16[1,2,128,1536]{3,2,1,0:T(8,128)(2,1)S(1)} %collective-permute-done.7.refs_1_.refs_11_), channel_id=1, source_target_pairs={{0,4},{4,0},{8,12},{12,8},{16,20},{20,16},{24,28},{28,24},{1,5},{5... | collective-permute-start | bytes 2359304 | tf_op jit(solution)/shard_map/ppermute | solution.py:391
  129.2 22.1 %collective-permute-start.18 = (bf16[1,2,128,1536]{3,2,1,0:T(8,128)(2,1)S(1)}, bf16[1,2,128,1536]{3,2,1,0:T(8,128)(2,1)S(1)}, u32[]{:S(2)}, u32[]{:S(2)}) collective-permute-start(bf16[1,2,128,1536]{3,2,1,0:T(8,128)(2,1)S(1)} %collective-permute-done.14.refs_9_.refs_15_), channel_id=1, source_target_pairs={{0,4},{4,0},{8,12},{12,8},{16,20},{20,16},{24,28},{28,24},{1,5},{5... | collective-permute-start | bytes 2359304 | tf_op jit(solution)/shard_map/ppermute | solution.py:391
  153.1 22.9 %collective-permute-start.39 = (bf16[1,4,2,128,256]{4,3,2,1,0:T(8,128)(2,1)S(1)}, bf16[1,4,2,128,256]{4,3,2,1,0:T(8,128)(2,1)S(1)}, u32[]{:S(2)}, u32[]{:S(2)}) collective-permute-start(bf16[1,4,2,128,256]{4,3,2,1,0:T(8,128)(2,1)S(1)} %bitcast.39), channel_id=1, source_target_pairs={{0,16},{4,20},{8,24},{12,28},{16,0},{20,4},{24,8},{28,12},{1,17},{... | collective-permute-start | bytes 1572872 | tf_op jit(solution)/shard_map/ppermute | solution.py:391
  153.1 24.3 %collective-permute-start.45 = (bf16[1,4,2,128,256]{4,3,2,1,0:T(8,128)(2,1)S(1)}, bf16[1,4,2,128,256]{4,3,2,1,0:T(8,128)(2,1)S(1)}, u32[]{:S(2)}, u32[]{:S(2)}) collective-permute-start(bf16[1,4,2,128,256]{4,3,2,1,0:T(8,128)(2,1)S(1)} %bitcast.40), channel_id=1, source_target_pairs={{0,8},{4,12},{8,0},{12,4},{16,24},{20,28},{24,16},{28,20},{1,9},{5... | collective-permute-start | bytes 1572872 | tf_op jit(solution)/shard_map/ppermute | solution.py:391
  155.1 23.5 %collective-permute-start.13 = (bf16[1,2,128,1536]{3,2,1,0:T(8,128)(2,1)S(1)}, bf16[1,2,128,1536]{3,2,1,0:T(8,128)(2,1)S(1)}, u32[]{:S(2)}, u32[]{:S(2)}) collective-permute-start(bf16[1,2,128,1536]{3,2,1,0:T(8,128)(2,1)S(1)} %collective-permute-done.9.refs_3_.refs_13_), channel_id=1, source_target_pairs={{0,4},{4,0},{8,12},{12,8},{16,20},{20,16},{24,28},{28,24},{1,5},{5... | collective-permute-start | bytes 2359304 | tf_op jit(solution)/shard_map/ppermute | solution.py:391
  178.6 29.5 %collective-permute-start.46 = (bf16[1,4,2,128,256]{4,3,2,1,0:T(8,128)(2,1)S(1)}, bf16[1,4,2,128,256]{4,3,2,1,0:T(8,128)(2,1)S(1)}, u32[]{:S(2)}, u32[]{:S(2)}) collective-permute-start(bf16[1,4,2,128,256]{4,3,2,1,0:T(8,128)(2,1)S(1)} %collective-permute-done.39.refs_4_), channel_id=1, source_target_pairs={{0,4},{4,0},{8,12},{12,8},{16,20},{20,16},{24,28},{28,24},{1,5},{5... | collective-permute-start | bytes 1572872 | tf_op jit(solution)/shard_map/ppermute | solution.py:391
  180.4 27.7 %collective-permute-start.44 = (bf16[1,4,2,128,256]{4,3,2,1,0:T(8,128)(2,1)S(1)}, bf16[1,4,2,128,256]{4,3,2,1,0:T(8,128)(2,1)S(1)}, u32[]{:S(2)}, u32[]{:S(2)}) collective-permute-start(bf16[1,4,2,128,256]{4,3,2,1,0:T(8,128)(2,1)S(1)} %collective-permute-done.42.refs_1_), channel_id=1, source_target_pairs={{0,4},{4,0},{8,12},{12,8},{16,20},{20,16},{24,28},{28,24},{1,5},{5... | collective-permute-start | bytes 1572872 | tf_op jit(solution)/shard_map/ppermute | solution.py:391
  180.5 27.6 %collective-permute-start.47 = (bf16[1,4,2,128,256]{4,3,2,1,0:T(8,128)(2,1)S(1)}, bf16[1,4,2,128,256]{4,3,2,1,0:T(8,128)(2,1)S(1)}, u32[]{:S(2)}, u32[]{:S(2)}) collective-permute-start(bf16[1,4,2,128,256]{4,3,2,1,0:T(8,128)(2,1)S(1)} %collective-permute-done.45.refs_5_), channel_id=1, source_target_pairs={{0,4},{4,0},{8,12},{12,8},{16,20},{20,16},{24,28},{28,24},{1,5},{5... | collective-permute-start | bytes 1572872 | tf_op jit(solution)/shard_map/ppermute | solution.py:391
  188.2 29.1 %collective-permute-start.38 = (bf16[1,4,2,128,256]{4,3,2,1,0:T(8,128)(2,1)S(1)}, bf16[1,4,2,128,256]{4,3,2,1,0:T(8,128)(2,1)S(1)}, u32[]{:S(2)}, u32[]{:S(2)}) collective-permute-start(bf16[1,4,2,128,256]{4,3,2,1,0:T(8,128)(2,1)S(1)} %collective-permute-done.37.refs_0_), channel_id=1, source_target_pairs={{0,4},{4,0},{8,12},{12,8},{16,20},{20,16},{24,28},{28,24},{1,5},{5... | collective-permute-start | bytes 1572872 | tf_op jit(solution)/shard_map/ppermute | solution.py:391
  190.3 27.0 %collective-permute-start.41 = (bf16[1,4,2,128,256]{4,3,2,1,0:T(8,128)(2,1)S(1)}, bf16[1,4,2,128,256]{4,3,2,1,0:T(8,128)(2,1)S(1)}, u32[]{:S(2)}, u32[]{:S(2)}) collective-permute-start(bf16[1,4,2,128,256]{4,3,2,1,0:T(8,128)(2,1)S(1)} %collective-permute-done.40.refs_2_), channel_id=1, source_target_pairs={{0,4},{4,0},{8,12},{12,8},{16,20},{20,16},{24,28},{28,24},{1,5},{5... | collective-permute-start | bytes 1572872 | tf_op jit(solution)/shard_map/ppermute | solution.py:391
  (36 other events, 403.1 us)
